TPU v7x, 128 devices: a whole 4x4x4 slice. The times are simulated.
128 devices in a mesh: req: 16 (over y, z), page: 8 (over x, core).
Axes of the slice: x: 4, y: 4, z: 4, core: 2. Of those that a mesh axis runs over, the one named last changes fastest.
Arguments:
- kv_store: bfloat16 [8192, 2, 8, 2048], P(('req', 'page')), may hold values from -6 to 6
- local_kv: bfloat16 [512, 2, 256, 2048], P(('req', 'page')), may hold values from -6 to 6
- new_qkv: bfloat16 [4, 512, 3, 2048], P(None, ('req', 'page')), may hold values from -32 to 32
- page_owner: int32 [512, 32], P(('req', 'page')), may hold values from 0 to 127, all different within a row; in each aligned block of 4 rows (0 to 3, 4 to 7, ...) at most 2 rows name the same one
- page_slot: int32 [512, 32], P(('req', 'page')), may hold values from 0 to 63
- prefix_len: int32 [512], P(('req', 'page')), may hold values from 225 to 256
- prefix_states: bfloat16 [16, 64, 64, 128], P('page'), may hold values from -6 to 6
- branch_id: int32 [512], P('req'), may hold values from 0 to 15
- mamba_x: bfloat16 [4, 512, 4096], P(None, ('req', 'page')), may hold values from -6 to 6
- mamba_bc: bfloat16 [4, 512, 256], P(None, ('req', 'page')), may hold values from -1.5 to 1.5
- mamba_dt: bfloat16 [4, 512, 64], P(None, ('req', 'page')), may hold values from -4 to 4
- decay_rate: float32 [64], replicated, may hold values from 0.05 to 4
Outputs:
- attn_out: bfloat16 [4, 512, 2048], P(None, ('req', 'page'))
- mamba_out: bfloat16 [4, 512, 4096], P(None, ('req', 'page'))
Inputs may be any that keep to these rules, and one draw needn't show every extreme that they name: `page_owner`: A request's 32 pages lie on different devices; among the 4 requests of one device (aligned blocks of rows) no device is named more than 2 times, and one is named exactly 2 times.
All inputs are finite; a program needn't handle non-finite values.
Results may differ from a plain program's by a relative error of at most 0.0049.
Values may be sent and summed in bfloat16 or wider, within the bound.
No kernel may reach another device: no remote copies, remote signals or barrier semaphores. Data moves between devices by JAX's collectives and lax.ppermute only.
A program may use at most 192 MiB of HBM per device.

v0:
```python
import math

import jax
import jax.numpy as jnp
from jax import lax
from jax.sharding import PartitionSpec as P

HEADS = 16


def ssm_step(ssm_state, step_input, bc_input, dt_input, decay_rate):
    slot_count, head_count, head_width, state_width = ssm_state.shape
    step_delta = jax.nn.softplus(dt_input.astype(jnp.float32))
    decay = jnp.exp(-decay_rate[None, :] * step_delta)
    scaled_input = (
        step_input.astype(jnp.float32).reshape(slot_count, head_count, head_width)
        * step_delta[:, :, None]
    )
    bc_float = bc_input.astype(jnp.float32)
    b_vector = bc_float[:, :state_width]
    c_vector = bc_float[:, state_width:]
    ssm_state = (
        decay[:, :, None, None] * ssm_state
        + scaled_input[:, :, :, None] * b_vector[:, None, None, :]
    )
    output_row = jnp.sum(ssm_state * c_vector[:, None, None, :], axis=-1)
    return (ssm_state, output_row.reshape(slot_count, -1).astype(jnp.bfloat16))


def on_device(
    kv_store,
    local_kv,
    new_qkv,
    page_owner,
    page_slot,
    prefix_len,
    prefix_states,
    branch_id,
    mamba_x,
    mamba_bc,
    mamba_dt,
    decay_rate,
):
    devices = lax.axis_size(("req", "page"))
    per_device = page_owner.shape[0]
    path_pages = page_owner.shape[1]
    capacity = min(per_device, max(2, 2 * per_device * path_pages // devices))
    features = kv_store.shape[-1]
    head_width = features // HEADS
    step_count = new_qkv.shape[0]
    owners = page_owner.reshape(-1)
    onehot = (owners[:, None] == jnp.arange(devices, dtype=jnp.int32)[None, :]).astype(jnp.int32)
    before = jnp.cumsum(onehot, axis=0) - onehot
    slot_rank = jnp.sum(before * onehot, axis=1)
    position = owners * capacity + slot_rank
    requests = (
        jnp.zeros((devices * capacity,), jnp.int32)
        .at[position]
        .set(page_slot.reshape(-1))
        .reshape(devices, capacity)
    )
    wanted = lax.all_to_all(requests, ("req", "page"), split_axis=0, concat_axis=0, tiled=True)
    served = kv_store[wanted]
    arrived = lax.all_to_all(served, ("req", "page"), split_axis=0, concat_axis=0, tiled=True)
    blocks = arrived.reshape((devices * capacity,) + served.shape[2:])[position]
    blocks = blocks.reshape((per_device, path_pages) + served.shape[2:])
    page_keys = blocks[:, :, 0].reshape(per_device, -1, HEADS, head_width)
    page_values = blocks[:, :, 1].reshape(per_device, -1, HEADS, head_width)
    local_keys = local_kv[:, 0].reshape(per_device, -1, HEADS, head_width)
    local_values = local_kv[:, 1].reshape(per_device, -1, HEADS, head_width)
    queries = new_qkv[:, :, 0].reshape(step_count, per_device, HEADS, head_width)
    new_keys = new_qkv[:, :, 1].reshape(step_count, per_device, HEADS, head_width)
    new_values = new_qkv[:, :, 2].reshape(step_count, per_device, HEADS, head_width)
    page_scores = jnp.einsum(
        "srhd,rkhd->rhsk", queries, page_keys, preferred_element_type=jnp.float32
    )
    local_scores = jnp.einsum(
        "srhd,rkhd->rhsk", queries, local_keys, preferred_element_type=jnp.float32
    )
    fresh_scores = jnp.einsum(
        "srhd,trhd->rhst", queries, new_keys, preferred_element_type=jnp.float32
    )
    scores = jnp.concatenate([page_scores, local_scores, fresh_scores], axis=-1) * (
        1.0 / math.sqrt(head_width)
    )
    page_total = page_keys.shape[1]
    local_total = local_keys.shape[1]
    key_index = jnp.arange(page_total + local_total + step_count, dtype=jnp.int32)
    new_index = key_index - page_total - local_total
    step_index = jnp.arange(step_count, dtype=jnp.int32)
    valid = (key_index[None, None, :] < prefix_len[:, None, None]) | (
        key_index[None, None, :] >= page_total
    ) & (new_index[None, None, :] <= step_index[None, :, None])
    scores = jnp.where(valid[:, None], scores, -jnp.inf)
    row_max = jnp.max(scores, axis=-1, keepdims=True)
    exp_scores = jnp.exp(scores - row_max)
    weights = (exp_scores / jnp.sum(exp_scores, axis=-1, keepdims=True)).astype(jnp.bfloat16)
    mixed = jnp.einsum(
        "rhsk,rkhd->srhd",
        weights[..., :page_total],
        page_values,
        preferred_element_type=jnp.float32,
    )
    mixed = mixed + jnp.einsum(
        "rhsk,rkhd->srhd",
        weights[..., page_total : page_total + local_total],
        local_values,
        preferred_element_type=jnp.float32,
    )
    mixed = mixed + jnp.einsum(
        "rhst,trhd->srhd",
        weights[..., page_total + local_total :],
        new_values,
        preferred_element_type=jnp.float32,
    )
    attn_out = mixed.reshape(step_count, per_device, features).astype(jnp.bfloat16)
    my_page = lax.axis_index("page")
    my_branches = lax.dynamic_slice_in_dim(branch_id, my_page * per_device, per_device)
    piece = lax.all_gather(prefix_states, "page", axis=0, tiled=True)
    branch_ids = jnp.arange(piece.shape[0], dtype=jnp.int32)
    selector = (my_branches[:, None] == branch_ids[None, :]).astype(jnp.bfloat16)
    ssm_state = jnp.einsum("rk,kabc->rabc", selector, piece, preferred_element_type=jnp.float32)
    outputs = []
    for step_idx in range(step_count):
        ssm_state, output_row = ssm_step(
            ssm_state, mamba_x[step_idx], mamba_bc[step_idx], mamba_dt[step_idx], decay_rate
        )
        outputs.append(output_row)
    mamba_out = jnp.stack(outputs)
    return (attn_out, mamba_out)


def solution(mesh):
    in_specs = (
        P(("req", "page"), None, None, None),
        P(("req", "page"), None, None, None),
        P(None, ("req", "page"), None, None),
        P(("req", "page"), None),
        P(("req", "page"), None),
        P(("req", "page")),
        P("page", None, None, None),
        P("req"),
        P(None, ("req", "page"), None),
        P(None, ("req", "page"), None),
        P(None, ("req", "page"), None),
        P(),
    )
    out_specs = (P(None, ("req", "page"), None), P(None, ("req", "page"), None))
    return jax.shard_map(
        on_device, mesh=mesh, in_specs=in_specs, out_specs=out_specs, check_vma=False
    )
```

profile of v0, /device:TPU:10, one launch (start us, length us, event | category | flops | bytes accessed | tf_op | source)
XLA Modules:
  0.0 402.1 jit_solution(8345322215403867154)
XLA Ops:
  7.2 0.7 all-gather.2.cloned.1.call-update
  7.9 0.8 eq.28
  8.7 0.7 broadcast_multiply_fusion.4
  9.4 0.8 reshape.451
  10.6 1.0 scatter_custom_fusion
  11.8 18.1 %all_to_all.17 = s32[128,1,2]{2,1,0:T(1,128)S(1)} all-to-all(s32[128,1,2]{2,1,0:T(1,128)S(1)} %bitcast.118), channel_id=1, replica_groups=mesh['req'=16,'page'=8] {'req','page'}, dimensions={0} | all-to-all | bytes 2048 | tf_op jit(solution)/shard_map/all_to_all | solution.py:62
  30.0 11.6 %gather_fusion = bf16[256,2,8,2048]{3,2,1,0:T(8,128)(2,1)} fusion(bf16[64,2,8,2048]{3,2,1,0:T(8,128)(2,1)} %param.12, s32[1024]{0:T(1024)S(1)} %pad_clamp_fusion.1), kind=kCustom, calls=%fused_computation | custom fusion | bytes 33555456 | tf_op jit(solution)/shard_map/gather | solution.py:63
  41.6 7.5 %all-to-all-start.1 = ((bf16[128,2,2,8,2048]{4,3,2,1,0:T(8,128)(2,1)}), bf16[128,2,2,8,2048]{4,3,2,1,0:T(8,128)(2,1)}, u32[]{:S(2)}, u32[]{:S(2)}) async-start(bf16[128,2,2,8,2048]{4,3,2,1,0:T(8,128)(2,1)} %bitcast.102), calls=%async_computation.1 | async-start | bytes 33554432 | tf_op jit(solution)/shard_map/all_to_all | solution.py:64
  50.1 2.0 copy.117
  52.3 2.0 copy.114
  54.2 2.0 copy.115
  56.8 6.2 %fusion.57 = (bf16[4,1,256,2048]{3,2,1,0:T(8,128)(2,1)}, bf16[4,1,256,2048]{3,2,1,0:T(8,128)(2,1)}) fusion(bf16[4,2,256,2048]{3,2,1,0:T(8,128)(2,1)} %param.13), kind=kLoop, calls=%fused_computation.108 | loop fusion | bytes 16777216 | tf_op jit(solution)/shard_map/slice | solution.py:70
  63.0 6.2 %copy.120 = bf16[4,1,256,2048]{2,3,0,1:T(8,128)(2,1)} copy(bf16[4,1,256,2048]{3,2,1,0:T(8,128)(2,1)} %get-tuple-element.7) | data formatting | bytes 8388608
  69.4 6.2 %copy.121 = bf16[4,1,256,2048]{2,3,0,1:T(8,128)(2,1)} copy(bf16[4,1,256,2048]{3,2,1,0:T(8,128)(2,1)} %get-tuple-element.6) | data formatting | bytes 8388608
  76.0 3.0 fusion.29
  79.0 2.8 broadcast_multiply_fusion
  81.8 1.0 copy-done.3
  82.8 2.6 broadcast_multiply_fusion.2
  85.4 227.3 %all-to-all-done.1 = bf16[128,2,2,8,2048]{4,3,2,1,0:T(8,128)(2,1)} async-done(((bf16[128,2,2,8,2048]{4,3,2,1,0:T(8,128)(2,1)}), bf16[128,2,2,8,2048]{4,3,2,1,0:T(8,128)(2,1)}, u32[]{:S(2)}, u32[]{:S(2)}) %all-to-all-start.1) | async-done | bytes 16777248 | tf_op jit(solution)/shard_map/all_to_all | solution.py:64
  312.7 12.3 %gather_fusion.1 = bf16[128,2,8,2048]{3,2,1,0:T(8,128)(2,1)} fusion(bf16[256,2,8,2048]{3,2,1,0:T(8,128)(2,1)} %bitcast.5, s32[1024]{0:T(1024)S(1)} %pad_clamp_fusion), kind=kCustom, calls=%fused_computation.1 | custom fusion | bytes 16777728 | tf_op jit(solution)/shard_map/gather | solution.py:65
  325.0 4.0 fusion.58
  329.0 1.4 copy.123
  330.4 1.4 copy.122
  331.9 1.2 fusion.9
  334.0 0.9 fusion.14
  334.9 0.9 copy-done
  335.8 1.2 fusion.17
  337.7 51.6 %multiply_reduce_fusion.1 = (bf16[4,64,64]{0,2,1:T(8,128)(2,1)}, bf16[4,64,64]{0,2,1:T(8,128)(2,1)S(1)}, bf16[4,64,64]{0,2,1:T(8,128)(2,1)}, bf16[4,64,64]{0,2,1:T(8,128)(2,1)}) fusion(f32[4,128]{1,0:T(4,128)S(1)} %get-tuple-element.43, f32[4,128]{1,0:T(4,128)S(1)} %get-tuple-element.44, f32[4,64,64]{0,2,1:T(8,128)} %get-tuple-element.46, ...), kind=kOutput, calls=%fused_computation.7 | convolution fusion | flops 108986432 | bytes 17190928 | tf_op jit(solution)/shard_map/rk,kabc->rabc/dot_general | solution.py:122
  389.2 1.6 copy.107
  390.8 1.6 copy.108
  392.4 1.6 copy.109
  394.4 0.8 pad_maximum_fusion
  (65 shorter events, 4.9 us)
Async XLA Ops:
  7.2 330.5 %all-gather.2.cloned.1.call-start = ((), (), s32[]{:S(2)}) async-start(), calls=%async_computation.2 | async-start | bytes 18874368 | tf_op jit(solution)/shard_map/all_gather | solution.py:119
  41.6 7.5 %copy-start.10 = (f32[64]{0:T(128)S(1)}, f32[64]{0:T(128)}, u32[]{:S(2)}) copy-start(f32[64]{0:T(128)} %param.23) | copy-start | bytes 772
  41.6 7.5 %copy-start.8 = (bf16[4,4,64]{2,1,0:T(4,128)(2,1)S(1)}, bf16[4,4,64]{2,1,0:T(4,128)(2,1)}, u32[]{:S(2)}) copy-start(bf16[4,4,64]{2,1,0:T(4,128)(2,1)} %param.22) | copy-start | bytes 6148
  41.6 7.8 %copy-start.6 = (bf16[4,4,4096]{2,1,0:T(4,128)(2,1)S(1)}, bf16[4,4,4096]{2,1,0:T(4,128)(2,1)}, u32[]{:S(2)}) copy-start(bf16[4,4,4096]{2,1,0:T(4,128)(2,1)} %param.20) | copy-start | bytes 393220
  41.6 271.1 %all-to-all-start.1 = ((bf16[128,2,2,8,2048]{4,3,2,1,0:T(8,128)(2,1)}), bf16[128,2,2,8,2048]{4,3,2,1,0:T(8,128)(2,1)}, u32[]{:S(2)}, u32[]{:S(2)}) async-start(bf16[128,2,2,8,2048]{4,3,2,1,0:T(8,128)(2,1)} %bitcast.102), calls=%async_computation.1 | async-start | bytes 33554432 | tf_op jit(solution)/shard_map/all_to_all | solution.py:64
  49.4 7.2 %copy-start.5 = (bf16[4,4,3,2048]{3,1,2,0:T(4,128)(2,1)S(1)}, bf16[4,4,3,2048]{3,1,2,0:T(4,128)(2,1)}, u32[]{:S(2)}) copy-start(bf16[4,4,3,2048]{3,1,2,0:T(4,128)(2,1)} %param.14) | copy-start | bytes 589828
  69.3 6.2 %copy-start.11 = (s32[32]{0:T(128)S(1)}, s32[32]{0:T(128)}, u32[]{:S(2)}) copy-start(s32[32]{0:T(128)} %param.19) | copy-start | bytes 388
  69.3 6.3 %copy-start.9 = (s32[4]{0:T(128)S(1)}, s32[4]{0:T(128)}, u32[]{:S(2)}) copy-start(s32[4]{0:T(128)} %param.17) | copy-start | bytes 52
  69.3 6.4 %copy-start.7 = (bf16[4,4,256]{2,1,0:T(4,128)(2,1)S(1)}, bf16[4,4,256]{2,1,0:T(4,128)(2,1)}, u32[]{:S(2)}) copy-start(bf16[4,4,256]{2,1,0:T(4,128)(2,1)} %param.21) | copy-start | bytes 24580
  75.6 3.5 copy-start.1
  79.0 2.8 copy-start.2
  79.0 3.8 copy-start.3
  333.6 2.2 copy-start
  334.0 3.7 copy-start.4
Sparse Core Ops, SparseCore 0:
  9.7 175.2 all-gather.1
where the time goes:
time: 403 us; the launch traced here: 402 us
  waiting for transfers between devices  228 us (57%)
  local copies, waits for them, and re-layouts  67.8 us (17%)
  matrix products  58.2 us (14%)
  blocking collectives  18.1 us (4%)
  between operations  14.3 us (4%)
  other arithmetic  8.22 us (2%)
  starting transfers between devices  7.53 us (2%)
    all_to_all x1, waiting for transfers between devices, on_device(): lax.all_to_all(served, ('req', 'page'), split_axis=0, concat_axis=0, tile...  227 us
    dot_general x1, matrix products, on_device(): jnp.einsum('rk,kabc->rabc', selector, piece, preferred_element_type=jnp.f...  51.6 us
    all_to_all x1, blocking collectives, on_device(): lax.all_to_all(requests, ('req', 'page'), split_axis=0, concat_axis=0, ti...  18.1 us
    unnamed x28, local copies, waits for them, and re-layouts  17.2 us
    gather x1, local copies, waits for them, and re-layouts, on_device(): blocks = arrived.reshape((devices * capacity,) + served.shape[2:])[position]  12.3 us
    gather x1, local copies, waits for them, and re-layouts, on_device(): served = kv_store[wanted]  11.6 us
  transfers between devices with their start and end apart: 2, of which 1 were waited for; matrix products, arithmetic and copies ran while one was open for 19% of the time, Pallas kernels for 0%

commit v1 on v0

v1 whole, which is shorter than its diff:
```python
import functools
import math

import jax
import jax.numpy as jnp
from jax import lax
from jax.experimental import pallas as pl
from jax.experimental.pallas import tpu as pltpu
from jax.sharding import PartitionSpec as P

HEADS = 16
HD = 128
STEPS = 4
RD = 4
ROWS = STEPS * RD
FEAT = HEADS * HD
DEV = 128
TOK = 8
MH = 64
MD = 64
ST = 128
MF = MH * MD
NPG = 8
BATCH = 8
NB = DEV // BATCH
BLK = FEAT + 128
NEG = -1e30
SCALE = 1.0 / math.sqrt(HD)
BF = jnp.bfloat16
F32 = jnp.float32
NT = (((1,), (1,)), ((), ()))
NN = (((1,), (0,)), ((), ()))


def dot(a, b, dims=NN):
    return lax.dot_general(a, b, dims, preferred_element_type=F32)


def split2(x):
    hi = x.astype(BF)
    return hi, (x - hi.astype(F32)).astype(BF)


def split3(x):
    hi = x.astype(BF)
    rest = x - hi.astype(F32)
    mid = rest.astype(BF)
    return hi, mid, (rest - mid.astype(F32)).astype(BF)


def local_kernel(q_ref, nk_ref, nv_ref, kv_ref, o_ref, m_ref, l_ref):
    q = q_ref[...]
    parts = [dot(q, kv_ref[r, 0], NT) for r in range(RD)]
    row = lax.broadcasted_iota(jnp.int32, (ROWS, 1), 0)
    keep = row % RD
    new = dot(q, nk_ref[...], NT) * SCALE
    col = lax.broadcasted_iota(jnp.int32, (ROWS, ROWS), 1)
    ok = (col % RD == keep) & (col // RD <= row // RD)
    new = jnp.where(ok, new, NEG)
    mine = jnp.where(keep == 0, parts[0], NEG)
    for r in range(1, RD):
        mine = jnp.where(keep == r, parts[r], mine)
    mine = mine * SCALE
    top = jnp.maximum(jnp.max(mine, axis=1, keepdims=True), jnp.max(new, axis=1, keepdims=True))
    p = jnp.exp(mine - top)
    pn = jnp.where(ok, jnp.exp(new - top), 0.0)
    total = jnp.sum(p, axis=1, keepdims=True) + jnp.sum(pn, axis=1, keepdims=True)
    out = dot(pn.astype(BF), nv_ref[...])
    for r in range(RD):
        out = out + dot(jnp.where(keep == r, p, 0.0).astype(BF), kv_ref[r, 1])
    o_ref[...] = out
    m_ref[...] = jnp.broadcast_to(top, (ROWS, HD))
    l_ref[...] = jnp.broadcast_to(total, (ROWS, HD))


def local_attention(q, nk, nv, local_kv):
    row = pl.BlockSpec((ROWS, HD), lambda h: (0, h))
    return pl.pallas_call(
        local_kernel,
        grid=(HEADS,),
        in_specs=[row, row, row, pl.BlockSpec((RD, 2, 256, HD), lambda h: (0, 0, 0, h))],
        out_specs=[row, row, row],
        out_shape=[jax.ShapeDtypeStruct((ROWS, FEAT), F32)] * 3,
        cost_estimate=pl.CostEstimate(flops=2 * 2 * 16 * 1024 * 2048, bytes_accessed=9_000_000, transcendentals=300_000),
        name="local_attention",
    )(q, nk, nv, local_kv)


def owner_kernel(slot_ref, kreq_ref, sel_ref, q_ref, kv_ref, o_ref, kbuf, vbuf, sem):
    step = pl.program_id(0)
    pages = 2 * BATCH

    def copies(at, buf):
        out = []
        for j in range(pages):
            page = slot_ref[at * pages + j]
            out.append(pltpu.make_async_copy(kv_ref.at[page, 0], kbuf.at[buf, j], sem.at[buf, 0, j]))
            out.append(pltpu.make_async_copy(kv_ref.at[page, 1], vbuf.at[buf, j], sem.at[buf, 1, j]))
        return out

    @pl.when(step == 0)
    def _():
        for c in copies(0, 0):
            c.start()

    now = lax.rem(step, 2)

    @pl.when(step + 1 < NB)
    def _():
        for c in copies(step + 1, 1 - now):
            c.start()

    for c in copies(step, now):
        c.wait()
    rows = BATCH * ROWS
    keys = pages * TOK
    row = lax.broadcasted_iota(jnp.int32, (rows, 1), 0)
    mine = (row // ROWS) * RD + row % RD
    ok = mine == kreq_ref[0]
    lane = lax.broadcasted_iota(jnp.int32, (rows, HD), 1)
    tops = jnp.zeros((rows, HD), F32)
    sums = jnp.zeros((rows, HD), F32)
    sel = sel_ref[...]
    for h in range(HEADS):
        at = slice(h * HD, (h + 1) * HD)
        q = q_ref[:, :, at].reshape(rows, HD)
        k = kbuf[now, :, :, at].reshape(keys, HD)
        v = vbuf[now, :, :, at].reshape(keys, HD)
        s = jnp.where(ok, dot(q, k, NT) * SCALE, NEG)
        top = jnp.max(s, axis=1, keepdims=True)
        p = jnp.where(ok, jnp.exp(s - top), 0.0)
        tops = jnp.where(lane == h, top, tops)
        sums = jnp.where(lane == h, jnp.sum(p, axis=1, keepdims=True), sums)
        out = dot(p.astype(BF), v).astype(BF)
        o_ref[:, at] = dot(sel, out).astype(BF)
    parts = list(split3(tops)) + list(split2(sums))
    stats = jnp.zeros((rows, HD), F32)
    for i, part in enumerate(parts):
        wide = part.astype(F32)
        if i:
            wide = pltpu.roll(wide, HEADS * i, 1)
        stats = stats + wide
    o_ref[:, FEAT:] = dot(sel, stats.astype(BF)).astype(BF)


def owner_attention(slots, kreq, sel, gathered, kv_store):
    rows = BATCH * 2 * STEPS
    return pl.pallas_call(
        owner_kernel,
        grid_spec=pltpu.PrefetchScalarGridSpec(
            num_scalar_prefetch=1,
            grid=(NB,),
            in_specs=[
                pl.BlockSpec((1, 1, 2 * BATCH * TOK), lambda i, s: (i, 0, 0)),
                pl.BlockSpec((rows, BATCH * ROWS), lambda i, s: (i, 0)),
                pl.BlockSpec((BATCH, ROWS, BLK), lambda i, s: (i, 0, 0)),
                pl.BlockSpec(memory_space=pl.ANY),
            ],
            out_specs=pl.BlockSpec((rows, BLK), lambda i, s: (i, 0)),
            scratch_shapes=[
                pltpu.VMEM((2, 2 * BATCH, TOK, FEAT), BF),
                pltpu.VMEM((2, 2 * BATCH, TOK, FEAT), BF),
                pltpu.SemaphoreType.DMA((2, 2, 2 * BATCH)),
            ],
        ),
        out_shape=jax.ShapeDtypeStruct((DEV * 2 * STEPS, BLK), BF),
        cost_estimate=pl.CostEstimate(flops=4 * 2048 * 128 * 2048, bytes_accessed=30_000_000, transcendentals=4_000_000),
        compiler_params=pltpu.CompilerParams(vmem_limit_bytes=32 * 1024 * 1024),
        name="owner_attention",
    )(slots, kreq, sel, gathered, kv_store)


def combine_kernel(own_ref, got_ref, o_ref, m_ref, l_ref, out_ref):
    cols = DEV * 2 * STEPS
    own = own_ref[...]
    row = lax.broadcasted_iota(jnp.int32, (ROWS, 1), 0)
    ok = row == own
    stats = jnp.transpose(got_ref[:, FEAT:].astype(F32))
    part = [stats[HEADS * i : HEADS * (i + 1)] for i in range(5)]
    tops = part[0] + part[1] + part[2]
    sums = part[3] + part[4]
    for h in range(HEADS):
        at = slice(h * HD, (h + 1) * HD)
        top = jnp.where(ok, tops[h : h + 1], NEG)
        lm = m_ref[:, h * HD : h * HD + 1]
        best = jnp.maximum(jnp.max(top, axis=1, keepdims=True), lm)
        w = jnp.where(ok, jnp.exp(top - best), 0.0)
        mine = jnp.exp(lm - best)
        total = jnp.sum(w * sums[h : h + 1], axis=1, keepdims=True) + mine * l_ref[:, h * HD : h * HD + 1]
        hi, lo = split2(w)
        got = got_ref[:, at]
        mix = dot(hi, got) + dot(lo, got) + mine * o_ref[:, at]
        out_ref[:, at] = (mix / total).astype(BF)


def combine(own, got, o, m, l):
    return pl.pallas_call(
        combine_kernel,
        out_shape=jax.ShapeDtypeStruct((ROWS, FEAT), BF),
        compiler_params=pltpu.CompilerParams(vmem_limit_bytes=32 * 1024 * 1024),
        cost_estimate=pl.CostEstimate(flops=4 * 16 * 1024 * 2048, bytes_accessed=5_000_000, transcendentals=300_000),
        name="combine_attention",
    )(own, got, o, m, l)


def state_kernel(br_ref, c_ref, st_ref, *outs):
    c = c_ref[...]
    first = dot(c, st_ref[0], NT)
    second = dot(c, st_ref[1], NT)
    which = br_ref[...]
    z = jnp.where(which == 0, first, 0.0) + jnp.where(which == 1, second, 0.0)
    z = z.astype(BF)
    for k in range(NPG):
        outs[k][...] = z[k * ROWS : (k + 1) * ROWS]


def state_products(which, c_all, states):
    wide = 1024
    return pl.pallas_call(
        state_kernel,
        grid=(MF // wide,),
        in_specs=[
            pl.BlockSpec((NPG * ROWS, 1), lambda i: (0, 0)),
            pl.BlockSpec((NPG * ROWS, ST), lambda i: (0, 0)),
            pl.BlockSpec((2, wide, ST), lambda i: (0, i, 0)),
        ],
        out_specs=[pl.BlockSpec((ROWS, wide), lambda i: (0, i))] * NPG,
        out_shape=[jax.ShapeDtypeStruct((ROWS, MF), BF)] * NPG,
        cost_estimate=pl.CostEstimate(flops=4 * 128 * 128 * 4096, bytes_accessed=3_200_000, transcendentals=0),
        name="state_products",
    )(which, c_all, states)


def scan_kernel(coef_ref, x_ref, *refs):
    zs, out_ref = refs[:-1], refs[-1]
    wide = out_ref.shape[1]
    head = lax.broadcasted_iota(jnp.int32, (MH, wide), 0)
    chan = lax.broadcasted_iota(jnp.int32, (MH, wide), 1) + pl.program_id(0) * wide
    spread = (head == chan // MD).astype(BF)
    hi, mid, lo = split3(coef_ref[...])
    coef = dot(hi, spread) + dot(mid, spread) + dot(lo, spread)
    z = zs[0][...].astype(F32)
    for ref in zs[1:]:
        z = z + ref[...].astype(F32)
    y = coef[:ROWS] * z
    x = x_ref[...].astype(F32)
    for t in range(STEPS):
        xt = jnp.concatenate([x[t * RD : (t + 1) * RD]] * STEPS, axis=0)
        y = y + coef[(t + 1) * ROWS : (t + 2) * ROWS] * xt
    out_ref[...] = y.astype(BF)


def scan_outputs(coef, x, zs):
    wide = 1024
    spec = pl.BlockSpec((ROWS, wide), lambda i: (0, i))
    return pl.pallas_call(
        scan_kernel,
        grid=(MF // wide,),
        in_specs=[pl.BlockSpec(coef.shape, lambda i: (0, 0))] + [spec] * (1 + NPG),
        out_specs=spec,
        out_shape=jax.ShapeDtypeStruct((ROWS, MF), BF),
        cost_estimate=pl.CostEstimate(flops=6 * 80 * 64 * 4096, bytes_accessed=1_500_000, transcendentals=0),
        name="scan_outputs",
    )(coef, x, *zs)


def coefficients(mamba_bc, mamba_dt, decay_rate):
    delta = jax.nn.softplus(mamba_dt.astype(F32))
    rate = -decay_rate[None, :] * delta
    decay = jnp.exp(rate)
    b, c = mamba_bc[:, :, :ST], mamba_bc[:, :, ST:]
    bc = jnp.einsum("trn,srn->tsr", b, c, preferred_element_type=F32)
    rows = []
    run = decay[0]
    for s in range(STEPS):
        rows.append(run)
        if s + 1 < STEPS:
            run = run * decay[s + 1]
    zero = jnp.zeros_like(run)
    for t in range(STEPS):
        carry = delta[t]
        for s in range(STEPS):
            if s < t:
                rows.append(zero)
                continue
            if s > t:
                carry = carry * decay[s]
            rows.append(carry * bc[t, s][:, None])
    return jnp.stack(rows).reshape((1 + STEPS) * ROWS, MH)


def on_device(
    kv_store,
    local_kv,
    new_qkv,
    page_owner,
    page_slot,
    prefix_len,
    prefix_states,
    branch_id,
    mamba_x,
    mamba_bc,
    mamba_dt,
    decay_rate,
):
    me = lax.axis_index(("req", "page"))
    my_page = lax.axis_index("page")
    q = new_qkv[:, :, 0].reshape(ROWS, FEAT)
    nk = new_qkv[:, :, 1].reshape(ROWS, FEAT)
    nv = new_qkv[:, :, 2].reshape(ROWS, FEAT)

    count = jnp.clip(prefix_len[:, None] - TOK * jnp.arange(page_owner.shape[1], dtype=jnp.int32)[None, :], 0, TOK)
    named = page_owner[:, :, None] == jnp.arange(DEV, dtype=jnp.int32)[None, None, :]
    t_slot = jnp.sum(jnp.where(named, page_slot[:, :, None], 0), axis=1)
    t_count = jnp.sum(jnp.where(named, count[:, :, None], 0), axis=1)
    tables = jnp.concatenate([t_slot, t_count, jnp.zeros((2 * RD, DEV), jnp.int32)], axis=0).astype(BF)
    block = jnp.concatenate([q, tables], axis=1)
    gathered = lax.all_gather(block[None], ("req", "page"), axis=0, tiled=True)

    c_own = mamba_bc[:, :, ST:].reshape(ROWS, ST)
    c_rel = [c_own]
    for k in range(1, NPG):
        c_rel.append(lax.ppermute(c_own, "page", [((i + k) % NPG, i) for i in range(NPG)]))
    order = (my_page + jnp.arange(NPG, dtype=jnp.int32)) % NPG
    branch = branch_id.reshape(NPG, RD)[order] - 2 * my_page
    branch = jnp.broadcast_to(branch[:, None, :], (NPG, STEPS, RD)).reshape(NPG * ROWS, 1)
    z_out = state_products(branch, jnp.concatenate(c_rel, axis=0), prefix_states.reshape(2, MF, ST))
    z_in = [z_out[0]]
    for k in range(1, NPG):
        z_in.append(lax.ppermute(z_out[k], "page", [(i, (i + k) % NPG) for i in range(NPG)]))
    coef = coefficients(mamba_bc, mamba_dt, decay_rate)
    mamba_out = scan_outputs(coef, mamba_x.reshape(ROWS, MF), z_in)

    o, m, l = local_attention(q, nk, nv, local_kv)

    mine = (jnp.arange(DEV, dtype=jnp.int32) == me).astype(BF)
    col = jnp.einsum("drl,l->rd", gathered[:, : 2 * RD, FEAT:], mine, preferred_element_type=F32).astype(jnp.int32)
    c_slot, c_count = col[:RD], col[RD:]
    hit = (c_count > 0).astype(jnp.int32)
    rank = jnp.cumsum(hit, axis=0) - hit
    request = jnp.arange(RD, dtype=jnp.int32)[:, None]
    at_slot, at_req, at_count = [], [], []
    for c in range(2):
        here = (hit > 0) & (rank == c)
        at_slot.append(jnp.sum(jnp.where(here, c_slot, 0), axis=0))
        at_count.append(jnp.sum(jnp.where(here, c_count, 0), axis=0))
        at_req.append(jnp.sum(jnp.where(here, request + 1, 0), axis=0) - 1)
    at_slot = jnp.stack(at_slot, axis=1)
    at_count = jnp.stack(at_count, axis=1)
    at_req = jnp.stack(at_req, axis=1)
    near = jnp.arange(DEV, dtype=jnp.int32)[:, None] % BATCH
    full = jnp.where(at_count > 0, near * RD + at_req, -1)
    tok = jnp.arange(TOK, dtype=jnp.int32)
    kreq = jnp.where(tok[None, None, :] < at_count[:, :, None], full[:, :, None], -1).reshape(NB, 1, 2 * BATCH * TOK)
    lane = jnp.arange(BATCH * ROWS, dtype=jnp.int32)
    lane_req = (lane // ROWS) * RD + lane % RD
    lane_step = (lane // RD) % STEPS
    steps = jnp.arange(STEPS, dtype=jnp.int32)
    sel = (full[:, :, None, None] == lane_req) & (steps[None, None, :, None] == lane_step)
    sel = sel.astype(BF).reshape(DEV * 2 * STEPS, BATCH * ROWS)
    part = owner_attention(at_slot.reshape(-1), kreq, sel, gathered, kv_store)
    got = lax.all_to_all(part.reshape(DEV, 2 * STEPS, BLK), ("req", "page"), 0, 0, tiled=True)

    own_hit = (t_count > 0).astype(jnp.int32)
    own_rank = jnp.cumsum(own_hit, axis=0) - own_hit
    places = []
    for c in range(2):
        here = (own_hit > 0) & (own_rank == c)
        places.append(jnp.sum(jnp.where(here, request + 1, 0), axis=0) - 1)
    places = jnp.stack(places, axis=1)[:, :, None]
    own = jnp.where(places >= 0, steps[None, None, :] * RD + places, -1).reshape(1, DEV * 2 * STEPS)
    attn = combine(own, got.reshape(DEV * 2 * STEPS, BLK), o, m, l)
    return attn.reshape(STEPS, RD, FEAT), mamba_out.reshape(STEPS, RD, MF)


def solution(mesh):
    in_specs = (
        P(("req", "page"), None, None, None),
        P(("req", "page"), None, None, None),
        P(None, ("req", "page"), None, None),
        P(("req", "page"), None),
        P(("req", "page"), None),
        P(("req", "page")),
        P("page", None, None, None),
        P("req"),
        P(None, ("req", "page"), None),
        P(None, ("req", "page"), None),
        P(None, ("req", "page"), None),
        P(),
    )
    out_specs = (P(None, ("req", "page"), None), P(None, ("req", "page"), None))
    return jax.shard_map(
        on_device, mesh=mesh, in_specs=in_specs, out_specs=out_specs, check_vma=False
    )
```

time: 403 us -> 276 us (0.68)
  the two profiles are of different devices: /device:TPU:10 before, /device:TPU:1 now
where the time goes in v1:
time: 276 us; the launch traced here: 275 us
  waiting for transfers between devices  111 us (40%)
  Pallas kernels  95.2 us (34%)
  starting transfers between devices  24.8 us (9%)
  local copies, waits for them, and re-layouts  21.3 us (8%)
  between operations  14.4 us (5%)
  other arithmetic  5.72 us (2%)
    pallas_call x1, Pallas kernels, owner_attention(): pl.pallas_call(owner_kernel, grid_spec=pltpu.PrefetchScalarGridSpec(num_s...  69.7 us
    all_gather x1, waiting for transfers between devices, on_device(): gathered = lax.all_gather(block[None], ('req', 'page'), axis=0, tiled=True)  63.1 us
    ppermute x7, waiting for transfers between devices, on_device(): lax.ppermute(c_own, 'page', [((i + k) % NPG, i) for i in range(NPG)])  44.6 us
    pallas_call x1, Pallas kernels, local_attention(): pl.pallas_call(local_kernel, grid=(HEADS,), in_specs=[row, row, row, pl.B...  13.5 us
    unnamed x46, local copies, waits for them, and re-layouts  11.9 us
    ppermute x7, starting transfers between devices, on_device(): lax.ppermute(c_own, 'page', [((i + k) % NPG, i) for i in range(NPG)])  11.2 us
    ppermute x7, starting transfers between devices, on_device(): lax.ppermute(z_out[k], 'page', [(i, (i + k) % NPG) for i in range(NPG)])  7.87 us
    all_to_all x1, starting transfers between devices, on_device(): lax.all_to_all(part.reshape(DEV, 2 * STEPS, BLK), ('req', 'page'), 0, 0,...  5.74 us
  transfers between devices with their start and end apart: 16, of which 3 were waited for; matrix products, arithmetic and copies ran while one was open for 5% of the time, Pallas kernels for 33%

profile of v1, /device:TPU:1, one launch (start us, length us, event | category | flops | bytes accessed | tf_op | source)
XLA Modules:
  0.0 274.6 jit_solution(14995040323317491672)
XLA Ops:
  7.2 0.7 subtract_clamp_fusion
  7.9 0.8 select_reduce_fusion
  8.8 1.0 fusion.19
  11.2 1.4 collective-permute-start
  12.6 2.6 collective-permute-start.1
  15.2 0.8 collective-permute-start.2
  16.0 2.4 collective-permute-start.3
  18.3 0.9 collective-permute-start.4
  19.9 0.7 reshape.537
  22.5 63.1 %all-gather.3.cloned.1.call-done = bf16[2048,2176]{1,0:T(8,128)(2,1)} async-done(((bf16[16,2176]{1,0:T(8,128)(2,1)}), bf16[2048,2176]{1,0:T(8,128)(2,1)}) %all-gather.3.cloned.1.call-update) | async-done | bytes 8912912 | tf_op jit(solution)/shard_map/all_gather | solution.py:318
  85.7 2.2 fusion
  89.6 3.5 %copy-done.1 = bf16[2048,2176]{1,0:T(8,128)(2,1)S(1)} copy-done((bf16[2048,2176]{1,0:T(8,128)(2,1)S(1)}, bf16[2048,2176]{1,0:T(8,128)(2,1)}, u32[]{:S(2)}) %copy-start.1) | copy-done | bytes 8912920
  93.1 2.2 copy-done.2
  95.3 69.7 %owner_attention.1 = bf16[1024,2176]{1,0:T(8,128)(2,1)S(1)} custom-call(s32[256]{0:T(256)S(1)} %reshape.531.slot_ref, s32[16,1,128]{2,1,0:T(1,128)S(1)} %bitcast.43, bf16[1024,128]{1,0:T(8,128)(2,1)S(1)} %bitcast.42, bf16[128,16,2176]{2,1,0:T(8,128)(2,1)S(1)} %bitcast.41, bf16[64,2,8,2048]{3,2,1,0:T(8,128)(2,1)S(1)} %copy-done.2), custom_call_target="tpu_custom_call" | custom-call | flops 2147483648 | bytes 30000000 | tf_op jit(solution)/shard_map/owner_attention/pallas_call | solution.py:148
  165.0 2.1 copy-done
  167.1 5.7 %all-to-all-start = ((bf16[128,8,2176]{2,1,0:T(8,128)(2,1)}), bf16[128,8,2176]{2,1,0:T(8,128)(2,1)}, u32[]{:S(2)}, u32[]{:S(2)}) async-start(bf16[128,8,2176]{2,1,0:T(8,128)(2,1)} %bitcast.39), calls=%async_computation | async-start | bytes 8912896 | tf_op jit(solution)/shard_map/all_to_all | solution.py:362
  174.2 1.4 collective-permute-start.5
  175.6 1.7 collective-permute-start.6
  177.3 44.6 %collective-permute-done.5 = bf16[16,128]{1,0:T(8,128)(2,1)S(1)} collective-permute-done((bf16[16,128]{1,0:T(8,128)(2,1)S(1)}, bf16[16,128]{1,0:T(8,128)(2,1)S(1)}, u32[]{:S(2)}, u32[]{:S(2)}) %collective-permute-start.5) | collective-permute-done | bytes 4128 | tf_op jit(solution)/shard_map/ppermute | solution.py:323
  222.6 4.1 %state_products.1 = (bf16[16,4096]{1,0:T(8,128)(2,1)}, bf16[16,4096]{1,0:T(8,128)(2,1)}, bf16[16,4096]{1,0:T(8,128)(2,1)}, bf16[16,4096]{1,0:T(8,128)(2,1)}, bf1...) custom-call(s32[128,1]{1,0:T(8,128)} %reshape.554.br_ref, ...), custom_call_target="tpu_custom_call" | custom-call | flops 268435456 | bytes 3200000 | tf_op jit(solution)/shard_map/state_products/pallas_call | solution.py:219
  227.3 1.4 collective-permute-start.8
  228.7 1.9 collective-permute-start.9
  230.6 1.4 collective-permute-start.10
  232.0 2.6 collective-permute-start.11
  234.5 3.1 %collective-permute-done.8.refs_2_ = bf16[16,4096]{1,0:T(8,128)(2,1)S(1)} collective-permute-done((bf16[16,4096]{1,0:T(8,128)(2,1)}, bf16[16,4096]{1,0:T(8,128)(2,1)S(1)}, u32[]{:S(2)}, u32[]{:S(2)}) %collective-permute-start.8) | collective-permute-done | bytes 131104 | tf_op jit(solution)/shard_map/ppermute | solution.py:330
  239.7 13.5 %local_attention.1 = (f32[16,2048]{1,0:T(8,128)}, f32[16,2048]{1,0:T(8,128)}, f32[16,2048]{1,0:T(8,128)}) custom-call(bf16[16,2048]{1,0:T(8,128)(2,1)} %copy-done.6, bf16[16,2048]{1,0:T(8,128)(2,1)} %reshape_squeeze.10.nk_ref, bf16[16,2048]{1,0:T(8,128)(2,1)} %reshape_squeeze.11.nv_ref, bf16[4,2,256,2048]{3,2,1,0:T(8,128)(2,1)} %kv_ref.3), custom_call_target="tpu_custom_call" | custom-call | flops 134217728 | bytes 9000000 | tf_op jit(solution)/shard_map/local_attention/pallas_call | solution.py:78
  254.0 3.7 %scan_outputs.1 = bf16[16,4096]{1,0:T(8,128)(2,1)} custom-call(f32[80,64]{1,0:T(8,128)} %bitcast.45, bf16[16,4096]{1,0:T(8,128)(2,1)} %reshape.536.x_ref, bf16[16,4096]{1,0:T(8,128)(2,1)} %get-tuple-element.16.refs_0_, bf16[16,4096]{1,0:T(8,128)(2,1)} %copy-done.8, bf16[16,4096]{1,0:T(8,128)(2,1)} %copy-done.9, bf16[16,4096]{1,0:T(8,128)(2,1)} %copy-done.10, ...), custom_call_target="tpu_custom_call" | custom-call | flops 125829120 | bytes 1500000 | tf_op jit(solution)/shard_map/scan_outputs/pallas_call | solution.py:256
  257.8 1.6 reshape.541
  260.2 0.9 copy-done.3
  261.1 0.9 copy-done.4
  262.0 0.9 copy-done.5
  262.9 4.2 %combine_attention.1 = bf16[16,2048]{1,0:T(8,128)(2,1)S(1)} custom-call(s32[1,1024]{1,0:T(1,128)S(1)} %select_n.150.own_ref, bf16[1024,2176]{1,0:T(8,128)(2,1)} %bitcast.15.got_ref, f32[16,2048]{1,0:T(8,128)S(1)} %copy-done.3, f32[16,2048]{1,0:T(8,128)S(1)} %copy-done.4, f32[16,2048]{1,0:T(8,128)S(1)} %copy-done.5), custom_call_target="tpu_custom_call" | custom-call | flops 134217728 | bytes 5000000 | tf_op jit(solution)/shard_map/combine_attention/pallas_call | solution.py:197
  (125 shorter events, 12.5 us)
Async XLA Ops:
  7.2 78.5 %all-gather.3.cloned.1.call-start = ((), (), s32[]{:S(2)}) async-start(), calls=%async_computation.1 | async-start | bytes 8982528 | tf_op jit(solution)/shard_map/all_gather | solution.py:318
  9.8 155.2 %copy-start.6 = (bf16[16,2048]{1,0:T(8,128)(2,1)}, bf16[16,2048]{1,0:T(8,128)(2,1)S(1)}, u32[]{:S(2)}) copy-start(bf16[16,2048]{1,0:T(8,128)(2,1)S(1)} %reshape_squeeze.9.q_ref) | copy-start | bytes 196612
  11.2 163.0 %collective-permute-start = (bf16[16,128]{1,0:T(8,128)(2,1)S(1)}, bf16[16,128]{1,0:T(8,128)(2,1)S(1)}, u32[]{:S(2)}, u32[]{:S(2)}) collective-permute-start(bf16[16,128]{1,0:T(8,128)(2,1)S(1)} %bitcast.46), channel_id=1, source_target_pairs={{1,0},{2,1},{3,2},{4,3},{5,4},{6,5},{7,6},{0,7},{9,8},{10,9},{11,1... | collective-permute-start | bytes 12296 | tf_op jit(solution)/shard_map/ppermute | solution.py:323
  12.6 162.9 %collective-permute-start.1 = (bf16[16,128]{1,0:T(8,128)(2,1)S(1)}, bf16[16,128]{1,0:T(8,128)(2,1)S(1)}, u32[]{:S(2)}, u32[]{:S(2)}) collective-permute-start(bf16[16,128]{1,0:T(8,128)(2,1)S(1)} %bitcast.47), channel_id=1, source_target_pairs={{2,0},{3,1},{4,2},{5,3},{6,4},{7,5},{0,6},{1,7},{10,8},{11,9},{12,... | collective-permute-start | bytes 12296 | tf_op jit(solution)/shard_map/ppermute | solution.py:323
  15.2 162.1 %collective-permute-start.2 = (bf16[16,128]{1,0:T(8,128)(2,1)S(1)}, bf16[16,128]{1,0:T(8,128)(2,1)S(1)}, u32[]{:S(2)}, u32[]{:S(2)}) collective-permute-start(bf16[16,128]{1,0:T(8,128)(2,1)S(1)} %bitcast.48), channel_id=1, source_target_pairs={{3,0},{4,1},{5,2},{6,3},{7,4},{0,5},{1,6},{2,7},{11,8},{12,9},{13,... | collective-permute-start | bytes 12296 | tf_op jit(solution)/shard_map/ppermute | solution.py:323
  16.0 161.3 %collective-permute-start.3 = (bf16[16,128]{1,0:T(8,128)(2,1)S(1)}, bf16[16,128]{1,0:T(8,128)(2,1)S(1)}, u32[]{:S(2)}, u32[]{:S(2)}) collective-permute-start(bf16[16,128]{1,0:T(8,128)(2,1)S(1)} %bitcast.49), channel_id=1, source_target_pairs={{4,0},{5,1},{6,2},{7,3},{0,4},{1,5},{2,6},{3,7},{12,8},{13,9},{14,... | collective-permute-start | bytes 12296 | tf_op jit(solution)/shard_map/ppermute | solution.py:323
  18.3 159.0 %collective-permute-start.4 = (bf16[16,128]{1,0:T(8,128)(2,1)S(1)}, bf16[16,128]{1,0:T(8,128)(2,1)S(1)}, u32[]{:S(2)}, u32[]{:S(2)}) collective-permute-start(bf16[16,128]{1,0:T(8,128)(2,1)S(1)} %bitcast.50), channel_id=1, source_target_pairs={{5,0},{6,1},{7,2},{0,3},{1,4},{2,5},{3,6},{4,7},{13,8},{14,9},{15,... | collective-permute-start | bytes 12296 | tf_op jit(solution)/shard_map/ppermute | solution.py:323
  89.5 3.5 %copy-start.1 = (bf16[2048,2176]{1,0:T(8,128)(2,1)S(1)}, bf16[2048,2176]{1,0:T(8,128)(2,1)}, u32[]{:S(2)}) copy-start(bf16[2048,2176]{1,0:T(8,128)(2,1)} %all-gather.3.cloned.1.call-done) | copy-start | bytes 26738692
  93.1 2.2 copy-start.2
  165.0 2.1 copy-start
  167.1 71.9 %copy-start.7 = (bf16[4,4,4096]{2,1,0:T(4,128)(2,1)S(1)}, bf16[4,4,4096]{2,1,0:T(4,128)(2,1)}, u32[]{:S(2)}) copy-start(bf16[4,4,4096]{2,1,0:T(4,128)(2,1)} %param.20) | copy-start | bytes 393220
  167.1 93.1 %all-to-all-start = ((bf16[128,8,2176]{2,1,0:T(8,128)(2,1)}), bf16[128,8,2176]{2,1,0:T(8,128)(2,1)}, u32[]{:S(2)}, u32[]{:S(2)}) async-start(bf16[128,8,2176]{2,1,0:T(8,128)(2,1)} %bitcast.39), calls=%async_computation | async-start | bytes 8912896 | tf_op jit(solution)/shard_map/all_to_all | solution.py:362
  174.2 47.8 %collective-permute-start.5 = (bf16[16,128]{1,0:T(8,128)(2,1)S(1)}, bf16[16,128]{1,0:T(8,128)(2,1)S(1)}, u32[]{:S(2)}, u32[]{:S(2)}) collective-permute-start(bf16[16,128]{1,0:T(8,128)(2,1)S(1)} %bitcast.52), channel_id=1, source_target_pairs={{6,0},{7,1},{0,2},{1,3},{2,4},{3,5},{4,6},{5,7},{14,8},{15,9},{8,1... | collective-permute-start | bytes 12296 | tf_op jit(solution)/shard_map/ppermute | solution.py:323
  175.6 46.4 %collective-permute-start.6 = (bf16[16,128]{1,0:T(8,128)(2,1)S(1)}, bf16[16,128]{1,0:T(8,128)(2,1)S(1)}, u32[]{:S(2)}, u32[]{:S(2)}) collective-permute-start(bf16[16,128]{1,0:T(8,128)(2,1)S(1)} %bitcast.53), channel_id=1, source_target_pairs={{7,0},{0,1},{1,2},{2,3},{3,4},{4,5},{5,6},{6,7},{15,8},{8,9},{9,10... | collective-permute-start | bytes 12296 | tf_op jit(solution)/shard_map/ppermute | solution.py:323
  226.6 7.9 %collective-permute-start.7 = (bf16[16,4096]{1,0:T(8,128)(2,1)}, bf16[16,4096]{1,0:T(8,128)(2,1)S(1)}, u32[]{:S(2)}, u32[]{:S(2)}) collective-permute-start(bf16[16,4096]{1,0:T(8,128)(2,1)} %get-tuple-element.17), channel_id=1, source_target_pairs={{0,1},{1,2},{2,3},{3,4},{4,5},{5,6},{6,7},{7,0},{8,9},{9,10},{10,1... | collective-permute-start | bytes 393224 | tf_op jit(solution)/shard_map/ppermute | solution.py:330
  227.3 10.3 %collective-permute-start.8 = (bf16[16,4096]{1,0:T(8,128)(2,1)}, bf16[16,4096]{1,0:T(8,128)(2,1)S(1)}, u32[]{:S(2)}, u32[]{:S(2)}) collective-permute-start(bf16[16,4096]{1,0:T(8,128)(2,1)} %get-tuple-element.18), channel_id=1, source_target_pairs={{0,2},{1,3},{2,4},{3,5},{4,6},{5,7},{6,0},{7,1},{8,10},{9,11},{10,... | collective-permute-start | bytes 393224 | tf_op jit(solution)/shard_map/ppermute | solution.py:330
  228.7 24.4 %collective-permute-start.9 = (bf16[16,4096]{1,0:T(8,128)(2,1)}, bf16[16,4096]{1,0:T(8,128)(2,1)S(1)}, u32[]{:S(2)}, u32[]{:S(2)}) collective-permute-start(bf16[16,4096]{1,0:T(8,128)(2,1)} %get-tuple-element.19), channel_id=1, source_target_pairs={{0,3},{1,4},{2,5},{3,6},{4,7},{5,0},{6,1},{7,2},{8,11},{9,12},{10,... | collective-permute-start | bytes 393224 | tf_op jit(solution)/shard_map/ppermute | solution.py:330
  230.6 22.6 %collective-permute-start.10 = (bf16[16,4096]{1,0:T(8,128)(2,1)}, bf16[16,4096]{1,0:T(8,128)(2,1)S(1)}, u32[]{:S(2)}, u32[]{:S(2)}) collective-permute-start(bf16[16,4096]{1,0:T(8,128)(2,1)} %get-tuple-element.20), channel_id=1, source_target_pairs={{0,4},{1,5},{2,6},{3,7},{4,0},{5,1},{6,2},{7,3},{8,12},{9,13},{10,... | collective-permute-start | bytes 393224 | tf_op jit(solution)/shard_map/ppermute | solution.py:330
  232.0 21.2 %collective-permute-start.11 = (bf16[16,4096]{1,0:T(8,128)(2,1)}, bf16[16,4096]{1,0:T(8,128)(2,1)S(1)}, u32[]{:S(2)}, u32[]{:S(2)}) collective-permute-start(bf16[16,4096]{1,0:T(8,128)(2,1)} %get-tuple-element.21), channel_id=1, source_target_pairs={{0,5},{1,6},{2,7},{3,0},{4,1},{5,2},{6,3},{7,4},{8,13},{9,14},{10,... | collective-permute-start | bytes 393224 | tf_op jit(solution)/shard_map/ppermute | solution.py:330
  234.5 18.7 %copy-start.8 = (bf16[16,4096]{1,0:T(8,128)(2,1)}, bf16[16,4096]{1,0:T(8,128)(2,1)S(1)}, u32[]{:S(2)}) copy-start(bf16[16,4096]{1,0:T(8,128)(2,1)S(1)} %collective-permute-done.7.refs_1_) | copy-start | bytes 393220
  234.5 18.7 %collective-permute-start.12 = (bf16[16,4096]{1,0:T(8,128)(2,1)}, bf16[16,4096]{1,0:T(8,128)(2,1)S(1)}, u32[]{:S(2)}, u32[]{:S(2)}) collective-permute-start(bf16[16,4096]{1,0:T(8,128)(2,1)} %get-tuple-element.22), channel_id=1, source_target_pairs={{0,6},{1,7},{2,0},{3,1},{4,2},{5,3},{6,4},{7,5},{8,14},{9,15},{10,... | collective-permute-start | bytes 393224 | tf_op jit(solution)/shard_map/ppermute | solution.py:330
  237.6 15.6 %copy-start.9 = (bf16[16,4096]{1,0:T(8,128)(2,1)}, bf16[16,4096]{1,0:T(8,128)(2,1)S(1)}, u32[]{:S(2)}) copy-start(bf16[16,4096]{1,0:T(8,128)(2,1)S(1)} %collective-permute-done.8.refs_2_) | copy-start | bytes 393220
  237.6 15.6 %collective-permute-start.13 = (bf16[16,4096]{1,0:T(8,128)(2,1)}, bf16[16,4096]{1,0:T(8,128)(2,1)S(1)}, u32[]{:S(2)}, u32[]{:S(2)}) collective-permute-start(bf16[16,4096]{1,0:T(8,128)(2,1)} %get-tuple-element.23), channel_id=1, source_target_pairs={{0,7},{1,0},{2,1},{3,2},{4,3},{5,4},{6,5},{7,6},{8,15},{9,8},{10,9... | collective-permute-start | bytes 393224 | tf_op jit(solution)/shard_map/ppermute | solution.py:330
  237.7 15.6 %copy-start.15 = (f32[20,4,64]{2,1,0:T(4,128)}, f32[20,4,64]{2,1,0:T(4,128)S(1)}, u32[]{:S(2)}) copy-start(f32[20,4,64]{2,1,0:T(4,128)S(1)} %constant_dynamic-update-slice_fusion) | copy-start | bytes 61444
  253.2 0.7 copy-start.10
  253.2 0.7 copy-start.11
  253.2 0.7 copy-start.12
  253.2 0.7 copy-start.13
  253.2 0.8 copy-start.14
  260.2 0.9 copy-start.3
  261.1 0.9 copy-start.4
  262.0 0.9 copy-start.5
  (1 other events, 0.6 us)
Sparse Core Ops, SparseCore 0:
  11.5 74.0 all-gather.2

commit v2 on v1

--- a/solution.py
+++ b/solution.py
@@ -21,8 +21,10 @@
 ST = 128
 MF = MH * MD
 NPG = 8
-BATCH = 8
+BATCH = 16
 NB = DEV // BATCH
+JOBS = 2 * BATCH
+LANES = JOBS * STEPS
 BLK = FEAT + 128
 NEG = -1e30
 SCALE = 1.0 / math.sqrt(HD)
@@ -86,14 +88,14 @@
     )(q, nk, nv, local_kv)
 
 
-def owner_kernel(slot_ref, kreq_ref, sel_ref, q_ref, kv_ref, o_ref, kbuf, vbuf, sem):
+def owner_kernel(slot_ref, cnt_ref, sel_ref, tile_ref, q_ref, kv_ref, o_ref, kbuf, vbuf, qbuf, sbuf, sem):
     step = pl.program_id(0)
-    pages = 2 * BATCH
+    now = lax.rem(step, 2)
 
     def copies(at, buf):
         out = []
-        for j in range(pages):
-            page = slot_ref[at * pages + j]
+        for j in range(JOBS):
+            page = slot_ref[at * JOBS + j]
             out.append(pltpu.make_async_copy(kv_ref.at[page, 0], kbuf.at[buf, j], sem.at[buf, 0, j]))
             out.append(pltpu.make_async_copy(kv_ref.at[page, 1], vbuf.at[buf, j], sem.at[buf, 1, j]))
         return out
@@ -103,71 +105,72 @@
         for c in copies(0, 0):
             c.start()
 
-    now = lax.rem(step, 2)
-
     @pl.when(step + 1 < NB)
     def _():
         for c in copies(step + 1, 1 - now):
             c.start()
 
+    q = q_ref[:, :, :FEAT].reshape(BATCH * ROWS, FEAT)
+    qbuf[...] = dot(sel_ref[...], q).astype(BF)
     for c in copies(step, now):
         c.wait()
-    rows = BATCH * ROWS
-    keys = pages * TOK
-    row = lax.broadcasted_iota(jnp.int32, (rows, 1), 0)
-    mine = (row // ROWS) * RD + row % RD
-    ok = mine == kreq_ref[0]
-    lane = lax.broadcasted_iota(jnp.int32, (rows, HD), 1)
-    tops = jnp.zeros((rows, HD), F32)
-    sums = jnp.zeros((rows, HD), F32)
-    sel = sel_ref[...]
+    lane = lax.broadcasted_iota(jnp.int32, (JOBS, TOK, LANES), 2)
+    job = lax.broadcasted_iota(jnp.int32, (JOBS, TOK, LANES), 0)
+    here = job == lane // STEPS
     for h in range(HEADS):
         at = slice(h * HD, (h + 1) * HD)
-        q = q_ref[:, :, at].reshape(rows, HD)
-        k = kbuf[now, :, :, at].reshape(keys, HD)
-        v = vbuf[now, :, :, at].reshape(keys, HD)
-        s = jnp.where(ok, dot(q, k, NT) * SCALE, NEG)
-        top = jnp.max(s, axis=1, keepdims=True)
-        p = jnp.where(ok, jnp.exp(s - top), 0.0)
-        tops = jnp.where(lane == h, top, tops)
-        sums = jnp.where(lane == h, jnp.sum(p, axis=1, keepdims=True), sums)
-        out = dot(p.astype(BF), v).astype(BF)
-        o_ref[:, at] = dot(sel, out).astype(BF)
-    parts = list(split3(tops)) + list(split2(sums))
-    stats = jnp.zeros((rows, HD), F32)
-    for i, part in enumerate(parts):
-        wide = part.astype(F32)
-        if i:
-            wide = pltpu.roll(wide, HEADS * i, 1)
-        stats = stats + wide
-    o_ref[:, FEAT:] = dot(sel, stats.astype(BF)).astype(BF)
-
-
-def owner_attention(slots, kreq, sel, gathered, kv_store):
-    rows = BATCH * 2 * STEPS
+        k = kbuf[now, :, :, at].reshape(JOBS * TOK, HD)
+        s = dot(k, qbuf[:, at], NT).reshape(JOBS, TOK, LANES)
+        sbuf[h] = jnp.sum(jnp.where(here, s, 0.0), axis=0)
+    tok = lax.broadcasted_iota(jnp.int32, (HEADS, TOK, LANES), 1)
+    ok = tok < cnt_ref[...]
+    s = jnp.where(ok, sbuf[...] * SCALE, NEG)
+    top = jnp.max(s, axis=1, keepdims=True)
+    p = jnp.where(ok, jnp.exp(s - top), 0.0)
+    total = jnp.sum(p, axis=1)
+    top = jnp.max(s, axis=1)
+    parts = [x.astype(F32) for x in list(split3(top)) + list(split2(total))]
+    parts.append(jnp.zeros((HD - HEADS * len(parts), LANES), F32))
+    o_ref[:, FEAT:] = jnp.transpose(jnp.concatenate(parts, axis=0)).astype(BF)
+    pt = jnp.transpose(p.reshape(HEADS * TOK, LANES)).astype(BF)
+    row = lax.broadcasted_iota(jnp.int32, (LANES, JOBS * TOK), 0)
+    key = lax.broadcasted_iota(jnp.int32, (LANES, JOBS * TOK), 1)
+    own = row // STEPS == key // TOK
+    for h in range(HEADS):
+        at = slice(h * HD, (h + 1) * HD)
+        w = dot(pt, tile_ref[h])
+        w = jnp.where(own, w, 0.0).astype(BF)
+        v = vbuf[now, :, :, at].reshape(JOBS * TOK, HD)
+        o_ref[:, at] = dot(w, v).astype(BF)
+
+
+def owner_attention(slots, counts, sel, tile, gathered, kv_store):
     return pl.pallas_call(
         owner_kernel,
         grid_spec=pltpu.PrefetchScalarGridSpec(
             num_scalar_prefetch=1,
             grid=(NB,),
             in_specs=[
-                pl.BlockSpec((1, 1, 2 * BATCH * TOK), lambda i, s: (i, 0, 0)),
-                pl.BlockSpec((rows, BATCH * ROWS), lambda i, s: (i, 0)),
+                pl.BlockSpec((1, 1, LANES), lambda i, s: (i, 0, 0)),
+                pl.BlockSpec((LANES, BATCH * ROWS), lambda i, s: (i, 0)),
+                pl.BlockSpec((HEADS, HEADS * TOK, JOBS * TOK), lambda i, s: (0, 0, 0)),
                 pl.BlockSpec((BATCH, ROWS, BLK), lambda i, s: (i, 0, 0)),
                 pl.BlockSpec(memory_space=pl.ANY),
             ],
-            out_specs=pl.BlockSpec((rows, BLK), lambda i, s: (i, 0)),
+            out_specs=pl.BlockSpec((LANES, BLK), lambda i, s: (i, 0)),
             scratch_shapes=[
-                pltpu.VMEM((2, 2 * BATCH, TOK, FEAT), BF),
-                pltpu.VMEM((2, 2 * BATCH, TOK, FEAT), BF),
-                pltpu.SemaphoreType.DMA((2, 2, 2 * BATCH)),
+                pltpu.VMEM((2, JOBS, TOK, FEAT), BF),
+                pltpu.VMEM((2, JOBS, TOK, FEAT), BF),
+                pltpu.VMEM((LANES, FEAT), BF),
+                pltpu.VMEM((HEADS, TOK, LANES), F32),
+                pltpu.SemaphoreType.DMA((2, 2, JOBS)),
             ],
         ),
         out_shape=jax.ShapeDtypeStruct((DEV * 2 * STEPS, BLK), BF),
-        cost_estimate=pl.CostEstimate(flops=4 * 2048 * 128 * 2048, bytes_accessed=30_000_000, transcendentals=4_000_000),
+        cost_estimate=pl.CostEstimate(flops=4 * 2048 * 128 * 2048, bytes_accessed=30_000_000, transcendentals=200_000),
         compiler_params=pltpu.CompilerParams(vmem_limit_bytes=32 * 1024 * 1024),
         name="owner_attention",
-    )(slots, kreq, sel, gathered, kv_store)
+    )(slots, counts, sel, tile, gathered, kv_store)
 
 
 def combine_kernel(own_ref, got_ref, o_ref, m_ref, l_ref, out_ref):
@@ -333,6 +336,7 @@
 
     o, m, l = local_attention(q, nk, nv, local_kv)
 
+    gathered, o, m, l, mamba_out = lax.optimization_barrier((gathered, o, m, l, mamba_out))
     mine = (jnp.arange(DEV, dtype=jnp.int32) == me).astype(BF)
     col = jnp.einsum("drl,l->rd", gathered[:, : 2 * RD, FEAT:], mine, preferred_element_type=F32).astype(jnp.int32)
     c_slot, c_count = col[:RD], col[RD:]
@@ -350,15 +354,18 @@
     at_req = jnp.stack(at_req, axis=1)
     near = jnp.arange(DEV, dtype=jnp.int32)[:, None] % BATCH
     full = jnp.where(at_count > 0, near * RD + at_req, -1)
-    tok = jnp.arange(TOK, dtype=jnp.int32)
-    kreq = jnp.where(tok[None, None, :] < at_count[:, :, None], full[:, :, None], -1).reshape(NB, 1, 2 * BATCH * TOK)
+    counts = jnp.broadcast_to(at_count[:, :, None], (DEV, 2, STEPS)).reshape(NB, 1, LANES)
+    tile_h = jnp.arange(HEADS, dtype=jnp.int32)[:, None, None]
+    tile_r = jnp.arange(HEADS * TOK, dtype=jnp.int32)[None, :, None]
+    tile_k = jnp.arange(JOBS * TOK, dtype=jnp.int32)[None, None, :]
+    tile = ((tile_r // TOK == tile_h) & (tile_r % TOK == tile_k % TOK)).astype(BF)
     lane = jnp.arange(BATCH * ROWS, dtype=jnp.int32)
     lane_req = (lane // ROWS) * RD + lane % RD
     lane_step = (lane // RD) % STEPS
     steps = jnp.arange(STEPS, dtype=jnp.int32)
     sel = (full[:, :, None, None] == lane_req) & (steps[None, None, :, None] == lane_step)
     sel = sel.astype(BF).reshape(DEV * 2 * STEPS, BATCH * ROWS)
-    part = owner_attention(at_slot.reshape(-1), kreq, sel, gathered, kv_store)
+    part = owner_attention(at_slot.reshape(-1), counts, sel, tile, gathered, kv_store)
     got = lax.all_to_all(part.reshape(DEV, 2 * STEPS, BLK), ("req", "page"), 0, 0, tiled=True)
 
     own_hit = (t_count > 0).astype(jnp.int32)

time: 276 us -> 210 us (0.76)
  Pallas kernels: 95.2 us -> 63.7 us
  waiting for transfers between devices: 111 us -> 80.9 us
    all_to_all x1, waiting for transfers between devices: 0.01 us -> 53.9 us  [on_device(): lax.all_to_all(part.reshape(DEV, 2 * STEPS, BLK), ('req', 'page'), 0, 0,...]
    ppermute x7, waiting for transfers between devices: 44.6 us -> 2.27 us  [on_device(): lax.ppermute(c_own, 'page', [((i + k) % NPG, i) for i in range(NPG)])]
    all_gather x1, waiting for transfers between devices: 63.1 us -> 21.8 us  [on_device(): gathered = lax.all_gather(block[None], ('req', 'page'), axis=0, tiled=True)]
    pallas_call x1, Pallas kernels: 69.7 us -> 38.2 us  [owner_attention(): pl.pallas_call(owner_kernel, grid_spec=pltpu.PrefetchScalarGridSpec(num_s...]
  transfers between devices with their start and end apart: 16 -> 16, of which waited for: 3 -> 5; matrix products, arithmetic and copies ran while one was open for 5% -> 5% of each run, Pallas kernels for 33% -> 10%
where the time goes in v2:
time: 210 us; the launch traced here: 209 us
  waiting for transfers between devices  80.9 us (39%)
  Pallas kernels  63.7 us (30%)
  starting transfers between devices  22.6 us (11%)
  local copies, waits for them, and re-layouts  18.9 us (9%)
  between operations  14.5 us (7%)
  other arithmetic  6 us (3%)
  matrix products  2.3 us (1%)
    all_to_all x1, waiting for transfers between devices, on_device(): lax.all_to_all(part.reshape(DEV, 2 * STEPS, BLK), ('req', 'page'), 0, 0,...  53.9 us
    pallas_call x1, Pallas kernels, owner_attention(): pl.pallas_call(owner_kernel, grid_spec=pltpu.PrefetchScalarGridSpec(num_s...  38.2 us
    all_gather x1, waiting for transfers between devices, on_device(): gathered = lax.all_gather(block[None], ('req', 'page'), axis=0, tiled=True)  21.8 us
    pallas_call x1, Pallas kernels, local_attention(): pl.pallas_call(local_kernel, grid=(HEADS,), in_specs=[row, row, row, pl.B...  13.5 us
    ppermute x7, starting transfers between devices, on_device(): lax.ppermute(c_own, 'page', [((i + k) % NPG, i) for i in range(NPG)])  9.7 us
    unnamed x46, local copies, waits for them, and re-layouts  9.26 us
    ppermute x7, starting transfers between devices, on_device(): lax.ppermute(z_out[k], 'page', [(i, (i + k) % NPG) for i in range(NPG)])  7.09 us
    all_to_all x1, starting transfers between devices, on_device(): lax.all_to_all(part.reshape(DEV, 2 * STEPS, BLK), ('req', 'page'), 0, 0,...  5.73 us
  transfers between devices with their start and end apart: 16, of which 5 were waited for; matrix products, arithmetic and copies ran while one was open for 5% of the time, Pallas kernels for 10%

profile of v2, /device:TPU:1, one launch (start us, length us, event | category | flops | bytes accessed | tf_op | source)
XLA Modules:
  0.0 208.9 jit_solution(6484590220900233864)
XLA Ops:
  7.2 1.0 fusion.22
  8.2 0.8 subtract_clamp_fusion
  9.0 0.8 select_reduce_fusion
  10.5 0.7 fusion.23
  11.2 1.4 collective-permute-start
  12.7 2.6 %collective-permute-start.1 = (bf16[16,128]{1,0:T(8,128)(2,1)S(1)}, bf16[16,128]{1,0:T(8,128)(2,1)S(1)}, u32[]{:S(2)}, u32[]{:S(2)}) collective-permute-start(bf16[16,128]{1,0:T(8,128)(2,1)S(1)} %bitcast.45), channel_id=1, source_target_pairs={{2,0},{3,1},{4,2},{5,3},{6,4},{7,5},{0,6},{1,7},{10,8},{11,9},{12,... | collective-permute-start | bytes 12296 | tf_op jit(solution)/shard_map/ppermute | solution.py:326
  15.2 0.8 collective-permute-start.2
  16.0 2.4 %collective-permute-start.3 = (bf16[16,128]{1,0:T(8,128)(2,1)S(1)}, bf16[16,128]{1,0:T(8,128)(2,1)S(1)}, u32[]{:S(2)}, u32[]{:S(2)}) collective-permute-start(bf16[16,128]{1,0:T(8,128)(2,1)S(1)} %bitcast.47), channel_id=1, source_target_pairs={{4,0},{5,1},{6,2},{7,3},{0,4},{1,5},{2,6},{3,7},{12,8},{13,9},{14,... | collective-permute-start | bytes 12296 | tf_op jit(solution)/shard_map/ppermute | solution.py:326
  18.4 0.9 collective-permute-start.4
  19.9 0.7 reshape.580
  25.0 1.1 collective-permute-start.6
  26.1 2.3 %collective-permute-done.5 = bf16[16,128]{1,0:T(8,128)(2,1)S(1)} collective-permute-done((bf16[16,128]{1,0:T(8,128)(2,1)S(1)}, bf16[16,128]{1,0:T(8,128)(2,1)S(1)}, u32[]{:S(2)}, u32[]{:S(2)}) %collective-permute-start.5) | collective-permute-done | bytes 4128 | tf_op jit(solution)/shard_map/ppermute | solution.py:326
  29.0 4.1 %state_products.1 = (bf16[16,4096]{1,0:T(8,128)(2,1)}, bf16[16,4096]{1,0:T(8,128)(2,1)}, bf16[16,4096]{1,0:T(8,128)(2,1)}, bf16[16,4096]{1,0:T(8,128)(2,1)}, bf1...) custom-call(s32[128,1]{1,0:T(8,128)} %reshape.602.br_ref, ...), custom_call_target="tpu_custom_call" | custom-call | flops 268435456 | bytes 3200000 | tf_op jit(solution)/shard_map/state_products/pallas_call | solution.py:222
  33.0 1.1 collective-permute-start.10
  34.1 2.3 %collective-permute-start.11 = (bf16[16,4096]{1,0:T(8,128)(2,1)}, bf16[16,4096]{1,0:T(8,128)(2,1)S(1)}, u32[]{:S(2)}, u32[]{:S(2)}) collective-permute-start(bf16[16,4096]{1,0:T(8,128)(2,1)} %get-tuple-element.26), channel_id=1, source_target_pairs={{0,5},{1,6},{2,7},{3,0},{4,1},{5,2},{6,3},{7,4},{8,13},{9,14},{10,... | collective-permute-start | bytes 393224 | tf_op jit(solution)/shard_map/ppermute | solution.py:333
  37.1 1.7 collective-permute-start.7
  38.8 0.7 collective-permute-done.10.refs_4_
  39.8 2.2 %collective-permute-done.11.refs_5_ = bf16[16,4096]{1,0:T(8,128)(2,1)S(1)} collective-permute-done((bf16[16,4096]{1,0:T(8,128)(2,1)}, bf16[16,4096]{1,0:T(8,128)(2,1)S(1)}, u32[]{:S(2)}, u32[]{:S(2)}) %collective-permute-start.11) | collective-permute-done | bytes 131104 | tf_op jit(solution)/shard_map/ppermute | solution.py:333
  42.0 1.1 collective-permute-start.9
  43.1 1.6 reshape.579.x_ref
  46.0 13.5 %local_attention.1 = (f32[16,2048]{1,0:T(8,128)}, f32[16,2048]{1,0:T(8,128)}, f32[16,2048]{1,0:T(8,128)}) custom-call(bf16[16,2048]{1,0:T(8,128)(2,1)} %copy-done.6, bf16[16,2048]{1,0:T(8,128)(2,1)} %reshape_squeeze.10.nk_ref, bf16[16,2048]{1,0:T(8,128)(2,1)} %reshape_squeeze.11.nv_ref, bf16[4,2,256,2048]{3,2,1,0:T(8,128)(2,1)} %kv_ref.2), custom_call_target="tpu_custom_call" | custom-call | flops 134217728 | bytes 9000000 | tf_op jit(solution)/shard_map/local_attention/pallas_call | solution.py:80
  60.4 3.7 %scan_outputs.1 = bf16[16,4096]{1,0:T(8,128)(2,1)} custom-call(f32[80,64]{1,0:T(8,128)} %bitcast.43, bf16[16,4096]{1,0:T(8,128)(2,1)} %reshape.579.x_ref, bf16[16,4096]{1,0:T(8,128)(2,1)} %get-tuple-element.21.refs_0_, bf16[16,4096]{1,0:T(8,128)(2,1)} %copy-done.12, bf16[16,4096]{1,0:T(8,128)(2,1)} %copy-done.13, bf16[16,4096]{1,0:T(8,128)(2,1)} %copy-done.14, ...), custom_call_target="tpu_custom_call" | custom-call | flops 125829120 | bytes 1500000 | tf_op jit(solution)/shard_map/scan_outputs/pallas_call | solution.py:259
  64.1 21.8 %all-gather.3.cloned.1.call-done = bf16[2048,2176]{1,0:T(8,128)(2,1)} async-done(((bf16[16,2176]{1,0:T(8,128)(2,1)}), bf16[2048,2176]{1,0:T(8,128)(2,1)}) %all-gather.3.cloned.1.call-update) | async-done | bytes 8912912 | tf_op jit(solution)/shard_map/all_gather | solution.py:321
  85.9 2.2 %fusion = f32[1,128,8]{2,0,1:T(1,128)S(1)} fusion(bf16[128,16,2176]{2,1,0:T(8,128)(2,1)} %bitcast.39, s32[]{:T(128)S(6)} %add.215), kind=kOutput, calls=%fused_computation.4 | convolution fusion | flops 262272 | bytes 266244 | tf_op jit(solution)/shard_map/drl,l->rd/dot_general | solution.py:341
  89.9 3.5 %copy-done.1 = bf16[2048,2176]{1,0:T(8,128)(2,1)S(1)} copy-done((bf16[2048,2176]{1,0:T(8,128)(2,1)S(1)}, bf16[2048,2176]{1,0:T(8,128)(2,1)}, u32[]{:S(2)}) %copy-start.1) | copy-done | bytes 8912920
  93.5 2.2 %copy-done.2 = bf16[64,2,8,2048]{3,2,1,0:T(8,128)(2,1)S(1)} copy-done((bf16[64,2,8,2048]{3,2,1,0:T(8,128)(2,1)S(1)}, bf16[64,2,8,2048]{3,2,1,0:T(8,128)(2,1)}, u32[]{:S(2)}) %copy-start.2) | copy-done | bytes 4194328
  95.6 38.2 %owner_attention.1 = bf16[1024,2176]{1,0:T(8,128)(2,1)S(1)} custom-call(s32[256]{0:T(256)S(1)} %reshape.584.slot_ref, s32[8,1,128]{2,1,0:T(1,128)S(1)} %bitcast.41, bf16[1024,256]{1,0:T(8,128)(2,1)S(1)} %reshape.590.sel_ref, bf16[16,128,256]{2,1,0:T(8,128)(2,1)S(1)} %and_convert_fusion.tile_ref, bf16[128,16,2176]{2,1,0:T(8,128)(2,1)S(1)} %bitcast.40, ...), custom_call_target="tpu_custom_call" | custom-call | flops 2147483648 | bytes 30000000 | tf_op jit(solution)/shard_map/owner_attention/pallas_call | solution.py:148
  133.8 2.1 copy-done
  135.9 5.7 %all-to-all-start = ((bf16[128,8,2176]{2,1,0:T(8,128)(2,1)}), bf16[128,8,2176]{2,1,0:T(8,128)(2,1)}, u32[]{:S(2)}, u32[]{:S(2)}) async-start(bf16[128,8,2176]{2,1,0:T(8,128)(2,1)} %bitcast.38), calls=%async_computation | async-start | bytes 8912896 | tf_op jit(solution)/shard_map/all_to_all | solution.py:369
  142.5 0.7 reshape.589
  143.3 53.9 %all-to-all-done = bf16[128,8,2176]{2,1,0:T(8,128)(2,1)} async-done(((bf16[128,8,2176]{2,1,0:T(8,128)(2,1)}), bf16[128,8,2176]{2,1,0:T(8,128)(2,1)}, u32[]{:S(2)}, u32[]{:S(2)}) %all-to-all-start) | async-done | bytes 4456480 | tf_op jit(solution)/shard_map/all_to_all | solution.py:369
  197.2 4.2 %combine_attention.1 = bf16[16,2048]{1,0:T(8,128)(2,1)S(1)} custom-call(s32[1,1024]{1,0:T(1,128)S(1)} %select_n.164.own_ref, bf16[1024,2176]{1,0:T(8,128)(2,1)} %bitcast.19.got_ref, f32[16,2048]{1,0:T(8,128)S(1)} %copy-done.3, f32[16,2048]{1,0:T(8,128)S(1)} %copy-done.4, f32[16,2048]{1,0:T(8,128)S(1)} %copy-done.5), custom_call_target="tpu_custom_call" | custom-call | flops 134217728 | bytes 5000000 | tf_op jit(solution)/shard_map/combine_attention/pallas_call | solution.py:200
  (132 shorter events, 12.4 us)
Async XLA Ops:
  7.2 78.7 %all-gather.3.cloned.1.call-start = ((), (), s32[]{:S(2)}) async-start(), calls=%async_computation.1 | async-start | bytes 8982528 | tf_op jit(solution)/shard_map/all_gather | solution.py:321
  8.2 37.8 %copy-start.6 = (bf16[16,2048]{1,0:T(8,128)(2,1)}, bf16[16,2048]{1,0:T(8,128)(2,1)S(1)}, u32[]{:S(2)}) copy-start(bf16[16,2048]{1,0:T(8,128)(2,1)S(1)} %reshape_squeeze.9.q_ref) | copy-start | bytes 196612
  11.2 13.2 %collective-permute-start = (bf16[16,128]{1,0:T(8,128)(2,1)S(1)}, bf16[16,128]{1,0:T(8,128)(2,1)S(1)}, u32[]{:S(2)}, u32[]{:S(2)}) collective-permute-start(bf16[16,128]{1,0:T(8,128)(2,1)S(1)} %bitcast.44), channel_id=1, source_target_pairs={{1,0},{2,1},{3,2},{4,3},{5,4},{6,5},{7,6},{0,7},{9,8},{10,9},{11,1... | collective-permute-start | bytes 12296 | tf_op jit(solution)/shard_map/ppermute | solution.py:326
  12.7 12.3 %collective-permute-start.1 = (bf16[16,128]{1,0:T(8,128)(2,1)S(1)}, bf16[16,128]{1,0:T(8,128)(2,1)S(1)}, u32[]{:S(2)}, u32[]{:S(2)}) collective-permute-start(bf16[16,128]{1,0:T(8,128)(2,1)S(1)} %bitcast.45), channel_id=1, source_target_pairs={{2,0},{3,1},{4,2},{5,3},{6,4},{7,5},{0,6},{1,7},{10,8},{11,9},{12,... | collective-permute-start | bytes 12296 | tf_op jit(solution)/shard_map/ppermute | solution.py:326
  15.2 10.8 %collective-permute-start.2 = (bf16[16,128]{1,0:T(8,128)(2,1)S(1)}, bf16[16,128]{1,0:T(8,128)(2,1)S(1)}, u32[]{:S(2)}, u32[]{:S(2)}) collective-permute-start(bf16[16,128]{1,0:T(8,128)(2,1)S(1)} %bitcast.46), channel_id=1, source_target_pairs={{3,0},{4,1},{5,2},{6,3},{7,4},{0,5},{1,6},{2,7},{11,8},{12,9},{13,... | collective-permute-start | bytes 12296 | tf_op jit(solution)/shard_map/ppermute | solution.py:326
  16.0 10.1 %collective-permute-start.3 = (bf16[16,128]{1,0:T(8,128)(2,1)S(1)}, bf16[16,128]{1,0:T(8,128)(2,1)S(1)}, u32[]{:S(2)}, u32[]{:S(2)}) collective-permute-start(bf16[16,128]{1,0:T(8,128)(2,1)S(1)} %bitcast.47), channel_id=1, source_target_pairs={{4,0},{5,1},{6,2},{7,3},{0,4},{1,5},{2,6},{3,7},{12,8},{13,9},{14,... | collective-permute-start | bytes 12296 | tf_op jit(solution)/shard_map/ppermute | solution.py:326
  18.4 7.7 %collective-permute-start.4 = (bf16[16,128]{1,0:T(8,128)(2,1)S(1)}, bf16[16,128]{1,0:T(8,128)(2,1)S(1)}, u32[]{:S(2)}, u32[]{:S(2)}) collective-permute-start(bf16[16,128]{1,0:T(8,128)(2,1)S(1)} %bitcast.48), channel_id=1, source_target_pairs={{5,0},{6,1},{7,2},{0,3},{1,4},{2,5},{3,6},{4,7},{13,8},{14,9},{15,... | collective-permute-start | bytes 12296 | tf_op jit(solution)/shard_map/ppermute | solution.py:326
  23.2 36.4 %copy-start.15 = (f32[20,4,64]{2,1,0:T(4,128)}, f32[20,4,64]{2,1,0:T(4,128)S(1)}, u32[]{:S(2)}) copy-start(f32[20,4,64]{2,1,0:T(4,128)S(1)} %constant_dynamic-update-slice_fusion) | copy-start | bytes 61444
  24.4 4.0 %collective-permute-start.5 = (bf16[16,128]{1,0:T(8,128)(2,1)S(1)}, bf16[16,128]{1,0:T(8,128)(2,1)S(1)}, u32[]{:S(2)}, u32[]{:S(2)}) collective-permute-start(bf16[16,128]{1,0:T(8,128)(2,1)S(1)} %bitcast.50), channel_id=1, source_target_pairs={{6,0},{7,1},{0,2},{1,3},{2,4},{3,5},{4,6},{5,7},{14,8},{15,9},{8,1... | collective-permute-start | bytes 12296 | tf_op jit(solution)/shard_map/ppermute | solution.py:326
  25.0 3.4 %collective-permute-start.6 = (bf16[16,128]{1,0:T(8,128)(2,1)S(1)}, bf16[16,128]{1,0:T(8,128)(2,1)S(1)}, u32[]{:S(2)}, u32[]{:S(2)}) collective-permute-start(bf16[16,128]{1,0:T(8,128)(2,1)S(1)} %bitcast.51), channel_id=1, source_target_pairs={{7,0},{0,1},{1,2},{2,3},{3,4},{4,5},{5,6},{6,7},{15,8},{8,9},{9,10... | collective-permute-start | bytes 12296 | tf_op jit(solution)/shard_map/ppermute | solution.py:326
  33.0 6.5 %collective-permute-start.10 = (bf16[16,4096]{1,0:T(8,128)(2,1)}, bf16[16,4096]{1,0:T(8,128)(2,1)S(1)}, u32[]{:S(2)}, u32[]{:S(2)}) collective-permute-start(bf16[16,4096]{1,0:T(8,128)(2,1)} %get-tuple-element.25), channel_id=1, source_target_pairs={{0,4},{1,5},{2,6},{3,7},{4,0},{5,1},{6,2},{7,3},{8,12},{9,13},{10,... | collective-permute-start | bytes 393224 | tf_op jit(solution)/shard_map/ppermute | solution.py:333
  34.1 7.9 %collective-permute-start.11 = (bf16[16,4096]{1,0:T(8,128)(2,1)}, bf16[16,4096]{1,0:T(8,128)(2,1)S(1)}, u32[]{:S(2)}, u32[]{:S(2)}) collective-permute-start(bf16[16,4096]{1,0:T(8,128)(2,1)} %get-tuple-element.26), channel_id=1, source_target_pairs={{0,5},{1,6},{2,7},{3,0},{4,1},{5,2},{6,3},{7,4},{8,13},{9,14},{10,... | collective-permute-start | bytes 393224 | tf_op jit(solution)/shard_map/ppermute | solution.py:333
  36.5 23.0 %collective-permute-start.12 = (bf16[16,4096]{1,0:T(8,128)(2,1)}, bf16[16,4096]{1,0:T(8,128)(2,1)S(1)}, u32[]{:S(2)}, u32[]{:S(2)}) collective-permute-start(bf16[16,4096]{1,0:T(8,128)(2,1)} %get-tuple-element.27), channel_id=1, source_target_pairs={{0,6},{1,7},{2,0},{3,1},{4,2},{5,3},{6,4},{7,5},{8,14},{9,15},{10,... | collective-permute-start | bytes 393224 | tf_op jit(solution)/shard_map/ppermute | solution.py:333
  37.0 22.5 %collective-permute-start.13 = (bf16[16,4096]{1,0:T(8,128)(2,1)}, bf16[16,4096]{1,0:T(8,128)(2,1)S(1)}, u32[]{:S(2)}, u32[]{:S(2)}) collective-permute-start(bf16[16,4096]{1,0:T(8,128)(2,1)} %get-tuple-element.28), channel_id=1, source_target_pairs={{0,7},{1,0},{2,1},{3,2},{4,3},{5,4},{6,5},{7,6},{8,15},{9,8},{10,9... | collective-permute-start | bytes 393224 | tf_op jit(solution)/shard_map/ppermute | solution.py:333
  37.1 22.5 %collective-permute-start.7 = (bf16[16,4096]{1,0:T(8,128)(2,1)}, bf16[16,4096]{1,0:T(8,128)(2,1)S(1)}, u32[]{:S(2)}, u32[]{:S(2)}) collective-permute-start(bf16[16,4096]{1,0:T(8,128)(2,1)} %get-tuple-element.22), channel_id=1, source_target_pairs={{0,1},{1,2},{2,3},{3,4},{4,5},{5,6},{6,7},{7,0},{8,9},{9,10},{10,1... | collective-permute-start | bytes 393224 | tf_op jit(solution)/shard_map/ppermute | solution.py:333
  39.5 20.1 %copy-start.8 = (bf16[16,4096]{1,0:T(8,128)(2,1)}, bf16[16,4096]{1,0:T(8,128)(2,1)S(1)}, u32[]{:S(2)}) copy-start(bf16[16,4096]{1,0:T(8,128)(2,1)S(1)} %collective-permute-done.10.refs_4_) | copy-start | bytes 393220
  39.5 20.1 %collective-permute-start.8 = (bf16[16,4096]{1,0:T(8,128)(2,1)}, bf16[16,4096]{1,0:T(8,128)(2,1)S(1)}, u32[]{:S(2)}, u32[]{:S(2)}) collective-permute-start(bf16[16,4096]{1,0:T(8,128)(2,1)} %get-tuple-element.23), channel_id=1, source_target_pairs={{0,2},{1,3},{2,4},{3,5},{4,6},{5,7},{6,0},{7,1},{8,10},{9,11},{10,... | collective-permute-start | bytes 393224 | tf_op jit(solution)/shard_map/ppermute | solution.py:333
  42.0 17.7 %copy-start.9 = (bf16[16,4096]{1,0:T(8,128)(2,1)}, bf16[16,4096]{1,0:T(8,128)(2,1)S(1)}, u32[]{:S(2)}) copy-start(bf16[16,4096]{1,0:T(8,128)(2,1)S(1)} %collective-permute-done.11.refs_5_) | copy-start | bytes 393220
  42.0 17.6 %collective-permute-start.9 = (bf16[16,4096]{1,0:T(8,128)(2,1)}, bf16[16,4096]{1,0:T(8,128)(2,1)S(1)}, u32[]{:S(2)}, u32[]{:S(2)}) collective-permute-start(bf16[16,4096]{1,0:T(8,128)(2,1)} %get-tuple-element.24), channel_id=1, source_target_pairs={{0,3},{1,4},{2,5},{3,6},{4,7},{5,0},{6,1},{7,2},{8,11},{9,12},{10,... | collective-permute-start | bytes 393224 | tf_op jit(solution)/shard_map/ppermute | solution.py:333
  59.6 0.7 copy-start.10
  59.6 0.7 copy-start.11
  59.6 0.7 copy-start.12
  59.6 0.7 copy-start.13
  59.6 0.8 copy-start.14
  89.9 3.5 %copy-start.1 = (bf16[2048,2176]{1,0:T(8,128)(2,1)S(1)}, bf16[2048,2176]{1,0:T(8,128)(2,1)}, u32[]{:S(2)}) copy-start(bf16[2048,2176]{1,0:T(8,128)(2,1)} %all-gather.3.cloned.1.call-done) | copy-start | bytes 26738692
  93.5 2.2 %copy-start.2 = (bf16[64,2,8,2048]{3,2,1,0:T(8,128)(2,1)S(1)}, bf16[64,2,8,2048]{3,2,1,0:T(8,128)(2,1)}, u32[]{:S(2)}) copy-start(bf16[64,2,8,2048]{3,2,1,0:T(8,128)(2,1)} %kv_ref.3) | copy-start | bytes 12582916
  133.8 2.1 %copy-start = (bf16[1024,2176]{1,0:T(8,128)(2,1)}, bf16[1024,2176]{1,0:T(8,128)(2,1)S(1)}, u32[]{:S(2)}) copy-start(bf16[1024,2176]{1,0:T(8,128)(2,1)S(1)} %owner_attention.1) | copy-start | bytes 13369348
  135.9 6.6 %copy-start.7 = (bf16[16,4096]{1,0:T(8,128)(2,1)S(1)}, bf16[16,4096]{1,0:T(8,128)(2,1)}, u32[]{:S(2)}) copy-start(bf16[16,4096]{1,0:T(8,128)(2,1)} %scan_outputs.1) | copy-start | bytes 393220
  135.9 61.2 %copy-start.3 = (f32[16,2048]{1,0:T(8,128)S(1)}, f32[16,2048]{1,0:T(8,128)}, u32[]{:S(2)}) copy-start(f32[16,2048]{1,0:T(8,128)} %get-tuple-element.30.o_ref) | copy-start | bytes 393220
  135.9 61.2 %copy-start.4 = (f32[16,2048]{1,0:T(8,128)S(1)}, f32[16,2048]{1,0:T(8,128)}, u32[]{:S(2)}) copy-start(f32[16,2048]{1,0:T(8,128)} %get-tuple-element.31.m_ref) | copy-start | bytes 393220
  135.9 61.2 %copy-start.5 = (f32[16,2048]{1,0:T(8,128)S(1)}, f32[16,2048]{1,0:T(8,128)}, u32[]{:S(2)}) copy-start(f32[16,2048]{1,0:T(8,128)} %get-tuple-element.32.l_ref) | copy-start | bytes 393220
  135.9 61.2 %all-to-all-start = ((bf16[128,8,2176]{2,1,0:T(8,128)(2,1)}), bf16[128,8,2176]{2,1,0:T(8,128)(2,1)}, u32[]{:S(2)}, u32[]{:S(2)}) async-start(bf16[128,8,2176]{2,1,0:T(8,128)(2,1)} %bitcast.38), calls=%async_computation | async-start | bytes 8912896 | tf_op jit(solution)/shard_map/all_to_all | solution.py:369
  (1 other events, 0.6 us)
Sparse Core Ops, SparseCore 0:
  11.0 74.8 all-gather.2

commit v3 on v1

v3 whole, which is shorter than its diff:
```python
import functools
import math

import jax
import jax.numpy as jnp
from jax import lax
from jax.experimental import pallas as pl
from jax.experimental.pallas import tpu as pltpu
from jax.sharding import PartitionSpec as P

HEADS = 16
HD = 128
STEPS = 4
RD = 4
ROWS = STEPS * RD
FEAT = HEADS * HD
DEV = 128
TOK = 8
MH = 64
MD = 64
ST = 128
MF = MH * MD
NPG = 8
GRP = 16
PAGES = 64
JOBS = 2 * GRP
KEYS = JOBS * TOK
NEAR = 8
QROWS = 40
NEG = -1e30
SCALE = 1.0 / math.sqrt(HD)
BF = jnp.bfloat16
F32 = jnp.float32
NT = (((1,), (1,)), ((), ()))
NN = (((1,), (0,)), ((), ()))


def dot(a, b, dims=NN):
    return lax.dot_general(a, b, dims, preferred_element_type=F32)


def split2(x):
    hi = x.astype(BF)
    return hi, (x - hi.astype(F32)).astype(BF)


def split3(x):
    hi = x.astype(BF)
    rest = x - hi.astype(F32)
    mid = rest.astype(BF)
    return hi, mid, (rest - mid.astype(F32)).astype(BF)


def local_kernel(q_ref, nk_ref, nv_ref, kv_ref, o_ref, m_ref, l_ref):
    q = q_ref[...]
    parts = [dot(q, kv_ref[r, 0], NT) for r in range(RD)]
    row = lax.broadcasted_iota(jnp.int32, (ROWS, 1), 0)
    keep = row % RD
    new = dot(q, nk_ref[...], NT) * SCALE
    col = lax.broadcasted_iota(jnp.int32, (ROWS, ROWS), 1)
    ok = (col % RD == keep) & (col // RD <= row // RD)
    new = jnp.where(ok, new, NEG)
    mine = jnp.where(keep == 0, parts[0], NEG)
    for r in range(1, RD):
        mine = jnp.where(keep == r, parts[r], mine)
    mine = mine * SCALE
    top = jnp.maximum(jnp.max(mine, axis=1, keepdims=True), jnp.max(new, axis=1, keepdims=True))
    p = jnp.exp(mine - top)
    pn = jnp.where(ok, jnp.exp(new - top), 0.0)
    total = jnp.sum(p, axis=1, keepdims=True) + jnp.sum(pn, axis=1, keepdims=True)
    out = dot(pn.astype(BF), nv_ref[...])
    for r in range(RD):
        out = out + dot(jnp.where(keep == r, p, 0.0).astype(BF), kv_ref[r, 1])
    o_ref[...] = out
    m_ref[...] = jnp.broadcast_to(top, (ROWS, HD))
    l_ref[...] = jnp.broadcast_to(total, (ROWS, HD))


def local_attention(q, nk, nv, local_kv):
    row = pl.BlockSpec((ROWS, HD), lambda h: (0, h))
    return pl.pallas_call(
        local_kernel,
        grid=(HEADS,),
        in_specs=[row, row, row, pl.BlockSpec((RD, 2, 256, HD), lambda h: (0, 0, 0, h))],
        out_specs=[row, row, row],
        out_shape=[jax.ShapeDtypeStruct((ROWS, FEAT), F32)] * 3,
        cost_estimate=pl.CostEstimate(flops=2 * 2 * 16 * 1024 * 2048, bytes_accessed=9_000_000, transcendentals=300_000),
        name="local_attention",
    )(q, nk, nv, local_kv)


def owner_kernel(page_ref, req_ref, q_ref, kv_ref, o_ref, kbuf, vbuf):
    step = pl.program_id(0)
    for d in range(NEAR):
        base = (step * NEAR + d) * JOBS
        for j in range(JOBS):
            page = page_ref[base + j]
            kbuf[d, j] = kv_ref[page, 0]
            vbuf[d, j] = kv_ref[page, 1]
    row = lax.broadcasted_iota(jnp.int32, (1, ROWS, 1), 1)
    ok = row % RD == req_ref[...]
    s = [dot(q_ref[d, :ROWS], kbuf[d].reshape(KEYS, HD), NT)[None] for d in range(NEAR)]
    s = jnp.where(ok, jnp.concatenate(s, axis=0) * SCALE, NEG)
    top = jnp.max(s, axis=2, keepdims=True)
    p = jnp.where(ok, jnp.exp(s - top), 0.0)
    total = jnp.sum(p, axis=2, keepdims=True)
    p = p.astype(BF)
    lane = lax.broadcasted_iota(jnp.int32, (NEAR, ROWS, HD), 2)
    stats = jnp.zeros((NEAR, ROWS, HD), F32)
    for i, part in enumerate(list(split3(top)) + list(split2(total))):
        stats = jnp.where(lane == i, part.astype(F32), stats)
    o_ref[:, :, HD:] = stats.astype(BF)
    for d in range(NEAR):
        o_ref[d, :, :HD] = dot(p[d], vbuf[d].reshape(KEYS, HD)).astype(BF)


def owner_attention(pages, reqs, got, store):
    return pl.pallas_call(
        owner_kernel,
        grid_spec=pltpu.PrefetchScalarGridSpec(
            num_scalar_prefetch=1,
            grid=(DEV // NEAR,),
            in_specs=[
                pl.BlockSpec((NEAR, 1, KEYS), lambda i, s: (i, 0, 0)),
                pl.BlockSpec((NEAR, QROWS, HD), lambda i, s: (i, 0, 0)),
                pl.BlockSpec(store.shape, lambda i, s: (0, 0, 0, 0), pipeline_mode=pl.Buffered(1)),
            ],
            out_specs=pl.BlockSpec((NEAR, ROWS, 2 * HD), lambda i, s: (i, 0, 0)),
            scratch_shapes=[
                pltpu.VMEM((NEAR, JOBS, TOK, HD), BF),
                pltpu.VMEM((NEAR, JOBS, TOK, HD), BF),
            ],
        ),
        out_shape=jax.ShapeDtypeStruct((DEV, ROWS, 2 * HD), BF),
        cost_estimate=pl.CostEstimate(flops=4 * 2048 * 256 * 128, bytes_accessed=8_000_000, transcendentals=600_000),
        compiler_params=pltpu.CompilerParams(vmem_limit_bytes=32 * 1024 * 1024),
        name="owner_attention",
    )(pages, reqs, got, store)


def combine_kernel(got_ref, o_ref, m_ref, l_ref, out_ref):
    stats = got_ref[:, :, HD:].reshape(NPG * ROWS, HD)
    lane = lax.broadcasted_iota(jnp.int32, (HD, HD), 0)
    top = dot(stats, (lane < 3).astype(BF)).reshape(NPG, ROWS, HD)
    total = dot(stats, ((lane >= 3) & (lane < 5)).astype(BF)).reshape(NPG, ROWS, HD)
    got = got_ref[:, :, :HD].astype(F32)
    lm = m_ref[...]
    best = jnp.maximum(jnp.max(top, axis=0), lm)
    w = jnp.exp(top - best[None])
    mine = jnp.exp(lm - best)
    mix = jnp.sum(w * got, axis=0) + mine * o_ref[...]
    out_ref[...] = (mix / (jnp.sum(w * total, axis=0) + mine * l_ref[...])).astype(BF)


def combine(got, o, m, l):
    row = pl.BlockSpec((ROWS, HD), lambda h: (0, h))
    return pl.pallas_call(
        combine_kernel,
        grid=(HEADS,),
        in_specs=[pl.BlockSpec((NPG, ROWS, 2 * HD), lambda h: (h, 0, 0)), row, row, row],
        out_specs=row,
        out_shape=jax.ShapeDtypeStruct((ROWS, FEAT), BF),
        cost_estimate=pl.CostEstimate(flops=4 * 16 * 1024 * 2048, bytes_accessed=2_000_000, transcendentals=300_000),
        name="combine_attention",
    )(got, o, m, l)


def state_kernel(br_ref, c_ref, st_ref, out_ref):
    c = c_ref[...]
    first = dot(c, st_ref[0], NT)
    second = dot(c, st_ref[1], NT)
    which = br_ref[...]
    z = jnp.where(which == 0, first, 0.0) + jnp.where(which == 1, second, 0.0)
    out_ref[...] = z.astype(BF)


def state_products(which, c_all, states):
    wide = 1024
    return pl.pallas_call(
        state_kernel,
        grid=(MF // wide,),
        in_specs=[
            pl.BlockSpec((NPG * ROWS, 1), lambda i: (0, 0)),
            pl.BlockSpec((NPG * ROWS, ST), lambda i: (0, 0)),
            pl.BlockSpec((2, wide, ST), lambda i: (0, i, 0)),
        ],
        out_specs=pl.BlockSpec((NPG * ROWS, wide), lambda i: (0, i)),
        out_shape=jax.ShapeDtypeStruct((NPG * ROWS, MF), BF),
        cost_estimate=pl.CostEstimate(flops=4 * 128 * 128 * 4096, bytes_accessed=3_200_000, transcendentals=0),
        name="state_products",
    )(which, c_all, states)


def scan_kernel(coef_ref, x_ref, z_ref, out_ref):
    wide = out_ref.shape[1]
    head = lax.broadcasted_iota(jnp.int32, (MH, wide), 0)
    chan = lax.broadcasted_iota(jnp.int32, (MH, wide), 1) + pl.program_id(0) * wide
    spread = (head == chan // MD).astype(BF)
    hi, mid, lo = split3(coef_ref[...])
    coef = dot(hi, spread) + dot(mid, spread) + dot(lo, spread)
    y = coef[:ROWS] * z_ref[...].astype(F32)
    x = x_ref[...].astype(F32)
    for t in range(STEPS):
        xt = jnp.concatenate([x[t * RD : (t + 1) * RD]] * STEPS, axis=0)
        y = y + coef[(t + 1) * ROWS : (t + 2) * ROWS] * xt
    out_ref[...] = y.astype(BF)


def scan_outputs(coef, x, z):
    wide = 1024
    spec = pl.BlockSpec((ROWS, wide), lambda i: (0, i))
    return pl.pallas_call(
        scan_kernel,
        grid=(MF // wide,),
        in_specs=[pl.BlockSpec(coef.shape, lambda i: (0, 0))] + [spec] * 2,
        out_specs=spec,
        out_shape=jax.ShapeDtypeStruct((ROWS, MF), BF),
        cost_estimate=pl.CostEstimate(flops=6 * 80 * 64 * 4096, bytes_accessed=1_500_000, transcendentals=0),
        name="scan_outputs",
    )(coef, x, z)


def coefficients(mamba_bc, mamba_dt, decay_rate):
    delta = jax.nn.softplus(mamba_dt.astype(F32))
    rate = -decay_rate[None, :] * delta
    decay = jnp.exp(rate)
    b, c = mamba_bc[:, :, :ST], mamba_bc[:, :, ST:]
    bc = jnp.einsum("trn,srn->tsr", b, c, preferred_element_type=F32)
    rows = []
    run = decay[0]
    for s in range(STEPS):
        rows.append(run)
        if s + 1 < STEPS:
            run = run * decay[s + 1]
    zero = jnp.zeros_like(run)
    for t in range(STEPS):
        carry = delta[t]
        for s in range(STEPS):
            if s < t:
                rows.append(zero)
                continue
            if s > t:
                carry = carry * decay[s]
            rows.append(carry * bc[t, s][:, None])
    return jnp.stack(rows).reshape((1 + STEPS) * ROWS, MH)


def on_device(
    kv_store,
    local_kv,
    new_qkv,
    page_owner,
    page_slot,
    prefix_len,
    prefix_states,
    branch_id,
    mamba_x,
    mamba_bc,
    mamba_dt,
    decay_rate,
):
    my_req, my_page = lax.axis_index("req"), lax.axis_index("page")
    q = new_qkv[:, :, 0].reshape(ROWS, FEAT)
    nk = new_qkv[:, :, 1].reshape(ROWS, FEAT)
    nv = new_qkv[:, :, 2].reshape(ROWS, FEAT)

    count = jnp.clip(prefix_len[:, None] - TOK * jnp.arange(page_owner.shape[1], dtype=jnp.int32)[None, :], 0, TOK)
    named = page_owner[:, :, None] == jnp.arange(DEV, dtype=jnp.int32)[None, None, :]
    t_slot = jnp.sum(jnp.where(named, page_slot[:, :, None], 0), axis=1)
    t_count = jnp.sum(jnp.where(named, count[:, :, None], 0), axis=1)
    tables = jnp.stack([t_slot, t_count]).reshape(2, RD, GRP, NPG).transpose(3, 0, 1, 2).reshape(NPG, 1, HD).astype(BF)
    tables = jnp.broadcast_to(jnp.pad(tables, ((0, 0), (0, TOK - 1), (0, 0)))[None], (GRP, NPG, TOK, HD))
    heads = jnp.broadcast_to(q.reshape(ROWS, HEADS, HD).transpose(1, 0, 2)[:, None], (GRP, NPG, ROWS, HD))
    c_own = jnp.broadcast_to(mamba_bc[:, :, ST:].reshape(1, 1, ROWS, ST), (GRP, NPG, ROWS, ST))
    sent = jnp.concatenate([heads, c_own, tables], axis=2).reshape(DEV, QROWS, HD)
    got_q = lax.all_to_all(sent, ("req", "page"), 0, 0, tiled=True)

    store = kv_store.reshape(PAGES, 2, TOK, HEADS, HD).transpose(3, 0, 1, 2, 4)
    store = lax.all_to_all(store, "req", 0, 0, tiled=True).reshape(GRP * PAGES, 2, TOK, HD)

    c_all = lax.dynamic_slice_in_dim(got_q, my_req * NPG, NPG)[:, ROWS : 2 * ROWS].reshape(NPG * ROWS, ST)
    branch = branch_id.reshape(NPG, 1, RD) - 2 * my_page
    branch = jnp.broadcast_to(branch, (NPG, STEPS, RD)).reshape(NPG * ROWS, 1)
    z = state_products(branch, c_all, prefix_states.reshape(2, MF, ST))
    z = lax.psum_scatter(z.reshape(NPG, ROWS, MF), "page", scatter_dimension=0, tiled=True)
    coef = coefficients(mamba_bc, mamba_dt, decay_rate)
    mamba_out = scan_outputs(coef, mamba_x.reshape(ROWS, MF), z.reshape(ROWS, MF))

    o, m, l = local_attention(q, nk, nv, local_kv)

    table = got_q[:, 2 * ROWS].astype(jnp.int32).reshape(DEV, 2, RD, GRP)
    c_slot, c_count = table[:, 0], table[:, 1]
    hit = (c_count > 0).astype(jnp.int32)
    rank = jnp.cumsum(hit, axis=1) - hit
    request = jnp.arange(RD, dtype=jnp.int32)[None, :, None]
    at_slot, at_req, at_count = [], [], []
    for c in range(2):
        here = (hit > 0) & (rank == c)
        at_slot.append(jnp.sum(jnp.where(here, c_slot, 0), axis=1))
        at_count.append(jnp.sum(jnp.where(here, c_count, 0), axis=1))
        at_req.append(jnp.sum(jnp.where(here, request, 0), axis=1))
    owner = jnp.arange(GRP, dtype=jnp.int32)[None, None, :]
    pages = (jnp.stack(at_slot, axis=1) + PAGES * owner).reshape(DEV * JOBS)
    tok = jnp.arange(TOK, dtype=jnp.int32)
    reqs = jnp.where(tok < jnp.stack(at_count, axis=1)[..., None], jnp.stack(at_req, axis=1)[..., None], -1)
    store, o, m, l = lax.optimization_barrier((store, o, m, l))
    part = owner_attention(pages, reqs.reshape(DEV, 1, KEYS), got_q, store)
    got = lax.all_to_all(part, ("req", "page"), 0, 0, tiled=True)
    attn = combine(got, o, m, l)
    return attn.reshape(STEPS, RD, FEAT), mamba_out.reshape(STEPS, RD, MF)


def solution(mesh):
    in_specs = (
        P(("req", "page"), None, None, None),
        P(("req", "page"), None, None, None),
        P(None, ("req", "page"), None, None),
        P(("req", "page"), None),
        P(("req", "page"), None),
        P(("req", "page")),
        P("page", None, None, None),
        P("req"),
        P(None, ("req", "page"), None),
        P(None, ("req", "page"), None),
        P(None, ("req", "page"), None),
        P(),
    )
    out_specs = (P(None, ("req", "page"), None), P(None, ("req", "page"), None))
    return jax.shard_map(
        on_device, mesh=mesh, in_specs=in_specs, out_specs=out_specs, check_vma=False
    )
```

time: 276 us -> 185 us (0.67)
  Pallas kernels: 95.2 us -> 46.9 us
  waiting for transfers between devices: 111 us -> 65.9 us
  starting transfers between devices: 24.8 us -> 35 us
  local copies, waits for them, and re-layouts: 21.3 us -> 17.2 us
    all_to_all x1 -> x3, waiting for transfers between devices: 0.01 us -> 65.9 us  [the longest x1 53 us: on_device(): lax.all_to_all(store, 'req', 0, 0, tiled=True)]
    all_gather x1 -> x0, waiting for transfers between devices: 63.1 us -> none  [on_device(): gathered = lax.all_gather(block[None], ('req', 'page'), axis=0, tiled=True)]
    pallas_call x1, Pallas kernels: 69.7 us -> 16 us  [owner_attention(): pl.pallas_call(owner_kernel, grid_spec=pltpu.PrefetchScalarGridSpec(num_s...]
    ppermute x14 -> x0, waiting for transfers between devices: 47.7 us -> none  [the longest x7 44.6 us: on_device(): lax.ppermute(c_own, 'page', [((i + k) % NPG, i) for i in range(NPG)])]
    all_to_all x1 -> x3, starting transfers between devices: 5.74 us -> 35 us  [the longest x1 16.3 us: on_device(): got = lax.all_to_all(part, ('req', 'page'), 0, 0, tiled=True)]
    ppermute x14 -> x0, starting transfers between devices: 19 us -> none  [the longest x7 11.2 us: on_device(): lax.ppermute(c_own, 'page', [((i + k) % NPG, i) for i in range(NPG)])]
    unnamed x46 -> x18, local copies, waits for them, and re-layouts: 11.9 us -> 1.72 us
    pallas_call x1, Pallas kernels: 4.19 us -> 9.77 us  [combine(): pl.pallas_call(combine_kernel, grid=(HEADS,), in_specs=[pl.BlockSpec((NPG...]
  transfers between devices with their start and end apart: 16 -> 4, of which waited for: 3 -> 3; matrix products, arithmetic and copies ran while one was open for 5% -> 7% of each run, Pallas kernels for 33% -> 20%
where the time goes in v3:
time: 185 us; the launch traced here: 183 us
  waiting for transfers between devices  65.9 us (36%)
  Pallas kernels  46.9 us (25%)
  starting transfers between devices  35 us (19%)
  local copies, waits for them, and re-layouts  17.2 us (9%)
  between operations  14.3 us (8%)
  other arithmetic  4.01 us (2%)
    all_to_all x1, waiting for transfers between devices, on_device(): lax.all_to_all(store, 'req', 0, 0, tiled=True)  53 us
    all_to_all x1, starting transfers between devices, on_device(): got = lax.all_to_all(part, ('req', 'page'), 0, 0, tiled=True)  16.3 us
    pallas_call x1, Pallas kernels, owner_attention(): pl.pallas_call(owner_kernel, grid_spec=pltpu.PrefetchScalarGridSpec(num_s...  16 us
    pallas_call x1, Pallas kernels, local_attention(): pl.pallas_call(local_kernel, grid=(HEADS,), in_specs=[row, row, row, pl.B...  13.6 us
    all_to_all x1, waiting for transfers between devices, on_device(): got = lax.all_to_all(part, ('req', 'page'), 0, 0, tiled=True)  12.7 us
    all_to_all x1, starting transfers between devices, on_device(): got_q = lax.all_to_all(sent, ('req', 'page'), 0, 0, tiled=True)  11.5 us
    pallas_call x1, Pallas kernels, combine(): pl.pallas_call(combine_kernel, grid=(HEADS,), in_specs=[pl.BlockSpec((NPG...  9.77 us
    all_to_all x1, starting transfers between devices, on_device(): lax.all_to_all(store, 'req', 0, 0, tiled=True)  7.2 us
  transfers between devices with their start and end apart: 4, of which 3 were waited for; matrix products, arithmetic and copies ran while one was open for 7% of the time, Pallas kernels for 20%

profile of v3, /device:TPU:1, one launch (start us, length us, event | category | flops | bytes accessed | tf_op | source)
XLA Modules:
  0.0 183.4 jit_solution(11851332698271732353)
XLA Ops:
  7.2 0.7 subtract_clamp_fusion
  7.9 0.8 select_reduce_fusion.1
  9.0 0.7 fusion.9
  9.8 1.0 fusion.8
  11.1 1.3 pad_maximum_fusion
  12.4 11.5 %all-to-all-start = ((bf16[128,40,128]{2,1,0:T(8,128)(2,1)}), bf16[128,40,128]{2,1,0:T(8,128)(2,1)S(1)}, u32[]{:S(2)}, u32[]{:S(2)}) async-start(bf16[128,40,128]{2,1,0:T(8,128)(2,1)} %bitcast.4), calls=%async_computation | async-start | bytes 2621440 | tf_op jit(solution)/shard_map/all_to_all | solution.py:276
  23.9 0.6 reshape_squeeze.9.q_ref
  24.6 0.7 reshape_squeeze.10.nk_ref
  25.3 0.6 reshape_squeeze.11.nv_ref
  26.0 0.7 reshape.269.br_ref
  26.7 13.6 %local_attention.1 = (f32[16,2048]{1,0:T(8,128)}, f32[16,2048]{1,0:T(8,128)}, f32[16,2048]{1,0:T(8,128)}) custom-call(bf16[16,2048]{1,0:T(8,128)(2,1)} %reshape_squeeze.9.q_ref, bf16[16,2048]{1,0:T(8,128)(2,1)} %reshape_squeeze.10.nk_ref, bf16[16,2048]{1,0:T(8,128)(2,1)} %reshape_squeeze.11.nv_ref, bf16[4,2,256,2048]{3,2,1,0:T(8,128)(2,1)} %kv_ref.1), custom_call_target="tpu_custom_call" | custom-call | flops 134217728 | bytes 9000000 | tf_op jit(solution)/shard_map/local_attention/pallas_call | solution.py:81
  40.3 0.1 convolution_bitcast_fusion
  40.4 0.2 slice_reduce_fusion
  40.6 5.2 %copy_bitcast_fusion = bf16[16,64,2,8,128]{4,3,2,1,0:T(8,128)(2,1)} fusion(bf16[64,2,8,2048]{3,2,1,0:T(8,128)(2,1)} %param.12), kind=kLoop, calls=%fused_computation | loop fusion | bytes 8388608 | tf_op jit(solution)/shard_map/transpose | solution.py:278
  45.8 0.2 all-to-all-done.q_ref
  46.0 7.2 %all-to-all-start.1 = ((bf16[16,64,2,8,128]{4,3,2,1,0:T(8,128)(2,1)}), bf16[16,64,2,8,128]{4,3,2,1,0:T(8,128)(2,1)}, u32[]{:S(2)}, u32[]{:S(2)}) async-start(bf16[16,64,2,8,128]{4,3,2,1,0:T(8,128)(2,1)} %copy_bitcast_fusion), calls=%async_computation.1 | async-start | bytes 8388608 | tf_op jit(solution)/shard_map/all_to_all | solution.py:279
  54.0 0.6 constant_dynamic-slice_fusion
  54.6 4.2 %state_products.1 = bf16[128,4096]{1,0:T(8,128)(2,1)} custom-call(s32[128,1]{1,0:T(8,128)} %reshape.269.br_ref, bf16[128,128]{1,0:T(8,128)(2,1)} %bitcast.63, bf16[2,4096,128]{2,1,0:T(8,128)(2,1)} %bitcast.57), custom_call_target="tpu_custom_call" | custom-call | flops 268435456 | bytes 3200000 | tf_op jit(solution)/shard_map/state_products/pallas_call | solution.py:179
  58.9 0.1 copy.61
  59.1 0.2 add.25.page_ref
  59.5 0.2 compare_select_fusion.req_ref
  59.7 53.0 %all-to-all-done.1 = bf16[16,64,2,8,128]{4,3,2,1,0:T(8,128)(2,1)} async-done(((bf16[16,64,2,8,128]{4,3,2,1,0:T(8,128)(2,1)}), bf16[16,64,2,8,128]{4,3,2,1,0:T(8,128)(2,1)}, u32[]{:S(2)}, u32[]{:S(2)}) %all-to-all-start.1) | async-done | bytes 4194336 | tf_op jit(solution)/shard_map/all_to_all | solution.py:279
  112.7 16.0 %owner_attention.1 = bf16[128,16,256]{2,1,0:T(8,128)(2,1)} custom-call(s32[4096]{0:T(1024)S(1)} %add.25.page_ref, s32[128,1,256]{2,1,0:T(1,128)S(1)} %compare_select_fusion.req_ref, bf16[128,40,128]{2,1,0:T(8,128)(2,1)S(1)} %all-to-all-done.q_ref, bf16[1024,2,8,128]{3,2,1,0:T(8,128)(2,1)} %bitcast.18.kv_ref), custom_call_target="tpu_custom_call" | custom-call | flops 268435456 | bytes 8000000 | tf_op jit(solution)/shard_map/owner_attention/pallas_call | solution.py:118
  128.7 16.3 %all-to-all-start.2 = ((bf16[128,16,256]{2,1,0:T(8,128)(2,1)}), bf16[128,16,256]{2,1,0:T(8,128)(2,1)S(1)}, u32[]{:S(2)}, u32[]{:S(2)}) async-start(bf16[128,16,256]{2,1,0:T(8,128)(2,1)} %owner_attention.1), calls=%async_computation.2 | async-start | bytes 2097152 | tf_op jit(solution)/shard_map/all_to_all | solution.py:308
  145.0 0.7 reshape.261.x_ref
  146.0 0.6 copy-done.3
  146.6 3.4 %scan_outputs.1 = bf16[16,4096]{1,0:T(8,128)(2,1)} custom-call(f32[80,64]{1,0:T(8,128)} %bitcast.72, bf16[16,4096]{1,0:T(8,128)(2,1)} %reshape.261.x_ref, bf16[16,4096]{1,0:T(8,128)(2,1)} %bitcast.73), custom_call_target="tpu_custom_call" | custom-call | flops 125829120 | bytes 1500000 | tf_op jit(solution)/shard_map/scan_outputs/pallas_call | solution.py:212
  150.0 1.6 reshape.267
  151.6 12.7 %all-to-all-done.2.got_ref = bf16[128,16,256]{2,1,0:T(8,128)(2,1)S(1)} async-done(((bf16[128,16,256]{2,1,0:T(8,128)(2,1)}), bf16[128,16,256]{2,1,0:T(8,128)(2,1)S(1)}, u32[]{:S(2)}, u32[]{:S(2)}) %all-to-all-start.2) | async-done | bytes 1048608 | tf_op jit(solution)/shard_map/all_to_all | solution.py:308
  164.3 1.0 copy-done
  165.3 9.8 %combine_attention.1 = bf16[16,2048]{1,0:T(8,128)(2,1)} custom-call(bf16[128,16,256]{2,1,0:T(8,128)(2,1)} %copy-done, f32[16,2048]{1,0:T(8,128)} %get-tuple-element.13.o_ref, f32[16,2048]{1,0:T(8,128)} %get-tuple-element.14.m_ref, f32[16,2048]{1,0:T(8,128)} %get-tuple-element.15.l_ref), custom_call_target="tpu_custom_call" | custom-call | flops 134217728 | bytes 2000000 | tf_op jit(solution)/shard_map/combine_attention/pallas_call | solution.py:157
  175.1 1.5 reshape.259
  (63 shorter events, 2.2 us)
Async XLA Ops:
  11.1 14.8 %copy-start.4 = (f32[64]{0:T(128)S(1)}, f32[64]{0:T(128)}, u32[]{:S(2)}) copy-start(f32[64]{0:T(128)} %param.23) | copy-start | bytes 772
  11.1 14.8 %copy-start.5 = (s32[32]{0:T(128)S(1)}, s32[32]{0:T(128)}, u32[]{:S(2)}) copy-start(s32[32]{0:T(128)} %param.19) | copy-start | bytes 388
  12.4 33.7 %all-to-all-start = ((bf16[128,40,128]{2,1,0:T(8,128)(2,1)}), bf16[128,40,128]{2,1,0:T(8,128)(2,1)S(1)}, u32[]{:S(2)}, u32[]{:S(2)}) async-start(bf16[128,40,128]{2,1,0:T(8,128)(2,1)} %bitcast.4), calls=%async_computation | async-start | bytes 2621440 | tf_op jit(solution)/shard_map/all_to_all | solution.py:276
  45.8 7.4 %copy-start.2 = (bf16[4,4,64]{2,1,0:T(4,128)(2,1)S(1)}, bf16[4,4,64]{2,1,0:T(4,128)(2,1)}, u32[]{:S(2)}) copy-start(bf16[4,4,64]{2,1,0:T(4,128)(2,1)} %param.22) | copy-start | bytes 6148
  46.0 66.7 %all-to-all-start.1 = ((bf16[16,64,2,8,128]{4,3,2,1,0:T(8,128)(2,1)}), bf16[16,64,2,8,128]{4,3,2,1,0:T(8,128)(2,1)}, u32[]{:S(2)}, u32[]{:S(2)}) async-start(bf16[16,64,2,8,128]{4,3,2,1,0:T(8,128)(2,1)} %copy_bitcast_fusion), calls=%async_computation.1 | async-start | bytes 8388608 | tf_op jit(solution)/shard_map/all_to_all | solution.py:279
  53.2 92.8 %reduce-scatter.2.cloned.1.call-start = ((), (), s32[]{:S(2)}) async-start(), calls=%async_computation.4 | async-start | bytes 1179648 | tf_op jit(solution)/shard_map/reduce_scatter | solution.py:285
  112.7 32.4 %copy-start.1 = (bf16[4,4,4096]{2,1,0:T(4,128)(2,1)S(1)}, bf16[4,4,4096]{2,1,0:T(4,128)(2,1)}, u32[]{:S(2)}) copy-start(bf16[4,4,4096]{2,1,0:T(4,128)(2,1)} %param.20) | copy-start | bytes 393220
  128.7 35.6 %all-to-all-start.2 = ((bf16[128,16,256]{2,1,0:T(8,128)(2,1)}), bf16[128,16,256]{2,1,0:T(8,128)(2,1)S(1)}, u32[]{:S(2)}, u32[]{:S(2)}) async-start(bf16[128,16,256]{2,1,0:T(8,128)(2,1)} %owner_attention.1), calls=%async_computation.2 | async-start | bytes 2097152 | tf_op jit(solution)/shard_map/all_to_all | solution.py:308
  146.0 0.6 copy-start.3
  164.3 1.0 copy-start
Sparse Core Ops, SparseCore 0:
  58.9 31.3 reduce-scatter.1

commit v4 on v3

v4 whole, which is shorter than its diff:
```python
import functools
import math

import jax
import jax.numpy as jnp
from jax import lax
from jax.experimental import pallas as pl
from jax.experimental.pallas import tpu as pltpu
from jax.sharding import PartitionSpec as P

HEADS = 16
HD = 128
STEPS = 4
RD = 4
ROWS = STEPS * RD
FEAT = HEADS * HD
DEV = 128
TOK = 8
MH = 64
MD = 64
ST = 128
MF = MH * MD
NPG = 8
PAGES = 64
JOBS = 32
KEYS = JOBS * TOK
NEAR = 8
TILES = 19
META = 18
HPC = 4
NEG = -1e30
SCALE = 1.0 / math.sqrt(HD)
BF = jnp.bfloat16
F32 = jnp.float32
NT = (((1,), (1,)), ((), ()))
NN = (((1,), (0,)), ((), ()))


def dot(a, b, dims=NN):
    return lax.dot_general(a, b, dims, preferred_element_type=F32)


def split2(x):
    hi = x.astype(BF)
    return hi, (x - hi.astype(F32)).astype(BF)


def split3(x):
    hi = x.astype(BF)
    rest = x - hi.astype(F32)
    mid = rest.astype(BF)
    return hi, mid, (rest - mid.astype(F32)).astype(BF)


def local_kernel(q_ref, nk_ref, nv_ref, kv_ref, o_ref, m_ref, l_ref):
    q = q_ref[...]
    parts = [dot(q, kv_ref[r, 0], NT) for r in range(RD)]
    row = lax.broadcasted_iota(jnp.int32, (ROWS, 1), 0)
    keep = row % RD
    new = dot(q, nk_ref[...], NT) * SCALE
    col = lax.broadcasted_iota(jnp.int32, (ROWS, ROWS), 1)
    ok = (col % RD == keep) & (col // RD <= row // RD)
    new = jnp.where(ok, new, NEG)
    mine = jnp.where(keep == 0, parts[0], NEG)
    for r in range(1, RD):
        mine = jnp.where(keep == r, parts[r], mine)
    mine = mine * SCALE
    top = jnp.maximum(jnp.max(mine, axis=1, keepdims=True), jnp.max(new, axis=1, keepdims=True))
    p = jnp.exp(mine - top)
    pn = jnp.where(ok, jnp.exp(new - top), 0.0)
    total = jnp.sum(p, axis=1, keepdims=True) + jnp.sum(pn, axis=1, keepdims=True)
    out = dot(pn.astype(BF), nv_ref[...])
    for r in range(RD):
        out = out + dot(jnp.where(keep == r, p, 0.0).astype(BF), kv_ref[r, 1])
    o_ref[...] = out
    m_ref[...] = jnp.broadcast_to(top, (ROWS, HD))
    l_ref[...] = jnp.broadcast_to(total, (ROWS, HD))


def local_attention(q, nk, nv, local_kv):
    row = pl.BlockSpec((ROWS, HD), lambda h: (0, h))
    return pl.pallas_call(
        local_kernel,
        grid=(HEADS,),
        in_specs=[row, row, row, pl.BlockSpec((RD, 2, 256, HD), lambda h: (0, 0, 0, h))],
        out_specs=[row, row, row],
        out_shape=[jax.ShapeDtypeStruct((ROWS, FEAT), F32)] * 3,
        cost_estimate=pl.CostEstimate(flops=2 * 2 * 16 * 1024 * 2048, bytes_accessed=9_000_000, transcendentals=300_000),
        name="local_attention",
    )(q, nk, nv, local_kv)


def pack_kernel(len_ref, own_ref, slot_ref, kv_ref, q_ref, out_ref, lists, qbuf):
    g = pl.program_id(0)

    @pl.when(g == 0)
    def _():
        path = own_ref.shape[1]
        lane = lax.broadcasted_iota(jnp.int32, (8, HD), 1)
        row = lax.broadcasted_iota(jnp.int32, (8, HD), 0)
        owner = jnp.concatenate([own_ref[r : r + 1] for r in range(RD)], axis=1)
        slot = jnp.concatenate([slot_ref[r : r + 1] for r in range(RD)], axis=1)
        req = lane // path
        size = jnp.where(req == 0, len_ref[0], len_ref[1])
        size = jnp.where(req == 2, len_ref[2], jnp.where(req == 3, len_ref[3], size))
        count = jnp.clip(size - TOK * (lane % path), 0, TOK)
        vals = jnp.where(row == 0, owner, jnp.where(row == 1, slot % 8, 0))
        vals = jnp.where(row == 2, req + 1, jnp.where(row == 3, count, vals))
        vals = vals.astype(F32).astype(BF)
        inside = (slot // 8 == row) & (count > 0)
        up = lax.broadcasted_iota(jnp.int32, (HD, HD), 0) < lax.broadcasted_iota(jnp.int32, (HD, HD), 1)
        rank = dot(inside.astype(F32).astype(BF), up.astype(F32).astype(BF))
        rank = jnp.transpose(jnp.where(inside, rank, -1.0))
        place = lax.broadcasted_iota(jnp.int32, (HD, HD), 1).astype(F32)
        for i in range(NPG):
            mine = rank[:, i : i + 1]
            out = dot(vals, (mine == place).astype(F32).astype(BF))
            number = jnp.sum((mine >= 0).astype(F32), axis=0, keepdims=True)
            lists[i] = jnp.where(row == 4, number, out).astype(BF)
        for t in range(STEPS):
            qbuf[t * RD : (t + 1) * RD] = q_ref[t, 0].astype(F32)

    mine = lists[g]
    for m in range(HEADS):
        at = slice(m * HD, (m + 1) * HD)
        out_ref[m, 0, :16] = kv_ref[:, :, :, at].reshape(16, TOK, HD)
        out_ref[m, 0, 16:18] = qbuf[:, at].astype(BF).reshape(2, TOK, HD)
        out_ref[m, 0, 18] = mine


def pack(lens, owner, slot, kv_store, qkv):
    whole = lambda x: pl.BlockSpec(x.shape, lambda g, n: (0,) * len(x.shape))
    return pl.pallas_call(
        pack_kernel,
        grid_spec=pltpu.PrefetchScalarGridSpec(
            num_scalar_prefetch=1,
            grid=(NPG,),
            in_specs=[
                whole(owner),
                whole(slot),
                pl.BlockSpec((PAGES // NPG, 2, TOK, FEAT), lambda g, n: (g, 0, 0, 0)),
                whole(qkv),
            ],
            out_specs=pl.BlockSpec((HEADS, 1, TILES, TOK, HD), lambda g, n: (0, g, 0, 0, 0)),
            scratch_shapes=[pltpu.VMEM((NPG, 8, HD), BF), pltpu.VMEM((ROWS, FEAT), F32)],
        ),
        out_shape=jax.ShapeDtypeStruct((HEADS, NPG, TILES, TOK, HD), BF),
        cost_estimate=pl.CostEstimate(flops=1_000_000, bytes_accessed=10_000_000, transcendentals=0),
        name="pack",
    )(lens, owner, slot, kv_store, qkv)


def owner_kernel(got_ref, o_ref, kbuf, vbuf, acc, tops, sums, index, tile_ref, sem):
    step = pl.program_id(0)

    @pl.when(step == 0)
    def _():
        lists = got_ref[pl.ds(META, DEV, stride=TILES)].astype(F32)
        index[:DEV] = (lists[:, 0] * TILES + 2 * lists[:, 1]).astype(jnp.int32)
        index[DEV:] = jnp.transpose(lists[:, 4])[:TOK].astype(jnp.int32)
        copy = pltpu.make_async_copy(index, tile_ref, sem)
        copy.start()
        copy.wait()

    base = step * NEAR

    def fetch(d, at):
        d_all = base + d
        for j in range(JOBS):
            tile = tile_ref[d_all, at + j]
            kbuf[d, j] = got_ref[tile]
            vbuf[d, j] = got_ref[tile + 1]

    def spread(meta, first):
        key = lax.broadcasted_iota(jnp.int32, (HD, KEYS), 1)
        pos = lax.broadcasted_iota(jnp.int32, (HD, KEYS), 0)
        return dot(meta, (pos == first + key // TOK).astype(F32).astype(BF))

    def scores(d, q):
        return dot(q, kbuf[d].reshape(KEYS, HD), NT)

    def mix(d, p):
        return dot(p, vbuf[d].reshape(KEYS, HD))

    def write(dst, top, total, out):
        lane = lax.broadcasted_iota(jnp.int32, top.shape[:-1] + (HD,), top.ndim - 1)
        stats = jnp.zeros(lane.shape, F32)
        for i, part in enumerate(list(split3(top)) + list(split2(total))):
            stats = jnp.where(lane == i, part.astype(F32), stats)
        o_ref[dst, :, HD:] = stats.astype(BF)
        o_ref[dst, :, :HD] = out.astype(BF)

    for d in range(NEAR):
        fetch(d, 0)
    tok = (lax.broadcasted_iota(jnp.int32, (1, KEYS), 1) % TOK).astype(F32)
    want = (lax.broadcasted_iota(jnp.int32, (ROWS, 1), 0) % RD + 1).astype(F32)
    queries = [got_ref[pl.ds((base + d) * TILES + 16, 2)].reshape(ROWS, HD) for d in range(NEAR)]
    meta = jnp.concatenate([got_ref[(base + d) * TILES + META] for d in range(NEAR)], axis=0)
    wide = spread(meta, 0).reshape(NEAR, 8, KEYS)
    ok = (wide[:, 2:3] == want[None]) & (tok[None] < wide[:, 3:4])
    s = jnp.concatenate([scores(d, queries[d])[None] for d in range(NEAR)], axis=0)
    s = jnp.where(ok, s * SCALE, NEG)
    top = jnp.max(s, axis=2, keepdims=True)
    p = jnp.where(ok, jnp.exp(s - top), 0.0)
    total = jnp.sum(p, axis=2, keepdims=True)
    p = p.astype(BF)
    out = jnp.concatenate([mix(d, p[d])[None] for d in range(NEAR)], axis=0)
    write(slice(None), top, total, out)
    most = tile_ref[DEV, base]
    for d in range(1, NEAR):
        most = jnp.maximum(most, tile_ref[DEV, base + d])

    @pl.when(most > JOBS)
    def _():
        acc[...] = out
        tops[...] = jnp.broadcast_to(top, tops.shape)
        sums[...] = jnp.broadcast_to(total, sums.shape)
        for d in range(NEAR):
            num = tile_ref[DEV, base + d]

            @pl.loop(1, (num + JOBS - 1) // JOBS)
            def _(c):
                fetch(d, c * JOBS)
                wide = spread(got_ref[(base + d) * TILES + META], c * JOBS)
                ok = (wide[2:3] == want) & (tok < wide[3:4])
                s = jnp.where(ok, scores(d, got_ref[pl.ds((base + d) * TILES + 16, 2)].reshape(ROWS, HD)) * SCALE, NEG)
                best = jnp.maximum(tops[d], jnp.max(s, axis=1, keepdims=True))
                p = jnp.where(ok, jnp.exp(s - best[:, :1]), 0.0)
                old = jnp.exp(tops[d] - best)
                acc[d] = old * acc[d] + mix(d, p.astype(BF))
                sums[d] = old * sums[d] + jnp.sum(p, axis=1, keepdims=True)
                tops[d] = best

            @pl.when(num > JOBS)
            def _():
                write(d, tops[d], sums[d], acc[d])


def owner_attention(got):
    return pl.pallas_call(
        owner_kernel,
        grid=(DEV // NEAR,),
        in_specs=[pl.BlockSpec(got.shape, lambda i: (0, 0, 0), pipeline_mode=pl.Buffered(1))],
        out_specs=pl.BlockSpec((NEAR, ROWS, 2 * HD), lambda i: (i, 0, 0)),
        scratch_shapes=[
            pltpu.VMEM((NEAR, JOBS, TOK, HD), BF),
            pltpu.VMEM((NEAR, JOBS, TOK, HD), BF),
            pltpu.VMEM((NEAR, ROWS, HD), F32),
            pltpu.VMEM((NEAR, ROWS, HD), F32),
            pltpu.VMEM((NEAR, ROWS, HD), F32),
            pltpu.VMEM((DEV + TOK, HD), jnp.int32),
            pltpu.SMEM((DEV + TOK, HD), jnp.int32),
            pltpu.SemaphoreType.DMA,
        ],
        out_shape=jax.ShapeDtypeStruct((DEV, ROWS, 2 * HD), BF),
        cost_estimate=pl.CostEstimate(flops=4 * 2048 * 256 * 128, bytes_accessed=8_000_000, transcendentals=600_000),
        compiler_params=pltpu.CompilerParams(vmem_limit_bytes=32 * 1024 * 1024),
        name="owner_attention",
    )(got)


def combine_kernel(got_ref, o_ref, m_ref, l_ref, out_ref):
    lane = lax.broadcasted_iota(jnp.int32, (HD, HD), 0)
    top_of = (lane < 3).astype(F32).astype(BF)
    sum_of = ((lane >= 3) & (lane < 5)).astype(F32).astype(BF)
    stats = got_ref[:, :, HD:].reshape(HPC * NPG * ROWS, HD)
    tops = dot(stats, top_of).reshape(HPC, NPG, ROWS, HD)
    sums = dot(stats, sum_of).reshape(HPC, NPG, ROWS, HD)
    for h in range(HPC):
        at = slice(h * HD, (h + 1) * HD)
        got = got_ref[h * NPG : (h + 1) * NPG, :, :HD].astype(F32)
        lm = m_ref[:, at]
        best = jnp.maximum(jnp.max(tops[h], axis=0), lm)
        w = jnp.exp(tops[h] - best[None])
        mine = jnp.exp(lm - best)
        mixed = jnp.sum(w * got, axis=0) + mine * o_ref[:, at]
        mixed = (mixed / (jnp.sum(w * sums[h], axis=0) + mine * l_ref[:, at])).astype(BF)
        for t in range(STEPS):
            out_ref[t, :, at] = mixed[t * RD : (t + 1) * RD]


def combine(got, o, m, l):
    row = pl.BlockSpec((ROWS, HPC * HD), lambda h: (0, h))
    return pl.pallas_call(
        combine_kernel,
        grid=(HEADS // HPC,),
        in_specs=[pl.BlockSpec((HPC * NPG, ROWS, 2 * HD), lambda h: (h, 0, 0)), row, row, row],
        out_specs=pl.BlockSpec((STEPS, RD, HPC * HD), lambda h: (0, 0, h)),
        out_shape=jax.ShapeDtypeStruct((STEPS, RD, FEAT), BF),
        cost_estimate=pl.CostEstimate(flops=4 * 16 * 1024 * 2048, bytes_accessed=2_000_000, transcendentals=300_000),
        name="combine_attention",
    )(got, o, m, l)


def state_kernel(br_ref, c_ref, st_ref, out_ref):
    c = c_ref[...]
    first = dot(c, st_ref[0], NT)
    second = dot(c, st_ref[1], NT)
    which = br_ref[...]
    z = jnp.where(which == 0, first, 0.0) + jnp.where(which == 1, second, 0.0)
    out_ref[...] = z.astype(BF)


def state_products(which, c_all, states):
    wide = 1024
    return pl.pallas_call(
        state_kernel,
        grid=(MF // wide,),
        in_specs=[
            pl.BlockSpec((NPG * ROWS, 1), lambda i: (0, 0)),
            pl.BlockSpec((NPG * ROWS, ST), lambda i: (0, 0)),
            pl.BlockSpec((2, wide, ST), lambda i: (0, i, 0)),
        ],
        out_specs=pl.BlockSpec((NPG * ROWS, wide), lambda i: (0, i)),
        out_shape=jax.ShapeDtypeStruct((NPG * ROWS, MF), BF),
        cost_estimate=pl.CostEstimate(flops=4 * 128 * 128 * 4096, bytes_accessed=3_200_000, transcendentals=0),
        name="state_products",
    )(which, c_all, states)


def scan_kernel(coef_ref, x_ref, z_ref, out_ref):
    wide = out_ref.shape[2]
    head = lax.broadcasted_iota(jnp.int32, (MH, wide), 0)
    chan = lax.broadcasted_iota(jnp.int32, (MH, wide), 1) + pl.program_id(0) * wide
    spread = (head == chan // MD).astype(BF)
    hi, mid, lo = split3(coef_ref[...])
    coef = dot(hi, spread) + dot(mid, spread) + dot(lo, spread)
    y = coef[:ROWS] * z_ref[...].astype(F32)
    x = x_ref[...].astype(F32)
    for t in range(STEPS):
        xt = jnp.concatenate([x[t * RD : (t + 1) * RD]] * STEPS, axis=0)
        y = y + coef[(t + 1) * ROWS : (t + 2) * ROWS] * xt
    y = y.astype(BF)
    for t in range(STEPS):
        out_ref[t] = y[t * RD : (t + 1) * RD]


def scan_outputs(coef, x, z):
    wide = 1024
    spec = pl.BlockSpec((ROWS, wide), lambda i: (0, i))
    return pl.pallas_call(
        scan_kernel,
        grid=(MF // wide,),
        in_specs=[pl.BlockSpec(coef.shape, lambda i: (0, 0))] + [spec] * 2,
        out_specs=pl.BlockSpec((STEPS, RD, wide), lambda i: (0, 0, i)),
        out_shape=jax.ShapeDtypeStruct((STEPS, RD, MF), BF),
        cost_estimate=pl.CostEstimate(flops=6 * 80 * 64 * 4096, bytes_accessed=1_500_000, transcendentals=0),
        name="scan_outputs",
    )(coef, x, z)


def coefficients(mamba_bc, mamba_dt, decay_rate):
    delta = jax.nn.softplus(mamba_dt.astype(F32))
    rate = -decay_rate[None, :] * delta
    decay = jnp.exp(rate)
    b, c = mamba_bc[:, :, :ST], mamba_bc[:, :, ST:]
    bc = jnp.einsum("trn,srn->tsr", b, c, preferred_element_type=F32)
    rows = []
    run = decay[0]
    for s in range(STEPS):
        rows.append(run)
        if s + 1 < STEPS:
            run = run * decay[s + 1]
    zero = jnp.zeros_like(run)
    for t in range(STEPS):
        carry = delta[t]
        for s in range(STEPS):
            if s < t:
                rows.append(zero)
                continue
            if s > t:
                carry = carry * decay[s]
            rows.append(carry * bc[t, s][:, None])
    return jnp.stack(rows).reshape((1 + STEPS) * ROWS, MH)


def on_device(
    kv_store,
    local_kv,
    new_qkv,
    page_owner,
    page_slot,
    prefix_len,
    prefix_states,
    branch_id,
    mamba_x,
    mamba_bc,
    mamba_dt,
    decay_rate,
):
    my_page = lax.axis_index("page")
    q = new_qkv[:, :, 0].reshape(ROWS, FEAT)
    nk = new_qkv[:, :, 1].reshape(ROWS, FEAT)
    nv = new_qkv[:, :, 2].reshape(ROWS, FEAT)

    x_own = mamba_x.reshape(ROWS, MF)
    c_own = jnp.concatenate([mamba_bc[:, :, ST:].reshape(ROWS, ST), x_own], axis=1)
    c_all = lax.all_gather(c_own, "page", axis=0, tiled=True)
    branch = branch_id.reshape(NPG, 1, RD) - 2 * my_page
    branch = jnp.broadcast_to(branch, (NPG, STEPS, RD)).reshape(NPG * ROWS, 1)
    z = state_products(branch, c_all, prefix_states.reshape(2, MF, ST))
    z = lax.psum_scatter(z.reshape(NPG, ROWS, MF), "page", scatter_dimension=0, tiled=True)

    sent = pack(prefix_len, page_owner, page_slot, kv_store, new_qkv.transpose(0, 2, 1, 3))
    got_q = lax.all_to_all(sent.reshape(DEV, TILES, TOK, HD), ("req", "page"), 0, 0, tiled=True)

    coef = coefficients(mamba_bc, mamba_dt, decay_rate)
    mamba_out = scan_outputs(coef, x_own, z.reshape(ROWS, MF))

    o, m, l = local_attention(q, nk, nv, local_kv)

    got_q, o, m, l = lax.optimization_barrier((got_q, o, m, l))
    part = owner_attention(got_q.reshape(DEV * TILES, TOK, HD))
    got = lax.all_to_all(part, ("req", "page"), 0, 0, tiled=True)
    attn = combine(got, o, m, l)
    return attn, mamba_out


def solution(mesh):
    in_specs = (
        P(("req", "page"), None, None, None),
        P(("req", "page"), None, None, None),
        P(None, ("req", "page"), None, None),
        P(("req", "page"), None),
        P(("req", "page"), None),
        P(("req", "page")),
        P("page", None, None, None),
        P("req"),
        P(None, ("req", "page"), None),
        P(None, ("req", "page"), None),
        P(None, ("req", "page"), None),
        P(),
    )
    out_specs = (P(None, ("req", "page"), None), P(None, ("req", "page"), None))
    return jax.shard_map(
        on_device, mesh=mesh, in_specs=in_specs, out_specs=out_specs, check_vma=False
    )
```

time: 185 us -> 151 us (0.82)
  starting transfers between devices: 35 us -> 16.7 us
  local copies, waits for them, and re-layouts: 17.2 us -> 4.73 us
  waiting for transfers between devices: 65.9 us -> 61.2 us
  Pallas kernels: 46.9 us -> 51.5 us
  other arithmetic: 4.01 us -> 1.51 us
    all_to_all x2 -> x1, waiting for transfers between devices: 53.2 us -> 15.6 us  [on_device(): lax.all_to_all(sent.reshape(DEV, TILES, TOK, HD), ('req', 'page'), 0, 0,...]
    all_gather x0 -> x1, waiting for transfers between devices: none -> 30.5 us  [on_device(): c_all = lax.all_gather(c_own, 'page', axis=0, tiled=True)]
    all_to_all x1, starting transfers between devices: 16.3 us -> 4.73 us  [on_device(): got = lax.all_to_all(part, ('req', 'page'), 0, 0, tiled=True)]
    all_to_all x2 -> x1, starting transfers between devices: 18.7 us -> 11.9 us  [on_device(): lax.all_to_all(sent.reshape(DEV, TILES, TOK, HD), ('req', 'page'), 0, 0,...]
    transpose x2 -> x0, local copies, waits for them, and re-layouts: 5.26 us -> none  [the longest x1 5.25 us: on_device(): store = kv_store.reshape(PAGES, 2, TOK, HEADS, HD).transpose(3, 0, 1, 2, 4)]
    pallas_call x2 -> x3, Pallas kernels: 25.8 us -> 30.3 us  [the longest x1 18.1 us: owner_attention(): pl.pallas_call(owner_kernel, grid=(DEV // NEAR,), in_specs=[pl.BlockSpec(...]
    reshape x3 -> x1, local copies, waits for them, and re-layouts: 3.8 us -> 0.04 us  [on_device(): x_own = mamba_x.reshape(ROWS, MF)]
    all_to_all x1, waiting for transfers between devices: 12.7 us -> 15.1 us  [on_device(): got = lax.all_to_all(part, ('req', 'page'), 0, 0, tiled=True)]
  transfers between devices with their start and end apart: 4 -> 4, of which waited for: 3 -> 3; matrix products, arithmetic and copies ran while one was open for 7% -> 3% of each run, Pallas kernels for 20% -> 26%
where the time goes in v4:
time: 151 us; the launch traced here: 150 us
  waiting for transfers between devices  61.2 us (41%)
  Pallas kernels  51.5 us (34%)
  starting transfers between devices  16.7 us (11%)
  between operations  14.2 us (9%)
  local copies, waits for them, and re-layouts  4.73 us (3%)
  other arithmetic  1.51 us (1%)
    all_gather x1, waiting for transfers between devices, on_device(): c_all = lax.all_gather(c_own, 'page', axis=0, tiled=True)  30.5 us
    pallas_call x1, Pallas kernels, owner_attention(): pl.pallas_call(owner_kernel, grid=(DEV // NEAR,), in_specs=[pl.BlockSpec(...  18.1 us
    all_to_all x1, waiting for transfers between devices, on_device(): lax.all_to_all(sent.reshape(DEV, TILES, TOK, HD), ('req', 'page'), 0, 0,...  15.6 us
    all_to_all x1, waiting for transfers between devices, on_device(): got = lax.all_to_all(part, ('req', 'page'), 0, 0, tiled=True)  15.1 us
    pallas_call x1, Pallas kernels, local_attention(): pl.pallas_call(local_kernel, grid=(HEADS,), in_specs=[row, row, row, pl.B...  13.6 us
    all_to_all x1, starting transfers between devices, on_device(): lax.all_to_all(sent.reshape(DEV, TILES, TOK, HD), ('req', 'page'), 0, 0,...  11.9 us
    pallas_call x1, Pallas kernels, pack(): pl.pallas_call(pack_kernel, grid_spec=pltpu.PrefetchScalarGridSpec(num_sc...  8.49 us
    all_to_all x1, starting transfers between devices, on_device(): got = lax.all_to_all(part, ('req', 'page'), 0, 0, tiled=True)  4.73 us
  transfers between devices with their start and end apart: 4, of which 3 were waited for; matrix products, arithmetic and copies ran while one was open for 3% of the time, Pallas kernels for 26%

profile of v4, /device:TPU:1, one launch (start us, length us, event | category | flops | bytes accessed | tf_op | source)
XLA Modules:
  0.0 150.0 jit_solution(521940918710118680)
XLA Ops:
  7.2 8.5 %pack.1 = bf16[16,8,19,8,128]{4,3,2,1,0:T(8,128)(2,1)} custom-call(s32[4]{0:T(128)} %len_ref.1, s32[4,32]{1,0:T(4,128)} %own_ref.1, s32[4,32]{1,0:T(4,128)} %slot_ref.1, bf16[64,2,8,2048]{3,2,1,0:T(8,128)(2,1)} %kv_ref.2, bf16[4,3,4,2048]{3,2,1,0:T(4,128)(2,1)} %bitcast.19), custom_call_target="tpu_custom_call" | custom-call | flops 1000000 | bytes 10000000 | tf_op jit(solution)/shard_map/pack/pallas_call | solution.py:133
  15.7 11.9 %all-to-all-start = ((bf16[128,19,8,128]{3,2,1,0:T(8,128)(2,1)}), bf16[128,19,8,128]{3,2,1,0:T(8,128)(2,1)}, u32[]{:S(2)}, u32[]{:S(2)}) async-start(bf16[128,19,8,128]{3,2,1,0:T(8,128)(2,1)} %bitcast.16), calls=%async_computation | async-start | bytes 9961472 | tf_op jit(solution)/shard_map/all_to_all | solution.py:405
  27.7 0.7 pad_maximum_fusion
  28.5 0.1 sub.16
  28.6 0.7 reshape.133.br_ref
  29.4 0.1 convolution_bitcast_fusion
  29.5 0.2 slice_reduce_fusion
  29.8 0.1 constant_dynamic-update-slice_fusion.13
  29.8 0.1 constant_dynamic-update-slice_fusion.12
  29.9 0.1 fusion.6
  30.0 30.5 %all-gather.2.cloned.1.call-done.c_ref = bf16[128,4224]{1,0:T(8,128)(2,1)} async-done(((bf16[16,4224]{1,0:T(8,128)(2,1)}), bf16[128,4224]{1,0:T(8,128)(2,1)}) %all-gather.2.cloned.1.call-update) | async-done | bytes 1081360 | tf_op jit(solution)/shard_map/all_gather | solution.py:398
  60.5 4.2 %state_products.1 = bf16[128,4096]{1,0:T(8,128)(2,1)} custom-call(s32[128,1]{1,0:T(8,128)} %reshape.133.br_ref, bf16[128,4224]{1,0:T(8,128)(2,1)} %all-gather.2.cloned.1.call-done.c_ref, bf16[2,4096,128]{2,1,0:T(8,128)(2,1)} %bitcast.18), custom_call_target="tpu_custom_call" | custom-call | flops 268435456 | bytes 3200000 | tf_op jit(solution)/shard_map/state_products/pallas_call | solution.py:306
  64.8 0.1 constant_dynamic-update-slice_fusion.11
  64.8 0.6 reshape_squeeze.9.q_ref
  65.5 0.6 reshape_squeeze.10.nk_ref
  66.1 0.6 reshape_squeeze.11.nv_ref
  66.8 13.6 %local_attention.1 = (f32[16,2048]{1,0:T(8,128)}, f32[16,2048]{1,0:T(8,128)}, f32[16,2048]{1,0:T(8,128)}) custom-call(bf16[16,2048]{1,0:T(8,128)(2,1)} %reshape_squeeze.9.q_ref, bf16[16,2048]{1,0:T(8,128)(2,1)} %reshape_squeeze.10.nk_ref, bf16[16,2048]{1,0:T(8,128)(2,1)} %reshape_squeeze.11.nv_ref, bf16[4,2,256,2048]{3,2,1,0:T(8,128)(2,1)} %kv_ref.3), custom_call_target="tpu_custom_call" | custom-call | flops 134217728 | bytes 9000000 | tf_op jit(solution)/shard_map/local_attention/pallas_call | solution.py:82
  80.4 0.1 constant_dynamic-update-slice_fusion.10
  80.5 0.1 constant_dynamic-update-slice_fusion.8
  80.6 0.1 constant_dynamic-update-slice_fusion.7
  80.6 15.6 %all-to-all-done = bf16[128,19,8,128]{3,2,1,0:T(8,128)(2,1)} async-done(((bf16[128,19,8,128]{3,2,1,0:T(8,128)(2,1)}), bf16[128,19,8,128]{3,2,1,0:T(8,128)(2,1)}, u32[]{:S(2)}, u32[]{:S(2)}) %all-to-all-start) | async-done | bytes 4980768 | tf_op jit(solution)/shard_map/all_to_all | solution.py:405
  96.2 18.1 %owner_attention.1 = bf16[128,16,256]{2,1,0:T(8,128)(2,1)} custom-call(bf16[2432,8,128]{2,1,0:T(8,128)(2,1)} %bitcast.2.got_ref), custom_call_target="tpu_custom_call" | custom-call | flops 268435456 | bytes 8000000 | tf_op jit(solution)/shard_map/owner_attention/pallas_call | solution.py:240
  114.3 4.7 %all-to-all-start.1 = ((bf16[128,16,256]{2,1,0:T(8,128)(2,1)}), bf16[128,16,256]{2,1,0:T(8,128)(2,1)S(1)}, u32[]{:S(2)}, u32[]{:S(2)}) async-start(bf16[128,16,256]{2,1,0:T(8,128)(2,1)} %owner_attention.1), calls=%async_computation.1 | async-start | bytes 2097152 | tf_op jit(solution)/shard_map/all_to_all | solution.py:414
  119.0 0.1 constant_dynamic-update-slice_fusion.6
  119.1 0.1 constant_dynamic-update-slice_fusion.4
  119.2 0.1 constant_dynamic-update-slice_fusion.3
  119.3 0.1 constant_dynamic-update-slice_fusion
  119.4 0.6 copy-done.6
  120.0 3.4 %scan_outputs.1 = bf16[4,4,4096]{2,1,0:T(4,128)(2,1)} custom-call(f32[80,64]{1,0:T(8,128)} %bitcast.21, bf16[16,4096]{1,0:T(8,128)(2,1)} %copy-done.2, bf16[16,4096]{1,0:T(8,128)(2,1)} %bitcast.22), custom_call_target="tpu_custom_call" | custom-call | flops 125829120 | bytes 1500000 | tf_op jit(solution)/shard_map/scan_outputs/pallas_call | solution.py:341
  123.4 15.1 %all-to-all-done.1.got_ref = bf16[128,16,256]{2,1,0:T(8,128)(2,1)S(1)} async-done(((bf16[128,16,256]{2,1,0:T(8,128)(2,1)}), bf16[128,16,256]{2,1,0:T(8,128)(2,1)S(1)}, u32[]{:S(2)}, u32[]{:S(2)}) %all-to-all-start.1) | async-done | bytes 1048608 | tf_op jit(solution)/shard_map/all_to_all | solution.py:414
  138.5 1.0 copy-done
  139.5 3.7 %combine_attention.1 = bf16[4,4,2048]{2,1,0:T(4,128)(2,1)} custom-call(bf16[128,16,256]{2,1,0:T(8,128)(2,1)} %copy-done, f32[16,2048]{1,0:T(8,128)} %get-tuple-element.13.o_ref, f32[16,2048]{1,0:T(8,128)} %get-tuple-element.14.m_ref, f32[16,2048]{1,0:T(8,128)} %get-tuple-element.15.l_ref), custom_call_target="tpu_custom_call" | custom-call | flops 134217728 | bytes 2000000 | tf_op jit(solution)/shard_map/combine_attention/pallas_call | solution.py:284
  (35 shorter events, 0.3 us)
Async XLA Ops:
  15.7 12.0 %copy-start.3 = (bf16[4,4,4096]{2,1,0:T(4,128)(2,1)S(1)}, bf16[4,4,4096]{2,1,0:T(4,128)(2,1)}, u32[]{:S(2)}) copy-start(bf16[4,4,4096]{2,1,0:T(4,128)(2,1)} %param.20) | copy-start | bytes 393220
  15.7 12.1 %copy-start.4 = (bf16[4,4,256]{2,1,0:T(4,128)(2,1)S(1)}, bf16[4,4,256]{2,1,0:T(4,128)(2,1)}, u32[]{:S(2)}) copy-start(bf16[4,4,256]{2,1,0:T(4,128)(2,1)} %param.21) | copy-start | bytes 24580
  15.7 12.8 %copy-start.7 = (f32[64]{0:T(128)S(1)}, f32[64]{0:T(128)}, u32[]{:S(2)}) copy-start(f32[64]{0:T(128)} %param.23) | copy-start | bytes 772
  15.7 12.9 %copy-start.8 = (s32[32]{0:T(128)S(1)}, s32[32]{0:T(128)}, u32[]{:S(2)}) copy-start(s32[32]{0:T(128)} %param.19) | copy-start | bytes 388
  15.7 13.8 %copy-start.5 = (bf16[4,4,64]{2,1,0:T(4,128)(2,1)S(1)}, bf16[4,4,64]{2,1,0:T(4,128)(2,1)}, u32[]{:S(2)}) copy-start(bf16[4,4,64]{2,1,0:T(4,128)(2,1)} %param.22) | copy-start | bytes 6148
  15.7 14.2 %copy-start.1 = (bf16[4,4,3,2048]{3,1,2,0:T(4,128)(2,1)S(1)}, bf16[4,4,3,2048]{3,1,2,0:T(4,128)(2,1)}, u32[]{:S(2)}) copy-start(bf16[4,4,3,2048]{3,1,2,0:T(4,128)(2,1)} %param.14) | copy-start | bytes 589828
  15.7 80.5 %all-to-all-start = ((bf16[128,19,8,128]{3,2,1,0:T(8,128)(2,1)}), bf16[128,19,8,128]{3,2,1,0:T(8,128)(2,1)}, u32[]{:S(2)}, u32[]{:S(2)}) async-start(bf16[128,19,8,128]{3,2,1,0:T(8,128)(2,1)} %bitcast.16), calls=%async_computation | async-start | bytes 9961472 | tf_op jit(solution)/shard_map/all_to_all | solution.py:405
  27.6 32.9 %all-gather.2.cloned.1.call-start = ((), (), s32[]{:S(2)}) async-start(), calls=%async_computation.3 | async-start | bytes 1216512 | tf_op jit(solution)/shard_map/all_gather | solution.py:398
  27.7 52.7 %copy-start.2 = (bf16[16,4096]{1,0:T(8,128)(2,1)}, bf16[16,4096]{1,0:T(8,128)(2,1)S(1)}, u32[]{:S(2)}) copy-start(bf16[16,4096]{1,0:T(8,128)(2,1)S(1)} %reshape.127.x_ref) | copy-start | bytes 393220
  28.4 90.9 %reduce-scatter.2.cloned.1.call-start = ((), (), s32[]{:S(2)}) async-start(), calls=%async_computation.4 | async-start | bytes 1179648 | tf_op jit(solution)/shard_map/reduce_scatter | solution.py:402
  114.3 24.2 %all-to-all-start.1 = ((bf16[128,16,256]{2,1,0:T(8,128)(2,1)}), bf16[128,16,256]{2,1,0:T(8,128)(2,1)S(1)}, u32[]{:S(2)}, u32[]{:S(2)}) async-start(bf16[128,16,256]{2,1,0:T(8,128)(2,1)} %owner_attention.1), calls=%async_computation.1 | async-start | bytes 2097152 | tf_op jit(solution)/shard_map/all_to_all | solution.py:414
  119.4 0.6 copy-start.6
  138.5 1.0 copy-start
Sparse Core Ops, SparseCore 0:
  30.1 30.3 all-gather.1
  64.9 33.1 reduce-scatter.1

commit v5 on v4

--- a/solution.py
+++ b/solution.py
@@ -24,11 +24,11 @@
 PAGES = 64
 JOBS = 32
 KEYS = JOBS * TOK
-NEAR = 8
+NEAR = 16
 TILES = 19
 META = 18
-HPC = 4
 NEG = -1e30
+VMEM_LIMIT = 20 * 1024 * 1024
 SCALE = 1.0 / math.sqrt(HD)
 BF = jnp.bfloat16
 F32 = jnp.float32
@@ -86,68 +86,72 @@
         out_specs=[row, row, row],
         out_shape=[jax.ShapeDtypeStruct((ROWS, FEAT), F32)] * 3,
         cost_estimate=pl.CostEstimate(flops=2 * 2 * 16 * 1024 * 2048, bytes_accessed=9_000_000, transcendentals=300_000),
+        compiler_params=pltpu.CompilerParams(vmem_limit_bytes=VMEM_LIMIT),
         name="local_attention",
     )(q, nk, nv, local_kv)
 
 
-def pack_kernel(len_ref, own_ref, slot_ref, kv_ref, q_ref, out_ref, lists, qbuf):
-    g = pl.program_id(0)
-
-    @pl.when(g == 0)
-    def _():
-        path = own_ref.shape[1]
-        lane = lax.broadcasted_iota(jnp.int32, (8, HD), 1)
-        row = lax.broadcasted_iota(jnp.int32, (8, HD), 0)
-        owner = jnp.concatenate([own_ref[r : r + 1] for r in range(RD)], axis=1)
-        slot = jnp.concatenate([slot_ref[r : r + 1] for r in range(RD)], axis=1)
-        req = lane // path
-        size = jnp.where(req == 0, len_ref[0], len_ref[1])
-        size = jnp.where(req == 2, len_ref[2], jnp.where(req == 3, len_ref[3], size))
-        count = jnp.clip(size - TOK * (lane % path), 0, TOK)
-        vals = jnp.where(row == 0, owner, jnp.where(row == 1, slot % 8, 0))
-        vals = jnp.where(row == 2, req + 1, jnp.where(row == 3, count, vals))
-        vals = vals.astype(F32).astype(BF)
-        inside = (slot // 8 == row) & (count > 0)
-        up = lax.broadcasted_iota(jnp.int32, (HD, HD), 0) < lax.broadcasted_iota(jnp.int32, (HD, HD), 1)
-        rank = dot(inside.astype(F32).astype(BF), up.astype(F32).astype(BF))
-        rank = jnp.transpose(jnp.where(inside, rank, -1.0))
-        place = lax.broadcasted_iota(jnp.int32, (HD, HD), 1).astype(F32)
-        for i in range(NPG):
-            mine = rank[:, i : i + 1]
-            out = dot(vals, (mine == place).astype(F32).astype(BF))
-            number = jnp.sum((mine >= 0).astype(F32), axis=0, keepdims=True)
-            lists[i] = jnp.where(row == 4, number, out).astype(BF)
-        for t in range(STEPS):
-            qbuf[t * RD : (t + 1) * RD] = q_ref[t, 0].astype(F32)
-
-    mine = lists[g]
+def pack_kernel(len_ref, own_ref, slot_ref, kv_ref, q_ref, out_ref, buf, lists, qbuf, sem):
+    copies = []
+    for m in range(HEADS):
+        src = kv_ref.at[:, :, :, pl.ds(m * HD, HD)]
+        copies.append(pltpu.make_async_copy(src, buf.at[m, :, pl.ds(0, 16)], sem.at[0, m]))
+        copies[-1].start()
+    path = own_ref.shape[1]
+    lane = lax.broadcasted_iota(jnp.int32, (8, HD), 1)
+    row = lax.broadcasted_iota(jnp.int32, (8, HD), 0)
+    owner = jnp.concatenate([own_ref[r : r + 1] for r in range(RD)], axis=1)
+    slot = jnp.concatenate([slot_ref[r : r + 1] for r in range(RD)], axis=1)
+    req = lane // path
+    size = jnp.where(req == 0, len_ref[0], len_ref[1])
+    size = jnp.where(req == 2, len_ref[2], jnp.where(req == 3, len_ref[3], size))
+    count = jnp.clip(size - TOK * (lane % path), 0, TOK)
+    vals = jnp.where(row == 0, owner, jnp.where(row == 1, slot % 8, 0))
+    vals = jnp.where(row == 2, req + 1, jnp.where(row == 3, count, vals))
+    vals = vals.astype(F32).astype(BF)
+    inside = (slot // 8 == row) & (count > 0)
+    up = lax.broadcasted_iota(jnp.int32, (HD, HD), 0) < lax.broadcasted_iota(jnp.int32, (HD, HD), 1)
+    rank = dot(inside.astype(F32).astype(BF), up.astype(F32).astype(BF))
+    rank = jnp.transpose(jnp.where(inside, rank, -1.0))
+    place = lax.broadcasted_iota(jnp.int32, (HD, HD), 1).astype(F32)
+    for i in range(NPG):
+        mine = rank[:, i : i + 1]
+        out = dot(vals, (mine == place).astype(F32).astype(BF))
+        number = jnp.sum((mine >= 0).astype(F32), axis=0, keepdims=True)
+        lists[i] = jnp.where(row == 4, number, out).astype(BF)
+    for t in range(STEPS):
+        qbuf[t * RD : (t + 1) * RD] = q_ref[t, 0].astype(F32)
+
     for m in range(HEADS):
         at = slice(m * HD, (m + 1) * HD)
-        out_ref[m, 0, :16] = kv_ref[:, :, :, at].reshape(16, TOK, HD)
-        out_ref[m, 0, 16:18] = qbuf[:, at].astype(BF).reshape(2, TOK, HD)
-        out_ref[m, 0, 18] = mine
+        q = qbuf[:, at].astype(BF).reshape(1, 2, TOK, HD)
+        buf[m, :, 16:18] = jnp.broadcast_to(q, (NPG, 2, TOK, HD))
+        buf[m, :, META] = lists[...]
+    back = []
+    for m in range(HEADS):
+        copies[m].wait()
+        back.append(pltpu.make_async_copy(buf.at[m], out_ref.at[m], sem.at[1, m]))
+        back[-1].start()
+    for copy in back:
+        copy.wait()
 
 
 def pack(lens, owner, slot, kv_store, qkv):
-    whole = lambda x: pl.BlockSpec(x.shape, lambda g, n: (0,) * len(x.shape))
+    vmem = pl.BlockSpec(memory_space=pltpu.VMEM)
     return pl.pallas_call(
         pack_kernel,
-        grid_spec=pltpu.PrefetchScalarGridSpec(
-            num_scalar_prefetch=1,
-            grid=(NPG,),
-            in_specs=[
-                whole(owner),
-                whole(slot),
-                pl.BlockSpec((PAGES // NPG, 2, TOK, FEAT), lambda g, n: (g, 0, 0, 0)),
-                whole(qkv),
-            ],
-            out_specs=pl.BlockSpec((HEADS, 1, TILES, TOK, HD), lambda g, n: (0, g, 0, 0, 0)),
-            scratch_shapes=[pltpu.VMEM((NPG, 8, HD), BF), pltpu.VMEM((ROWS, FEAT), F32)],
-        ),
+        in_specs=[pl.BlockSpec(memory_space=pltpu.SMEM), vmem, vmem, pl.BlockSpec(memory_space=pl.ANY), vmem],
+        out_specs=pl.BlockSpec(memory_space=pl.ANY),
+        scratch_shapes=[
+            pltpu.VMEM((HEADS, NPG, TILES, TOK, HD), BF),
+            pltpu.VMEM((NPG, TOK, HD), BF),
+            pltpu.VMEM((ROWS, FEAT), F32),
+            pltpu.SemaphoreType.DMA((2, HEADS)),
+        ],
         out_shape=jax.ShapeDtypeStruct((HEADS, NPG, TILES, TOK, HD), BF),
         cost_estimate=pl.CostEstimate(flops=1_000_000, bytes_accessed=10_000_000, transcendentals=0),
         name="pack",
-    )(lens, owner, slot, kv_store, qkv)
+    )(lens, owner, slot, kv_store.reshape(NPG, 16, TOK, FEAT), qkv)
 
 
 def owner_kernel(got_ref, o_ref, kbuf, vbuf, acc, tops, sums, index, tile_ref, sem):
@@ -240,7 +244,7 @@
     return pl.pallas_call(
         owner_kernel,
         grid=(DEV // NEAR,),
-        in_specs=[pl.BlockSpec(got.shape, lambda i: (0, 0, 0), pipeline_mode=pl.Buffered(1))],
+        in_specs=[pl.BlockSpec(memory_space=pltpu.VMEM)],
         out_specs=pl.BlockSpec((NEAR, ROWS, 2 * HD), lambda i: (i, 0, 0)),
         scratch_shapes=[
             pltpu.VMEM((NEAR, JOBS, TOK, HD), BF),
@@ -254,8 +258,8 @@
         ],
         out_shape=jax.ShapeDtypeStruct((DEV, ROWS, 2 * HD), BF),
         cost_estimate=pl.CostEstimate(flops=4 * 2048 * 256 * 128, bytes_accessed=8_000_000, transcendentals=600_000),
-        compiler_params=pltpu.CompilerParams(vmem_limit_bytes=32 * 1024 * 1024),
-        name="owner_attention",
+                compiler_params=pltpu.CompilerParams(vmem_limit_bytes=VMEM_LIMIT),
+                name="owner_attention",
     )(got)
 
 
@@ -263,10 +267,10 @@
     lane = lax.broadcasted_iota(jnp.int32, (HD, HD), 0)
     top_of = (lane < 3).astype(F32).astype(BF)
     sum_of = ((lane >= 3) & (lane < 5)).astype(F32).astype(BF)
-    stats = got_ref[:, :, HD:].reshape(HPC * NPG * ROWS, HD)
-    tops = dot(stats, top_of).reshape(HPC, NPG, ROWS, HD)
-    sums = dot(stats, sum_of).reshape(HPC, NPG, ROWS, HD)
-    for h in range(HPC):
+    stats = got_ref[:, :, HD:].reshape(HEADS * NPG * ROWS, HD)
+    tops = dot(stats, top_of).reshape(HEADS, NPG, ROWS, HD)
+    sums = dot(stats, sum_of).reshape(HEADS, NPG, ROWS, HD)
+    for h in range(HEADS):
         at = slice(h * HD, (h + 1) * HD)
         got = got_ref[h * NPG : (h + 1) * NPG, :, :HD].astype(F32)
         lm = m_ref[:, at]
@@ -280,14 +284,14 @@
 
 
 def combine(got, o, m, l):
-    row = pl.BlockSpec((ROWS, HPC * HD), lambda h: (0, h))
+    vmem = pl.BlockSpec(memory_space=pltpu.VMEM)
     return pl.pallas_call(
         combine_kernel,
-        grid=(HEADS // HPC,),
-        in_specs=[pl.BlockSpec((HPC * NPG, ROWS, 2 * HD), lambda h: (h, 0, 0)), row, row, row],
-        out_specs=pl.BlockSpec((STEPS, RD, HPC * HD), lambda h: (0, 0, h)),
+        in_specs=[vmem] * 4,
+        out_specs=vmem,
         out_shape=jax.ShapeDtypeStruct((STEPS, RD, FEAT), BF),
         cost_estimate=pl.CostEstimate(flops=4 * 16 * 1024 * 2048, bytes_accessed=2_000_000, transcendentals=300_000),
+        compiler_params=pltpu.CompilerParams(vmem_limit_bytes=VMEM_LIMIT),
         name="combine_attention",
     )(got, o, m, l)
 
@@ -314,6 +318,7 @@
         out_specs=pl.BlockSpec((NPG * ROWS, wide), lambda i: (0, i)),
         out_shape=jax.ShapeDtypeStruct((NPG * ROWS, MF), BF),
         cost_estimate=pl.CostEstimate(flops=4 * 128 * 128 * 4096, bytes_accessed=3_200_000, transcendentals=0),
+        compiler_params=pltpu.CompilerParams(vmem_limit_bytes=VMEM_LIMIT),
         name="state_products",
     )(which, c_all, states)
 
@@ -345,6 +350,7 @@
         out_specs=pl.BlockSpec((STEPS, RD, wide), lambda i: (0, 0, i)),
         out_shape=jax.ShapeDtypeStruct((STEPS, RD, MF), BF),
         cost_estimate=pl.CostEstimate(flops=6 * 80 * 64 * 4096, bytes_accessed=1_500_000, transcendentals=0),
+        compiler_params=pltpu.CompilerParams(vmem_limit_bytes=VMEM_LIMIT),
         name="scan_outputs",
     )(coef, x, z)
 

time: 151 us -> 142 us (0.940)
  Pallas kernels: 51.5 us -> 37 us
  waiting for transfers between devices: 61.2 us -> 66.2 us
    pallas_call x2, Pallas kernels: 12.2 us -> 6.46 us  [the longest x1 5.29 us: pack(): pl.pallas_call(pack_kernel, in_specs=[pl.BlockSpec(memory_space=pltpu.SME...]
    pallas_call x1, Pallas kernels: 13.6 us -> 9.35 us  [local_attention(): pl.pallas_call(local_kernel, grid=(HEADS,), in_specs=[row, row, row, pl.B...]
    unnamed x23 -> x25, local copies, waits for them, and re-layouts: 1.67 us -> 5.59 us
    all_to_all x1, waiting for transfers between devices: 15.6 us -> 18.9 us  [on_device(): lax.all_to_all(sent.reshape(DEV, TILES, TOK, HD), ('req', 'page'), 0, 0,...]
    pallas_call x1, Pallas kernels: 4.21 us -> 2.51 us  [state_products(): pl.pallas_call(state_kernel, grid=(MF // wide,), in_specs=[pl.BlockSpec((...]
    pallas_call x1, Pallas kernels: 18.1 us -> 16.5 us  [owner_attention(): pl.pallas_call(owner_kernel, grid=(DEV // NEAR,), in_specs=[pl.BlockSpec(...]
  transfers between devices with their start and end apart: 4 -> 4, of which waited for: 3 -> 3; matrix products, arithmetic and copies ran while one was open for 3% -> 2% of each run, Pallas kernels for 26% -> 22%
where the time goes in v5:
time: 142 us
  waiting for transfers between devices  66.2 us (47%)
  Pallas kernels  37 us (26%)
  starting transfers between devices  16.6 us (12%)
  between operations  14.3 us (10%)
  local copies, waits for them, and re-layouts  6.15 us (4%)
  other arithmetic  1.51 us (1%)
    all_gather x1, waiting for transfers between devices, on_device(): c_all = lax.all_gather(c_own, 'page', axis=0, tiled=True)  31.2 us
    all_to_all x1, waiting for transfers between devices, on_device(): lax.all_to_all(sent.reshape(DEV, TILES, TOK, HD), ('req', 'page'), 0, 0,...  18.9 us
    pallas_call x1, Pallas kernels, owner_attention(): pl.pallas_call(owner_kernel, grid=(DEV // NEAR,), in_specs=[pl.BlockSpec(...  16.5 us
    all_to_all x1, waiting for transfers between devices, on_device(): got = lax.all_to_all(part, ('req', 'page'), 0, 0, tiled=True)  16.1 us
    all_to_all x1, starting transfers between devices, on_device(): lax.all_to_all(sent.reshape(DEV, TILES, TOK, HD), ('req', 'page'), 0, 0,...  11.9 us
    pallas_call x1, Pallas kernels, local_attention(): pl.pallas_call(local_kernel, grid=(HEADS,), in_specs=[row, row, row, pl.B...  9.35 us
    unnamed x25, local copies, waits for them, and re-layouts  5.59 us
    pallas_call x1, Pallas kernels, pack(): pl.pallas_call(pack_kernel, in_specs=[pl.BlockSpec(memory_space=pltpu.SME...  5.29 us
  transfers between devices with their start and end apart: 4, of which 3 were waited for; matrix products, arithmetic and copies ran while one was open for 2% of the time, Pallas kernels for 22%

profile of v5, /device:TPU:1, one launch (start us, length us, event | category | flops | bytes accessed | tf_op | source)
XLA Modules:
  0.0 141.8 jit_solution(1412429988873662138)
XLA Ops:
  7.2 5.3 %pack.1 = bf16[16,8,19,8,128]{4,3,2,1,0:T(8,128)(2,1)} custom-call(s32[4]{0:T(128)} %len_ref.1, s32[4,32]{1,0:T(4,128)} %own_ref.1, s32[4,32]{1,0:T(4,128)} %slot_ref.1, bf16[8,16,8,2048]{3,2,1,0:T(8,128)(2,1)} %bitcast.21, bf16[4,3,4,2048]{3,2,1,0:T(4,128)(2,1)} %bitcast.22), custom_call_target="tpu_custom_call" | custom-call | flops 1000000 | bytes 10000000 | tf_op jit(solution)/shard_map/pack/pallas_call | solution.py:141
  12.5 11.9 %all-to-all-start = ((bf16[128,19,8,128]{3,2,1,0:T(8,128)(2,1)}), bf16[128,19,8,128]{3,2,1,0:T(8,128)(2,1)}, u32[]{:S(2)}, u32[]{:S(2)}) async-start(bf16[128,19,8,128]{3,2,1,0:T(8,128)(2,1)} %bitcast.20), calls=%async_computation | async-start | bytes 9961472 | tf_op jit(solution)/shard_map/all_to_all | solution.py:411
  24.5 0.0 all-gather.2.cloned.1.call-start
  24.6 0.7 pad_maximum_fusion
  25.3 0.0 reduce-scatter.2.cloned.1.call-start
  25.4 0.1 sub.16
  25.5 0.1 reshape.137.br_ref
  25.6 0.1 convolution_bitcast_fusion
  25.7 0.2 slice_reduce_fusion
  26.0 0.1 constant_dynamic-update-slice_fusion.13
  26.1 0.1 constant_dynamic-update-slice_fusion.12
  26.1 0.1 fusion.6
  26.2 31.2 %all-gather.2.cloned.1.call-done.c_ref = bf16[128,4224]{1,0:T(8,128)(2,1)} async-done(((bf16[16,4224]{1,0:T(8,128)(2,1)}), bf16[128,4224]{1,0:T(8,128)(2,1)}) %all-gather.2.cloned.1.call-update) | async-done | bytes 1081360 | tf_op jit(solution)/shard_map/all_gather | solution.py:404
  57.4 1.2 copy-done.2
  58.6 2.5 %state_products.1 = bf16[128,4096]{1,0:T(8,128)(2,1)} custom-call(s32[128,1]{1,0:T(8,128)S(1)} %reshape.137.br_ref, bf16[128,4224]{1,0:T(8,128)(2,1)S(1)} %copy-done.2, bf16[2,4096,128]{2,1,0:T(8,128)(2,1)S(1)} %bitcast.17), custom_call_target="tpu_custom_call" | custom-call | flops 268435456 | bytes 3200000 | tf_op jit(solution)/shard_map/state_products/pallas_call | solution.py:310
  61.2 0.1 constant_dynamic-update-slice_fusion.11
  61.3 3.4 %copy-done = bf16[4,2,256,2048]{3,2,1,0:T(8,128)(2,1)S(1)} copy-done((bf16[4,2,256,2048]{3,2,1,0:T(8,128)(2,1)S(1)}, bf16[4,2,256,2048]{3,2,1,0:T(8,128)(2,1)}, u32[]{:S(2)}) %copy-start) | copy-done | bytes 8388632
  64.7 9.3 %local_attention.1 = (f32[16,2048]{1,0:T(8,128)S(1)}, f32[16,2048]{1,0:T(8,128)S(1)}, f32[16,2048]{1,0:T(8,128)S(1)}) custom-call(bf16[16,2048]{1,0:T(8,128)(2,1)S(1)} %reshape_squeeze.9.q_ref, bf16[16,2048]{1,0:T(8,128)(2,1)S(1)} %reshape_squeeze.10.nk_ref, bf16[16,2048]{1,0:T(8,128)(2,1)S(1)} %reshape_squeeze.11.nv_ref, bf16[4,2,256,2048]{3,2,1,0:T(8,128)(2,1)S(1)} %copy-done), custom_call_target="tpu_custom_call" | custom-call | flops 134217728 | bytes 9000000 | tf_op jit(solution)/shard_map/local_attention/pallas_call | solution.py:82
  74.1 0.1 constant_dynamic-update-slice_fusion.10
  74.1 0.1 constant_dynamic-update-slice_fusion.8
  74.2 0.1 constant_dynamic-update-slice_fusion.7
  74.3 18.9 %all-to-all-done = bf16[128,19,8,128]{3,2,1,0:T(8,128)(2,1)} async-done(((bf16[128,19,8,128]{3,2,1,0:T(8,128)(2,1)}), bf16[128,19,8,128]{3,2,1,0:T(8,128)(2,1)}, u32[]{:S(2)}, u32[]{:S(2)}) %all-to-all-start) | async-done | bytes 4980768 | tf_op jit(solution)/shard_map/all_to_all | solution.py:411
  93.2 16.5 %owner_attention.1 = bf16[128,16,256]{2,1,0:T(8,128)(2,1)} custom-call(bf16[2432,8,128]{2,1,0:T(8,128)(2,1)} %bitcast.3.got_ref), custom_call_target="tpu_custom_call" | custom-call | flops 268435456 | bytes 8000000 | tf_op jit(solution)/shard_map/owner_attention/pallas_call | solution.py:244
  109.7 4.6 %all-to-all-start.1 = ((bf16[128,16,256]{2,1,0:T(8,128)(2,1)}), bf16[128,16,256]{2,1,0:T(8,128)(2,1)S(1)}, u32[]{:S(2)}, u32[]{:S(2)}) async-start(bf16[128,16,256]{2,1,0:T(8,128)(2,1)} %owner_attention.1), calls=%async_computation.1 | async-start | bytes 2097152 | tf_op jit(solution)/shard_map/all_to_all | solution.py:420
  114.3 0.1 constant_dynamic-update-slice_fusion.6
  114.4 0.1 constant_dynamic-update-slice_fusion.4
  114.4 0.1 constant_dynamic-update-slice_fusion.3
  114.5 0.1 constant_dynamic-update-slice_fusion
  114.6 0.9 copy-done.3
  115.5 2.2 %scan_outputs.1 = bf16[4,4,4096]{2,1,0:T(4,128)(2,1)} custom-call(f32[80,64]{1,0:T(8,128)S(1)} %bitcast.18, bf16[16,4096]{1,0:T(8,128)(2,1)S(1)} %reshape.131.x_ref, bf16[16,4096]{1,0:T(8,128)(2,1)S(1)} %bitcast.19), custom_call_target="tpu_custom_call" | custom-call | flops 125829120 | bytes 1500000 | tf_op jit(solution)/shard_map/scan_outputs/pallas_call | solution.py:346
  117.7 16.1 %all-to-all-done.1.got_ref = bf16[128,16,256]{2,1,0:T(8,128)(2,1)S(1)} async-done(((bf16[128,16,256]{2,1,0:T(8,128)(2,1)}), bf16[128,16,256]{2,1,0:T(8,128)(2,1)S(1)}, u32[]{:S(2)}, u32[]{:S(2)}) %all-to-all-start.1) | async-done | bytes 1048608 | tf_op jit(solution)/shard_map/all_to_all | solution.py:420
  133.8 1.2 combine_attention.1
  (37 shorter events, 0.3 us)
Async XLA Ops:
  12.5 12.0 %copy-start.5 = (bf16[4,4,4096]{2,1,0:T(4,128)(2,1)S(1)}, bf16[4,4,4096]{2,1,0:T(4,128)(2,1)}, u32[]{:S(2)}) copy-start(bf16[4,4,4096]{2,1,0:T(4,128)(2,1)} %param.20) | copy-start | bytes 393220
  12.5 12.1 %copy-start.6 = (bf16[4,4,256]{2,1,0:T(4,128)(2,1)S(1)}, bf16[4,4,256]{2,1,0:T(4,128)(2,1)}, u32[]{:S(2)}) copy-start(bf16[4,4,256]{2,1,0:T(4,128)(2,1)} %param.21) | copy-start | bytes 24580
  12.5 12.9 %copy-start.8 = (f32[64]{0:T(128)S(1)}, f32[64]{0:T(128)}, u32[]{:S(2)}) copy-start(f32[64]{0:T(128)} %param.23) | copy-start | bytes 772
  12.5 12.9 %copy-start.9 = (s32[32]{0:T(128)S(1)}, s32[32]{0:T(128)}, u32[]{:S(2)}) copy-start(s32[32]{0:T(128)} %param.19) | copy-start | bytes 388
  12.5 13.2 %copy-start.7 = (bf16[4,4,64]{2,1,0:T(4,128)(2,1)S(1)}, bf16[4,4,64]{2,1,0:T(4,128)(2,1)}, u32[]{:S(2)}) copy-start(bf16[4,4,64]{2,1,0:T(4,128)(2,1)} %param.22) | copy-start | bytes 6148
  12.5 13.6 %copy-start.4 = (bf16[4,4,3,2048]{3,1,2,0:T(4,128)(2,1)S(1)}, bf16[4,4,3,2048]{3,1,2,0:T(4,128)(2,1)}, u32[]{:S(2)}) copy-start(bf16[4,4,3,2048]{3,1,2,0:T(4,128)(2,1)} %param.14) | copy-start | bytes 589828
  12.5 44.9 %copy-start.1 = (bf16[2,64,64,128]{3,2,1,0:T(8,128)(2,1)S(1)}, bf16[2,64,64,128]{3,2,1,0:T(8,128)(2,1)}, u32[]{:S(2)}) copy-start(bf16[2,64,64,128]{3,2,1,0:T(8,128)(2,1)} %param.18) | copy-start | bytes 6291460
  12.5 80.7 %all-to-all-start = ((bf16[128,19,8,128]{3,2,1,0:T(8,128)(2,1)}), bf16[128,19,8,128]{3,2,1,0:T(8,128)(2,1)}, u32[]{:S(2)}, u32[]{:S(2)}) async-start(bf16[128,19,8,128]{3,2,1,0:T(8,128)(2,1)} %bitcast.20), calls=%async_computation | async-start | bytes 9961472 | tf_op jit(solution)/shard_map/all_to_all | solution.py:411
  24.5 32.9 %all-gather.2.cloned.1.call-start = ((), (), s32[]{:S(2)}) async-start(), calls=%async_computation.3 | async-start | bytes 1216512 | tf_op jit(solution)/shard_map/all_gather | solution.py:404
  25.3 89.3 %reduce-scatter.2.cloned.1.call-start = ((), (), s32[]{:S(2)}) async-start(), calls=%async_computation.4 | async-start | bytes 1179648 | tf_op jit(solution)/shard_map/reduce_scatter | solution.py:408
  57.4 1.2 copy-start.2
  61.3 3.4 %copy-start = (bf16[4,2,256,2048]{3,2,1,0:T(8,128)(2,1)S(1)}, bf16[4,2,256,2048]{3,2,1,0:T(8,128)(2,1)}, u32[]{:S(2)}) copy-start(bf16[4,2,256,2048]{3,2,1,0:T(8,128)(2,1)} %kv_ref.1) | copy-start | bytes 25165828
  109.7 24.1 %all-to-all-start.1 = ((bf16[128,16,256]{2,1,0:T(8,128)(2,1)}), bf16[128,16,256]{2,1,0:T(8,128)(2,1)S(1)}, u32[]{:S(2)}, u32[]{:S(2)}) async-start(bf16[128,16,256]{2,1,0:T(8,128)(2,1)} %owner_attention.1), calls=%async_computation.1 | async-start | bytes 2097152 | tf_op jit(solution)/shard_map/all_to_all | solution.py:420
  114.6 0.9 copy-start.3
Sparse Core Ops, SparseCore 0:
  27.0 30.3 all-gather.1
  61.3 33.7 reduce-scatter.1

commit v6 on v5

--- a/solution.py
+++ b/solution.py
@@ -91,12 +91,18 @@
     )(q, nk, nv, local_kv)
 
 
-def pack_kernel(len_ref, own_ref, slot_ref, kv_ref, q_ref, out_ref, buf, lists, qbuf, sem):
+def pack_kernel(len_ref, own_all, slot_all, kv_ref, q_all, out_ref, buf, lists, qbuf, own_ref, slot_ref, q_ref, near, sem):
+    small = []
+    for i, (src, dst) in enumerate(((own_all, own_ref), (slot_all, slot_ref), (q_all, q_ref))):
+        small.append(pltpu.make_async_copy(src, dst, near.at[i]))
+        small[-1].start()
     copies = []
     for m in range(HEADS):
         src = kv_ref.at[:, :, :, pl.ds(m * HD, HD)]
         copies.append(pltpu.make_async_copy(src, buf.at[m, :, pl.ds(0, 16)], sem.at[0, m]))
         copies[-1].start()
+    for copy in small:
+        copy.wait()
     path = own_ref.shape[1]
     lane = lax.broadcasted_iota(jnp.int32, (8, HD), 1)
     row = lax.broadcasted_iota(jnp.int32, (8, HD), 0)
@@ -137,15 +143,18 @@
 
 
 def pack(lens, owner, slot, kv_store, qkv):
-    vmem = pl.BlockSpec(memory_space=pltpu.VMEM)
     return pl.pallas_call(
         pack_kernel,
-        in_specs=[pl.BlockSpec(memory_space=pltpu.SMEM), vmem, vmem, pl.BlockSpec(memory_space=pl.ANY), vmem],
+        in_specs=[pl.BlockSpec(memory_space=pltpu.SMEM)] + [pl.BlockSpec(memory_space=pl.ANY)] * 4,
         out_specs=pl.BlockSpec(memory_space=pl.ANY),
         scratch_shapes=[
             pltpu.VMEM((HEADS, NPG, TILES, TOK, HD), BF),
             pltpu.VMEM((NPG, TOK, HD), BF),
             pltpu.VMEM((ROWS, FEAT), F32),
+            pltpu.VMEM(owner.shape, jnp.int32),
+            pltpu.VMEM(slot.shape, jnp.int32),
+            pltpu.VMEM(qkv.shape, BF),
+            pltpu.SemaphoreType.DMA((3,)),
             pltpu.SemaphoreType.DMA((2, HEADS)),
         ],
         out_shape=jax.ShapeDtypeStruct((HEADS, NPG, TILES, TOK, HD), BF),
@@ -154,24 +163,30 @@
     )(lens, owner, slot, kv_store.reshape(NPG, 16, TOK, FEAT), qkv)
 
 
-def owner_kernel(got_ref, o_ref, kbuf, vbuf, acc, tops, sums, index, tile_ref, sem):
+def owner_kernel(all_ref, meta_ref, o_ref, kbuf, vbuf, acc, tops, sums, got_ref, lists, index, tile_ref, sem):
     step = pl.program_id(0)
 
     @pl.when(step == 0)
     def _():
-        lists = got_ref[pl.ds(META, DEV, stride=TILES)].astype(F32)
-        index[:DEV] = (lists[:, 0] * TILES + 2 * lists[:, 1]).astype(jnp.int32)
-        index[DEV:] = jnp.transpose(lists[:, 4])[:TOK].astype(jnp.int32)
-        copy = pltpu.make_async_copy(index, tile_ref, sem)
+        small = pltpu.make_async_copy(meta_ref.at[:, META], lists, sem.at[0])
+        large = pltpu.make_async_copy(all_ref, got_ref, sem.at[1])
+        small.start()
+        large.start()
+        small.wait()
+        table = lists[...].astype(F32)
+        index[:TOK] = jnp.transpose(table[:, 4])[:TOK].astype(jnp.int32)
+        index[TOK:] = jnp.transpose(table[:, 0] * TILES + 2 * table[:, 1]).astype(jnp.int32)
+        copy = pltpu.make_async_copy(index, tile_ref, sem.at[2])
         copy.start()
         copy.wait()
+        large.wait()
 
     base = step * NEAR
 
     def fetch(d, at):
         d_all = base + d
         for j in range(JOBS):
-            tile = tile_ref[d_all, at + j]
+            tile = tile_ref[TOK + at + j, d_all]
             kbuf[d, j] = got_ref[tile]
             vbuf[d, j] = got_ref[tile + 1]
 
@@ -210,9 +225,9 @@
     p = p.astype(BF)
     out = jnp.concatenate([mix(d, p[d])[None] for d in range(NEAR)], axis=0)
     write(slice(None), top, total, out)
-    most = tile_ref[DEV, base]
+    most = tile_ref[0, base]
     for d in range(1, NEAR):
-        most = jnp.maximum(most, tile_ref[DEV, base + d])
+        most = jnp.maximum(most, tile_ref[0, base + d])
 
     @pl.when(most > JOBS)
     def _():
@@ -220,7 +235,7 @@
         tops[...] = jnp.broadcast_to(top, tops.shape)
         sums[...] = jnp.broadcast_to(total, sums.shape)
         for d in range(NEAR):
-            num = tile_ref[DEV, base + d]
+            num = tile_ref[0, base + d]
 
             @pl.loop(1, (num + JOBS - 1) // JOBS)
             def _(c):
@@ -244,7 +259,7 @@
     return pl.pallas_call(
         owner_kernel,
         grid=(DEV // NEAR,),
-        in_specs=[pl.BlockSpec(memory_space=pltpu.VMEM)],
+        in_specs=[pl.BlockSpec(memory_space=pl.ANY)] * 2,
         out_specs=pl.BlockSpec((NEAR, ROWS, 2 * HD), lambda i: (i, 0, 0)),
         scratch_shapes=[
             pltpu.VMEM((NEAR, JOBS, TOK, HD), BF),
@@ -252,15 +267,16 @@
             pltpu.VMEM((NEAR, ROWS, HD), F32),
             pltpu.VMEM((NEAR, ROWS, HD), F32),
             pltpu.VMEM((NEAR, ROWS, HD), F32),
+            pltpu.VMEM((DEV * TILES, TOK, HD), BF),
+            pltpu.VMEM((DEV, TOK, HD), BF),
             pltpu.VMEM((DEV + TOK, HD), jnp.int32),
             pltpu.SMEM((DEV + TOK, HD), jnp.int32),
-            pltpu.SemaphoreType.DMA,
+            pltpu.SemaphoreType.DMA((3,)),
         ],
         out_shape=jax.ShapeDtypeStruct((DEV, ROWS, 2 * HD), BF),
         cost_estimate=pl.CostEstimate(flops=4 * 2048 * 256 * 128, bytes_accessed=8_000_000, transcendentals=600_000),
-                compiler_params=pltpu.CompilerParams(vmem_limit_bytes=VMEM_LIMIT),
-                name="owner_attention",
-    )(got)
+                        name="owner_attention",
+    )(got.reshape(DEV * TILES, TOK, HD), got)
 
 
 def combine_kernel(got_ref, o_ref, m_ref, l_ref, out_ref):
@@ -416,7 +432,7 @@
     o, m, l = local_attention(q, nk, nv, local_kv)
 
     got_q, o, m, l = lax.optimization_barrier((got_q, o, m, l))
-    part = owner_attention(got_q.reshape(DEV * TILES, TOK, HD))
+    part = owner_attention(got_q)
     got = lax.all_to_all(part, ("req", "page"), 0, 0, tiled=True)
     attn = combine(got, o, m, l)
     return attn, mamba_out

time: 142 us -> 142 us (level)
  no operation moved by 1% of the time
where the time goes in v6:
time: 142 us; the launch traced here: 141 us
  waiting for transfers between devices  66.2 us (47%)
  Pallas kernels  36.5 us (26%)
  starting transfers between devices  16.6 us (12%)
  between operations  14.3 us (10%)
  local copies, waits for them, and re-layouts  6.15 us (4%)
  other arithmetic  1.51 us (1%)
    all_gather x1, waiting for transfers between devices, on_device(): c_all = lax.all_gather(c_own, 'page', axis=0, tiled=True)  31.2 us
    all_to_all x1, waiting for transfers between devices, on_device(): lax.all_to_all(sent.reshape(DEV, TILES, TOK, HD), ('req', 'page'), 0, 0,...  18.9 us
    pallas_call x1, Pallas kernels, owner_attention(): pl.pallas_call(owner_kernel, grid=(DEV // NEAR,), in_specs=[pl.BlockSpec(...  16.4 us
    all_to_all x1, waiting for transfers between devices, on_device(): got = lax.all_to_all(part, ('req', 'page'), 0, 0, tiled=True)  16.1 us
    all_to_all x1, starting transfers between devices, on_device(): lax.all_to_all(sent.reshape(DEV, TILES, TOK, HD), ('req', 'page'), 0, 0,...  11.9 us
    pallas_call x1, Pallas kernels, local_attention(): pl.pallas_call(local_kernel, grid=(HEADS,), in_specs=[row, row, row, pl.B...  9.35 us
    unnamed x25, local copies, waits for them, and re-layouts  5.59 us
    pallas_call x1, Pallas kernels, pack(): pl.pallas_call(pack_kernel, in_specs=[pl.BlockSpec(memory_space=pltpu.SME...  4.9 us
  transfers between devices with their start and end apart: 4, of which 3 were waited for; matrix products, arithmetic and copies ran while one was open for 2% of the time, Pallas kernels for 22%

profile of v6, /device:TPU:1, one launch (start us, length us, event | category | flops | bytes accessed | tf_op | source)
XLA Modules:
  0.0 141.3 jit_solution(9629937160772156548)
XLA Ops:
  7.2 4.9 %pack.1 = bf16[16,8,19,8,128]{4,3,2,1,0:T(8,128)(2,1)} custom-call(s32[4]{0:T(128)} %len_ref.1, s32[4,32]{1,0:T(4,128)} %own_all.1, s32[4,32]{1,0:T(4,128)} %slot_all.1, bf16[8,16,8,2048]{3,2,1,0:T(8,128)(2,1)} %bitcast.21, bf16[4,3,4,2048]{3,2,1,0:T(4,128)(2,1)} %bitcast.22), custom_call_target="tpu_custom_call" | custom-call | flops 1000000 | bytes 10000000 | tf_op jit(solution)/shard_map/pack/pallas_call | solution.py:146
  12.2 11.9 %all-to-all-start = ((bf16[128,19,8,128]{3,2,1,0:T(8,128)(2,1)}), bf16[128,19,8,128]{3,2,1,0:T(8,128)(2,1)}, u32[]{:S(2)}, u32[]{:S(2)}) async-start(bf16[128,19,8,128]{3,2,1,0:T(8,128)(2,1)} %bitcast.20), calls=%async_computation | async-start | bytes 9961472 | tf_op jit(solution)/shard_map/all_to_all | solution.py:427
  24.1 0.0 all-gather.2.cloned.1.call-start
  24.2 0.7 pad_maximum_fusion
  24.9 0.0 reduce-scatter.2.cloned.1.call-start
  25.0 0.1 sub.16
  25.1 0.1 reshape.137.br_ref
  25.2 0.1 convolution_bitcast_fusion
  25.3 0.2 slice_reduce_fusion
  25.6 0.1 constant_dynamic-update-slice_fusion.13
  25.7 0.1 constant_dynamic-update-slice_fusion.12
  25.7 0.1 fusion.6
  25.8 31.2 %all-gather.2.cloned.1.call-done.c_ref = bf16[128,4224]{1,0:T(8,128)(2,1)} async-done(((bf16[16,4224]{1,0:T(8,128)(2,1)}), bf16[128,4224]{1,0:T(8,128)(2,1)}) %all-gather.2.cloned.1.call-update) | async-done | bytes 1081360 | tf_op jit(solution)/shard_map/all_gather | solution.py:420
  57.0 1.2 copy-done.2
  58.2 2.5 %state_products.1 = bf16[128,4096]{1,0:T(8,128)(2,1)} custom-call(s32[128,1]{1,0:T(8,128)S(1)} %reshape.137.br_ref, bf16[128,4224]{1,0:T(8,128)(2,1)S(1)} %copy-done.2, bf16[2,4096,128]{2,1,0:T(8,128)(2,1)S(1)} %bitcast.17), custom_call_target="tpu_custom_call" | custom-call | flops 268435456 | bytes 3200000 | tf_op jit(solution)/shard_map/state_products/pallas_call | solution.py:326
  60.8 0.1 constant_dynamic-update-slice_fusion.11
  60.9 3.4 %copy-done = bf16[4,2,256,2048]{3,2,1,0:T(8,128)(2,1)S(1)} copy-done((bf16[4,2,256,2048]{3,2,1,0:T(8,128)(2,1)S(1)}, bf16[4,2,256,2048]{3,2,1,0:T(8,128)(2,1)}, u32[]{:S(2)}) %copy-start) | copy-done | bytes 8388632
  64.3 9.3 %local_attention.1 = (f32[16,2048]{1,0:T(8,128)S(1)}, f32[16,2048]{1,0:T(8,128)S(1)}, f32[16,2048]{1,0:T(8,128)S(1)}) custom-call(bf16[16,2048]{1,0:T(8,128)(2,1)S(1)} %reshape_squeeze.9.q_ref, bf16[16,2048]{1,0:T(8,128)(2,1)S(1)} %reshape_squeeze.10.nk_ref, bf16[16,2048]{1,0:T(8,128)(2,1)S(1)} %reshape_squeeze.11.nv_ref, bf16[4,2,256,2048]{3,2,1,0:T(8,128)(2,1)S(1)} %copy-done), custom_call_target="tpu_custom_call" | custom-call | flops 134217728 | bytes 9000000 | tf_op jit(solution)/shard_map/local_attention/pallas_call | solution.py:82
  73.7 0.1 constant_dynamic-update-slice_fusion.10
  73.8 0.1 constant_dynamic-update-slice_fusion.8
  73.8 0.1 constant_dynamic-update-slice_fusion.7
  73.9 18.9 %all-to-all-done.meta_ref = bf16[128,19,8,128]{3,2,1,0:T(8,128)(2,1)} async-done(((bf16[128,19,8,128]{3,2,1,0:T(8,128)(2,1)}), bf16[128,19,8,128]{3,2,1,0:T(8,128)(2,1)}, u32[]{:S(2)}, u32[]{:S(2)}) %all-to-all-start) | async-done | bytes 4980768 | tf_op jit(solution)/shard_map/all_to_all | solution.py:427
  92.8 16.4 %owner_attention.1 = bf16[128,16,256]{2,1,0:T(8,128)(2,1)} custom-call(bf16[2432,8,128]{2,1,0:T(8,128)(2,1)} %bitcast.3.all_ref, bf16[128,19,8,128]{3,2,1,0:T(8,128)(2,1)} %all-to-all-done.meta_ref), custom_call_target="tpu_custom_call" | custom-call | flops 268435456 | bytes 8000000 | tf_op jit(solution)/shard_map/owner_attention/pallas_call | solution.py:259
  109.2 4.6 %all-to-all-start.1 = ((bf16[128,16,256]{2,1,0:T(8,128)(2,1)}), bf16[128,16,256]{2,1,0:T(8,128)(2,1)S(1)}, u32[]{:S(2)}, u32[]{:S(2)}) async-start(bf16[128,16,256]{2,1,0:T(8,128)(2,1)} %owner_attention.1), calls=%async_computation.1 | async-start | bytes 2097152 | tf_op jit(solution)/shard_map/all_to_all | solution.py:436
  113.8 0.1 constant_dynamic-update-slice_fusion.6
  113.9 0.1 constant_dynamic-update-slice_fusion.4
  114.0 0.1 constant_dynamic-update-slice_fusion.3
  114.1 0.1 constant_dynamic-update-slice_fusion
  114.2 0.9 copy-done.3
  115.1 2.2 %scan_outputs.1 = bf16[4,4,4096]{2,1,0:T(4,128)(2,1)} custom-call(f32[80,64]{1,0:T(8,128)S(1)} %bitcast.18, bf16[16,4096]{1,0:T(8,128)(2,1)S(1)} %reshape.131.x_ref, bf16[16,4096]{1,0:T(8,128)(2,1)S(1)} %bitcast.19), custom_call_target="tpu_custom_call" | custom-call | flops 125829120 | bytes 1500000 | tf_op jit(solution)/shard_map/scan_outputs/pallas_call | solution.py:362
  117.2 16.1 %all-to-all-done.1.got_ref = bf16[128,16,256]{2,1,0:T(8,128)(2,1)S(1)} async-done(((bf16[128,16,256]{2,1,0:T(8,128)(2,1)}), bf16[128,16,256]{2,1,0:T(8,128)(2,1)S(1)}, u32[]{:S(2)}, u32[]{:S(2)}) %all-to-all-start.1) | async-done | bytes 1048608 | tf_op jit(solution)/shard_map/all_to_all | solution.py:436
  133.3 1.2 combine_attention.1
  (37 shorter events, 0.3 us)
Async XLA Ops:
  12.1 12.0 %copy-start.5 = (bf16[4,4,4096]{2,1,0:T(4,128)(2,1)S(1)}, bf16[4,4,4096]{2,1,0:T(4,128)(2,1)}, u32[]{:S(2)}) copy-start(bf16[4,4,4096]{2,1,0:T(4,128)(2,1)} %param.20) | copy-start | bytes 393220
  12.1 12.1 %copy-start.6 = (bf16[4,4,256]{2,1,0:T(4,128)(2,1)S(1)}, bf16[4,4,256]{2,1,0:T(4,128)(2,1)}, u32[]{:S(2)}) copy-start(bf16[4,4,256]{2,1,0:T(4,128)(2,1)} %param.21) | copy-start | bytes 24580
  12.1 12.9 %copy-start.8 = (f32[64]{0:T(128)S(1)}, f32[64]{0:T(128)}, u32[]{:S(2)}) copy-start(f32[64]{0:T(128)} %param.23) | copy-start | bytes 772
  12.1 12.9 %copy-start.9 = (s32[32]{0:T(128)S(1)}, s32[32]{0:T(128)}, u32[]{:S(2)}) copy-start(s32[32]{0:T(128)} %param.19) | copy-start | bytes 388
  12.1 13.2 %copy-start.7 = (bf16[4,4,64]{2,1,0:T(4,128)(2,1)S(1)}, bf16[4,4,64]{2,1,0:T(4,128)(2,1)}, u32[]{:S(2)}) copy-start(bf16[4,4,64]{2,1,0:T(4,128)(2,1)} %param.22) | copy-start | bytes 6148
  12.1 13.6 %copy-start.4 = (bf16[4,4,3,2048]{3,1,2,0:T(4,128)(2,1)S(1)}, bf16[4,4,3,2048]{3,1,2,0:T(4,128)(2,1)}, u32[]{:S(2)}) copy-start(bf16[4,4,3,2048]{3,1,2,0:T(4,128)(2,1)} %param.14) | copy-start | bytes 589828
  12.1 44.9 %copy-start.1 = (bf16[2,64,64,128]{3,2,1,0:T(8,128)(2,1)S(1)}, bf16[2,64,64,128]{3,2,1,0:T(8,128)(2,1)}, u32[]{:S(2)}) copy-start(bf16[2,64,64,128]{3,2,1,0:T(8,128)(2,1)} %param.18) | copy-start | bytes 6291460
  12.2 80.7 %all-to-all-start = ((bf16[128,19,8,128]{3,2,1,0:T(8,128)(2,1)}), bf16[128,19,8,128]{3,2,1,0:T(8,128)(2,1)}, u32[]{:S(2)}, u32[]{:S(2)}) async-start(bf16[128,19,8,128]{3,2,1,0:T(8,128)(2,1)} %bitcast.20), calls=%async_computation | async-start | bytes 9961472 | tf_op jit(solution)/shard_map/all_to_all | solution.py:427
  24.1 32.9 %all-gather.2.cloned.1.call-start = ((), (), s32[]{:S(2)}) async-start(), calls=%async_computation.3 | async-start | bytes 1216512 | tf_op jit(solution)/shard_map/all_gather | solution.py:420
  24.9 89.3 %reduce-scatter.2.cloned.1.call-start = ((), (), s32[]{:S(2)}) async-start(), calls=%async_computation.4 | async-start | bytes 1179648 | tf_op jit(solution)/shard_map/reduce_scatter | solution.py:424
  57.0 1.2 copy-start.2
  60.9 3.4 %copy-start = (bf16[4,2,256,2048]{3,2,1,0:T(8,128)(2,1)S(1)}, bf16[4,2,256,2048]{3,2,1,0:T(8,128)(2,1)}, u32[]{:S(2)}) copy-start(bf16[4,2,256,2048]{3,2,1,0:T(8,128)(2,1)} %kv_ref.1) | copy-start | bytes 25165828
  109.2 24.1 %all-to-all-start.1 = ((bf16[128,16,256]{2,1,0:T(8,128)(2,1)}), bf16[128,16,256]{2,1,0:T(8,128)(2,1)S(1)}, u32[]{:S(2)}, u32[]{:S(2)}) async-start(bf16[128,16,256]{2,1,0:T(8,128)(2,1)} %owner_attention.1), calls=%async_computation.1 | async-start | bytes 2097152 | tf_op jit(solution)/shard_map/all_to_all | solution.py:436
  114.2 0.9 copy-start.3
Sparse Core Ops, SparseCore 0:
  26.6 30.3 all-gather.1
  60.9 33.6 reduce-scatter.1
